TPU v7x, 32 devices: a whole 2x2x4 slice. The times are simulated.
32 devices in a mesh: row: 4 (over x, core), col: 8 (over z, y).
Axes of the slice: x: 2, y: 2, z: 4, core: 2. Of those that a mesh axis runs over, the one named last changes fastest.
Arguments:
- latents: bfloat16 [8200, 1536], P('col', 'row'), may hold values from -30 to 30
- conditioning: bfloat16 [1040, 1536], P('col', 'row'), may hold values from -6 to 6
- teacher: bfloat16 [8200, 1536], P('col', 'row'), may hold values from -46 to 46
- gain_attn: float32 [1536], P('row'), may hold values from 0.5 to 1.5
- bias_attn: float32 [1536], P('row'), may hold values from -0.3 to 0.3
- gain_cross: float32 [1536], P('row'), may hold values from 0.5 to 1.5
- bias_cross: float32 [1536], P('row'), may hold values from -1.8 to 1.8
- gain_mlp: float32 [1536], P('row'), may hold values from 0.5 to 1.5
- bias_mlp: float32 [1536], P('row'), may hold values from -1.8 to 1.8
- w_query: bfloat16 [1536, 1536], P('col', 'row'), may hold values from -0.15625 to 0.15625
- w_key: bfloat16 [1536, 1536], P('col', 'row'), may hold values from -0.15625 to 0.15625
- w_value: bfloat16 [1536, 1536], P('col', 'row'), may hold values from -0.15625 to 0.15625
- w_out: bfloat16 [1536, 1536], P('row', 'col'), may hold values from -3 to 3
- w_cross_query: bfloat16 [1536, 1536], P('col', 'row'), may hold values from -0.15625 to 0.15625
- w_cross_key: bfloat16 [1536, 1536], P('col', 'row'), may hold values from -0.15625 to 0.15625
- w_cross_value: bfloat16 [1536, 1536], P('col', 'row'), may hold values from -0.15625 to 0.15625
- w_cross_out: bfloat16 [1536, 1536], P('row', 'col'), may hold values from -1 to 1
- w_gate: bfloat16 [1536, 6144], P('col', 'row'), may hold values from -0.15625 to 0.15625
- w_up: bfloat16 [1536, 6144], P('col', 'row'), may hold values from -0.15625 to 0.15625
- w_down: bfloat16 [6144, 1536], P('row', 'col'), may hold values from -0.078125 to 0.078125
Outputs:
- outputs: bfloat16 [8200, 1536], P('col', 'row')
- loss: float32 [], replicated
- grad_latents: bfloat16 [8200, 1536], P('col', 'row')
- grad_conditioning: bfloat16 [1040, 1536], P('col', 'row')
- grad_w_query: float32 [1536, 1536], P('col', 'row')
- grad_w_key: float32 [1536, 1536], P('col', 'row')
- grad_w_value: float32 [1536, 1536], P('col', 'row')
- grad_w_out: float32 [1536, 1536], P('row', 'col')
- grad_w_cross_query: float32 [1536, 1536], P('col', 'row')
- grad_w_cross_key: float32 [1536, 1536], P('col', 'row')
- grad_w_cross_value: float32 [1536, 1536], P('col', 'row')
- grad_w_cross_out: float32 [1536, 1536], P('row', 'col')
- grad_w_gate: float32 [1536, 6144], P('col', 'row')
- grad_w_up: float32 [1536, 6144], P('col', 'row')
- grad_w_down: float32 [6144, 1536], P('row', 'col')
- grad_gain_attn: float32 [1536], P(('row', 'col'))
- grad_bias_attn: float32 [1536], P(('row', 'col'))
- grad_gain_cross: float32 [1536], P(('row', 'col'))
- grad_bias_cross: float32 [1536], P(('row', 'col'))
- grad_gain_mlp: float32 [1536], P(('row', 'col'))
- grad_bias_mlp: float32 [1536], P(('row', 'col'))
All inputs are finite; a program needn't handle non-finite values.
Results may differ from a plain program's by a relative error of at most 0.017.
Values may be sent and summed in bfloat16 or wider, within the bound.
A program may use at most 192 MiB of HBM per device.

v0:
```python
import math

import jax
import jax.numpy as jnp
from jax import lax
from jax.sharding import PartitionSpec as P

HEAD = 64
ROT = 32
LEN = 1025
CLEN = 130


EPSILON = 1e-06


def rotary_tables(length, rotated):
    half_size = rotated // 2
    position = jnp.arange(length, dtype=jnp.float32)
    frequency = jnp.exp(
        jnp.arange(half_size, dtype=jnp.float32) * (-2.0 * math.log(10000.0) / rotated)
    )
    angles = position[:, None] * frequency[None, :]
    return (jnp.cos(angles)[:, None, :], jnp.sin(angles)[:, None, :])


def rotate(tensor, cosine, sine):
    half_size = ROT // 2
    front_half = tensor[..., :half_size]
    back_half = tensor[..., half_size:ROT]
    untouched = tensor[..., ROT:]
    return jnp.concatenate(
        [front_half * cosine - back_half * sine, back_half * cosine + front_half * sine, untouched],
        axis=-1,
    )


def rotate_back(gradient, cosine, sine):
    half_size = ROT // 2
    front_half = gradient[..., :half_size]
    back_half = gradient[..., half_size:ROT]
    untouched = gradient[..., ROT:]
    return jnp.concatenate(
        [front_half * cosine + back_half * sine, back_half * cosine - front_half * sine, untouched],
        axis=-1,
    )


def split_heads(matrix, length):
    return matrix.reshape(matrix.shape[0] // length, length, matrix.shape[1] // HEAD, HEAD)


def merge_heads(blocks):
    return blocks.reshape(blocks.shape[0] * blocks.shape[1], blocks.shape[2] * blocks.shape[3])


def product(left, right):
    return jnp.dot(left, right, preferred_element_type=jnp.float32)


def contract_rows(left, right):
    return lax.dot_general(
        left, right, (((0,), (0,)), ((), ())), preferred_element_type=jnp.float32
    )


def contract_cols(left, right):
    return lax.dot_general(
        left, right, (((1,), (1,)), ((), ())), preferred_element_type=jnp.float32
    )


def norm_forward(stream, norm_gain, norm_shift):
    columns = stream.shape[1] * lax.axis_size("row")
    totals, squares = lax.psum((jnp.sum(stream, axis=1), jnp.sum(stream * stream, axis=1)), "row")
    average = totals / columns
    inverse = lax.rsqrt(squares / columns - average * average + EPSILON)
    normed = (stream - average[:, None]) * inverse[:, None]
    return (normed, inverse, (normed * norm_gain + norm_shift).astype(jnp.bfloat16))


def norm_backward(gradient, normed, inverse, norm_gain):
    columns = gradient.shape[1] * lax.axis_size("row")
    scaled = gradient * norm_gain
    totals, crossed = lax.psum((jnp.sum(scaled, axis=1), jnp.sum(scaled * normed, axis=1)), "row")
    return inverse[:, None] * (
        scaled - totals[:, None] / columns - normed * (crossed[:, None] / columns)
    )


def spread_rows(low_rows):
    return lax.all_gather(low_rows, "row", axis=1, tiled=True)


def branch_total(partial_value):
    return lax.psum_scatter(
        partial_value.astype(jnp.bfloat16), "row", scatter_dimension=1, tiled=True
    ).astype(jnp.float32)


def spread_grads(low_grads):
    return lax.all_gather(low_grads, "row", axis=1, tiled=True)


def grad_total(partial_value):
    return lax.psum_scatter(
        partial_value.astype(jnp.bfloat16), "row", scatter_dimension=1, tiled=True
    ).astype(jnp.float32)


def attend(queries, key_rows, value_rows, scaling):
    scores = (
        jnp.einsum("qhd,khd->hqk", queries, key_rows, preferred_element_type=jnp.float32) * scaling
    )
    maximum = jnp.max(scores, axis=2, keepdims=True)
    shifted = jnp.exp(scores - maximum)
    totals = jnp.sum(shifted, axis=2, keepdims=True)
    weights = (shifted / totals).astype(jnp.bfloat16)
    mixed = jnp.einsum("hqk,khd->qhd", weights, value_rows, preferred_element_type=jnp.float32)
    return (mixed.astype(jnp.bfloat16), (maximum + jnp.log(totals))[:, :, 0])


def attend_backward(queries, key_rows, value_rows, logsum, grad_mixed, scaling):
    scores = (
        jnp.einsum("qhd,khd->hqk", queries, key_rows, preferred_element_type=jnp.float32) * scaling
    )
    weights = jnp.exp(scores - logsum[:, :, None])
    grad_weights = jnp.einsum(
        "qhd,khd->hqk", grad_mixed, value_rows, preferred_element_type=jnp.float32
    )
    grad_values = jnp.einsum(
        "hqk,qhd->khd", weights.astype(jnp.bfloat16), grad_mixed, preferred_element_type=jnp.float32
    )
    grad_scores = weights * (grad_weights - jnp.sum(weights * grad_weights, axis=2, keepdims=True))
    grad_raw = (grad_scores * scaling).astype(jnp.bfloat16)
    grad_queries = jnp.einsum(
        "hqk,khd->qhd", grad_raw, key_rows, preferred_element_type=jnp.float32
    )
    grad_keys = jnp.einsum("hqk,qhd->khd", grad_raw, queries, preferred_element_type=jnp.float32)
    return (grad_queries, grad_keys, grad_values)


def body(
    latents,
    conditioning,
    teacher,
    gain_attn,
    bias_attn,
    gain_cross,
    bias_cross,
    gain_mlp,
    bias_mlp,
    w_query,
    w_key,
    w_value,
    w_out,
    w_cross_query,
    w_cross_key,
    w_cross_value,
    w_cross_out,
    w_gate,
    w_up,
    w_down,
):
    scaling = HEAD ** (-0.5)
    cosine, sine = rotary_tables(LEN, ROT)
    shards = (
        w_query,
        w_key,
        w_value,
        w_cross_query,
        w_cross_key,
        w_cross_value,
        w_gate,
        w_up,
        w_out,
        w_cross_out,
        w_down,
    )
    (
        full_query,
        full_key,
        full_value,
        full_cquery,
        full_ckey,
        full_cvalue,
        full_gate,
        full_up,
        full_out,
        full_cout,
        full_down,
    ) = (
        lax.all_gather(shards[0], "col", axis=0, tiled=True),
        lax.all_gather(shards[1], "col", axis=0, tiled=True),
        lax.all_gather(shards[2], "col", axis=0, tiled=True),
        lax.all_gather(shards[3], "col", axis=0, tiled=True),
        lax.all_gather(shards[4], "col", axis=0, tiled=True),
        lax.all_gather(shards[5], "col", axis=0, tiled=True),
        lax.all_gather(shards[6], "col", axis=0, tiled=True),
        lax.all_gather(shards[7], "col", axis=0, tiled=True),
        lax.all_gather(shards[8], "col", axis=1, tiled=True),
        lax.all_gather(shards[9], "col", axis=1, tiled=True),
        lax.all_gather(shards[10], "col", axis=1, tiled=True),
    )
    cond_full = lax.all_gather(conditioning, "row", axis=1, tiled=True)

    def run_attend(group):
        return attend(group[0], group[1], group[2], scaling)

    def run_backward(group):
        return attend_backward(group[0], group[1], group[2], group[3], group[4], scaling)

    stream_zero = latents.astype(jnp.float32)
    normed_one, inverse_one, low_one = norm_forward(stream_zero, gain_attn, bias_attn)
    rows_one = spread_rows(low_one)
    queries = rotate(split_heads(product(rows_one, full_query), LEN), cosine, sine).astype(
        jnp.bfloat16
    )
    key_rows = rotate(split_heads(product(rows_one, full_key), LEN), cosine, sine).astype(
        jnp.bfloat16
    )
    value_rows = split_heads(product(rows_one, full_value), LEN).astype(jnp.bfloat16)
    mixed_one, logsum_one = lax.map(run_attend, (queries, key_rows, value_rows))
    mixed_one_flat = merge_heads(mixed_one)
    stream_one = stream_zero + branch_total(product(mixed_one_flat, full_out))
    normed_two, inverse_two, low_two = norm_forward(stream_one, gain_cross, bias_cross)
    rows_two = spread_rows(low_two)
    cross_queries = split_heads(product(rows_two, full_cquery), LEN).astype(jnp.bfloat16)
    cross_keys = split_heads(product(cond_full, full_ckey), CLEN).astype(jnp.bfloat16)
    cross_values = split_heads(product(cond_full, full_cvalue), CLEN).astype(jnp.bfloat16)
    mixed_two, logsum_two = lax.map(run_attend, (cross_queries, cross_keys, cross_values))
    mixed_two_flat = merge_heads(mixed_two)
    stream_two = stream_one + branch_total(product(mixed_two_flat, full_cout))
    normed_three, inverse_three, low_three = norm_forward(stream_two, gain_mlp, bias_mlp)
    rows_three = spread_rows(low_three)
    gate_values = product(rows_three, full_gate)
    up_values = product(rows_three, full_up)
    hidden = (jax.nn.silu(gate_values) * up_values).astype(jnp.bfloat16)
    final = stream_two + branch_total(product(hidden, full_down))
    outputs = final.astype(jnp.bfloat16)
    residual = final - teacher.astype(jnp.float32)
    count = residual.size * lax.axis_size("row") * lax.axis_size("col")
    loss = lax.psum(jnp.sum(residual * residual), ("row", "col")) / count
    (
        full_query,
        full_key,
        full_value,
        full_cquery,
        full_ckey,
        full_cvalue,
        full_gate,
        full_up,
        full_out,
        full_cout,
        full_down,
    ) = (
        lax.all_gather(shards[0], "col", axis=0, tiled=True),
        lax.all_gather(shards[1], "col", axis=0, tiled=True),
        lax.all_gather(shards[2], "col", axis=0, tiled=True),
        lax.all_gather(shards[3], "col", axis=0, tiled=True),
        lax.all_gather(shards[4], "col", axis=0, tiled=True),
        lax.all_gather(shards[5], "col", axis=0, tiled=True),
        lax.all_gather(shards[6], "col", axis=0, tiled=True),
        lax.all_gather(shards[7], "col", axis=0, tiled=True),
        lax.all_gather(shards[8], "col", axis=1, tiled=True),
        lax.all_gather(shards[9], "col", axis=1, tiled=True),
        lax.all_gather(shards[10], "col", axis=1, tiled=True),
    )
    grad_down_rows = spread_grads(residual.astype(jnp.bfloat16))
    part_down = contract_rows(hidden, grad_down_rows)
    grad_hidden = contract_cols(grad_down_rows, full_down)
    sigmoid_gate = jax.nn.sigmoid(gate_values)
    grad_gate = (
        grad_hidden * up_values * sigmoid_gate * (1.0 + gate_values * (1.0 - sigmoid_gate))
    ).astype(jnp.bfloat16)
    grad_up = (grad_hidden * gate_values * sigmoid_gate).astype(jnp.bfloat16)
    part_gate = contract_rows(rows_three, grad_gate)
    part_up = contract_rows(rows_three, grad_up)
    dnorm_three = grad_total(contract_cols(grad_gate, full_gate) + contract_cols(grad_up, full_up))
    part_gain_three = jnp.sum(dnorm_three * normed_three, axis=0)
    part_bias_three = jnp.sum(dnorm_three, axis=0)
    grad_stream_two = residual + norm_backward(dnorm_three, normed_three, inverse_three, gain_mlp)
    grad_cout_rows = spread_grads(grad_stream_two.astype(jnp.bfloat16))
    part_cout = contract_rows(mixed_two_flat, grad_cout_rows)
    grad_mixed_two = split_heads(contract_cols(grad_cout_rows, full_cout), LEN).astype(jnp.bfloat16)
    grad_cq, grad_ck, grad_cv = lax.map(
        run_backward, (cross_queries, cross_keys, cross_values, logsum_two, grad_mixed_two)
    )
    grad_cq_low = merge_heads(grad_cq).astype(jnp.bfloat16)
    grad_ck_low = merge_heads(grad_ck).astype(jnp.bfloat16)
    grad_cv_low = merge_heads(grad_cv).astype(jnp.bfloat16)
    part_cquery = contract_rows(rows_two, grad_cq_low)
    part_ckey = contract_rows(cond_full, grad_ck_low)
    part_cvalue = contract_rows(cond_full, grad_cv_low)
    grad_conditioning = lax.psum_scatter(
        (contract_cols(grad_ck_low, full_ckey) + contract_cols(grad_cv_low, full_cvalue)).astype(
            jnp.bfloat16
        ),
        "row",
        scatter_dimension=1,
        tiled=True,
    )
    dnorm_two = grad_total(contract_cols(grad_cq_low, full_cquery))
    part_gain_two = jnp.sum(dnorm_two * normed_two, axis=0)
    part_bias_two = jnp.sum(dnorm_two, axis=0)
    grad_stream_one = grad_stream_two + norm_backward(
        dnorm_two, normed_two, inverse_two, gain_cross
    )
    grad_out_rows = spread_grads(grad_stream_one.astype(jnp.bfloat16))
    part_out = contract_rows(mixed_one_flat, grad_out_rows)
    grad_mixed_one = split_heads(contract_cols(grad_out_rows, full_out), LEN).astype(jnp.bfloat16)
    grad_qrot, grad_krot, grad_vals = lax.map(
        run_backward, (queries, key_rows, value_rows, logsum_one, grad_mixed_one)
    )
    grad_q_low = merge_heads(rotate_back(grad_qrot, cosine, sine)).astype(jnp.bfloat16)
    grad_k_low = merge_heads(rotate_back(grad_krot, cosine, sine)).astype(jnp.bfloat16)
    grad_v_low = merge_heads(grad_vals).astype(jnp.bfloat16)
    part_query = contract_rows(rows_one, grad_q_low)
    part_key = contract_rows(rows_one, grad_k_low)
    part_value = contract_rows(rows_one, grad_v_low)
    dnorm_one = grad_total(
        contract_cols(grad_q_low, full_query)
        + contract_cols(grad_k_low, full_key)
        + contract_cols(grad_v_low, full_value)
    )
    part_gain_one = jnp.sum(dnorm_one * normed_one, axis=0)
    part_bias_one = jnp.sum(dnorm_one, axis=0)
    grad_latents = (
        grad_stream_one + norm_backward(dnorm_one, normed_one, inverse_one, gain_attn)
    ).astype(jnp.bfloat16)
    (
        grad_w_query,
        grad_w_key,
        grad_w_value,
        grad_w_cross_query,
        grad_w_cross_key,
        grad_w_cross_value,
        grad_w_gate,
        grad_w_up,
        grad_gain_attn,
        grad_bias_attn,
        grad_gain_cross,
        grad_bias_cross,
        grad_gain_mlp,
        grad_bias_mlp,
    ) = (
        lax.psum_scatter(
            part_query.astype(jnp.bfloat16), "col", scatter_dimension=0, tiled=True
        ).astype(jnp.float32),
        lax.psum_scatter(
            part_key.astype(jnp.bfloat16), "col", scatter_dimension=0, tiled=True
        ).astype(jnp.float32),
        lax.psum_scatter(
            part_value.astype(jnp.bfloat16), "col", scatter_dimension=0, tiled=True
        ).astype(jnp.float32),
        lax.psum_scatter(
            part_cquery.astype(jnp.bfloat16), "col", scatter_dimension=0, tiled=True
        ).astype(jnp.float32),
        lax.psum_scatter(
            part_ckey.astype(jnp.bfloat16), "col", scatter_dimension=0, tiled=True
        ).astype(jnp.float32),
        lax.psum_scatter(
            part_cvalue.astype(jnp.bfloat16), "col", scatter_dimension=0, tiled=True
        ).astype(jnp.float32),
        lax.psum_scatter(
            part_gate.astype(jnp.bfloat16), "col", scatter_dimension=0, tiled=True
        ).astype(jnp.float32),
        lax.psum_scatter(
            part_up.astype(jnp.bfloat16), "col", scatter_dimension=0, tiled=True
        ).astype(jnp.float32),
        lax.psum_scatter(
            part_gain_one.astype(jnp.bfloat16), "col", scatter_dimension=0, tiled=True
        ).astype(jnp.float32),
        lax.psum_scatter(
            part_bias_one.astype(jnp.bfloat16), "col", scatter_dimension=0, tiled=True
        ).astype(jnp.float32),
        lax.psum_scatter(
            part_gain_two.astype(jnp.bfloat16), "col", scatter_dimension=0, tiled=True
        ).astype(jnp.float32),
        lax.psum_scatter(
            part_bias_two.astype(jnp.bfloat16), "col", scatter_dimension=0, tiled=True
        ).astype(jnp.float32),
        lax.psum_scatter(
            part_gain_three.astype(jnp.bfloat16), "col", scatter_dimension=0, tiled=True
        ).astype(jnp.float32),
        lax.psum_scatter(
            part_bias_three.astype(jnp.bfloat16), "col", scatter_dimension=0, tiled=True
        ).astype(jnp.float32),
    )
    grad_w_out, grad_w_cross_out, grad_w_down = (
        lax.psum_scatter(
            part_out.astype(jnp.bfloat16), "col", scatter_dimension=1, tiled=True
        ).astype(jnp.float32),
        lax.psum_scatter(
            part_cout.astype(jnp.bfloat16), "col", scatter_dimension=1, tiled=True
        ).astype(jnp.float32),
        lax.psum_scatter(
            part_down.astype(jnp.bfloat16), "col", scatter_dimension=1, tiled=True
        ).astype(jnp.float32),
    )
    return (
        outputs,
        loss,
        grad_latents,
        grad_conditioning,
        grad_w_query,
        grad_w_key,
        grad_w_value,
        grad_w_out,
        grad_w_cross_query,
        grad_w_cross_key,
        grad_w_cross_value,
        grad_w_cross_out,
        grad_w_gate,
        grad_w_up,
        grad_w_down,
        grad_gain_attn,
        grad_bias_attn,
        grad_gain_cross,
        grad_bias_cross,
        grad_gain_mlp,
        grad_bias_mlp,
    )


def solution(mesh):
    in_specs = (
        P("col", "row"),
        P("col", "row"),
        P("col", "row"),
        P("row"),
        P("row"),
        P("row"),
        P("row"),
        P("row"),
        P("row"),
        P("col", "row"),
        P("col", "row"),
        P("col", "row"),
        P("row", "col"),
        P("col", "row"),
        P("col", "row"),
        P("col", "row"),
        P("row", "col"),
        P("col", "row"),
        P("col", "row"),
        P("row", "col"),
    )
    out_specs = (
        P("col", "row"),
        P(),
        P("col", "row"),
        P("col", "row"),
        P("col", "row"),
        P("col", "row"),
        P("col", "row"),
        P("row", "col"),
        P("col", "row"),
        P("col", "row"),
        P("col", "row"),
        P("row", "col"),
        P("col", "row"),
        P("col", "row"),
        P("row", "col"),
        P(("row", "col")),
        P(("row", "col")),
        P(("row", "col")),
        P(("row", "col")),
        P(("row", "col")),
        P(("row", "col")),
    )
    return jax.shard_map(body, mesh=mesh, in_specs=in_specs, out_specs=out_specs, check_vma=False)
```

profile of v0, /device:TPU:0, one launch (start us, length us, event | category | flops | bytes accessed | tf_op | source)
XLA Modules:
  0.0 2059.6 jit_solution(125462551434566398)
XLA Ops:
  9.5 12.7 all-reduce.11
  27.6 26.4 %all-gather.20.cloned.1.call-done = bf16[1536,384]{1,0:T(8,128)(2,1)} async-done(((bf16[192,384]{1,0:T(8,128)(2,1)}), bf16[1536,384]{1,0:T(8,128)(2,1)}) %all-gather.20.cloned.1.call-update) | async-done | bytes 1179664 | tf_op jit(solution)/shard_map/all_gather | solution.py:195
  54.0 29.6 %all-gather.18.cloned.1.call-done = bf16[1025,1536]{1,0:T(8,128)(2,1)} async-done(((bf16[1025,384]{1,0:T(8,128)(2,1)}), bf16[1025,1536]{1,0:T(8,128)(2,1)}) %all-gather.18.cloned.1.call-update) | async-done | bytes 3148816 | tf_op jit(solution)/shard_map/all_gather | solution.py:92
  89.5 37.3 %all-gather.24.cloned.1.call-done = bf16[1536,384]{1,0:T(8,128)(2,1)} async-done(((bf16[192,384]{1,0:T(8,128)(2,1)}), bf16[1536,384]{1,0:T(8,128)(2,1)}) %all-gather.24.cloned.1.call-update) | async-done | bytes 1179664 | tf_op jit(solution)/shard_map/all_gather | solution.py:194
  130.9 37.9 %all-gather.22.cloned.1.call-done = bf16[1536,384]{1,0:T(8,128)(2,1)} async-done(((bf16[192,384]{1,0:T(8,128)(2,1)}), bf16[1536,384]{1,0:T(8,128)(2,1)}) %all-gather.22.cloned.1.call-update) | async-done | bytes 1179664 | tf_op jit(solution)/shard_map/all_gather | solution.py:193
  173.2 11.7 fusion.132
  184.9 11.8 fusion.7
  196.8 11.8 fusion.47
  223.3 37.0 %reduce-scatter.55.cloned.1.call-done = bf16[384,1025]{1,0:T(8,128)(2,1)} async-done(((bf16[1536,1025]{1,0:T(8,128)(2,1)}), bf16[384,1025]{1,0:T(8,128)(2,1)}) %reduce-scatter.55.cloned.1.call-update) | async-done | bytes 787216
  263.2 10.1 all-reduce.10
  282.2 21.6 %all-gather.34.cloned.1.call-done = bf16[1536,384]{1,0:T(8,128)(2,1)} async-done(((bf16[192,384]{1,0:T(8,128)(2,1)}), bf16[1536,384]{1,0:T(8,128)(2,1)}) %all-gather.34.cloned.1.call-update) | async-done | bytes 1179664 | tf_op jit(solution)/shard_map/all_gather | solution.py:197
  305.6 40.5 %all-gather.28.cloned.1.call-done = bf16[1536,384]{1,0:T(8,128)(2,1)} async-done(((bf16[192,384]{1,0:T(8,128)(2,1)}), bf16[1536,384]{1,0:T(8,128)(2,1)}) %all-gather.28.cloned.1.call-update) | async-done | bytes 1179664 | tf_op jit(solution)/shard_map/all_gather | solution.py:198
  347.9 40.5 %all-gather.32.cloned.1.call-done = bf16[1536,384]{1,0:T(8,128)(2,1)} async-done(((bf16[192,384]{1,0:T(8,128)(2,1)}), bf16[1536,384]{1,0:T(8,128)(2,1)}) %all-gather.32.cloned.1.call-update) | async-done | bytes 1179664 | tf_op jit(solution)/shard_map/all_gather | solution.py:196
  388.4 29.5 %all-gather.30.cloned.1.call-done = bf16[1025,1536]{1,0:T(8,128)(2,1)} async-done(((bf16[1025,384]{1,0:T(8,128)(2,1)}), bf16[1025,1536]{1,0:T(8,128)(2,1)}) %all-gather.30.cloned.1.call-update) | async-done | bytes 3148816 | tf_op jit(solution)/shard_map/all_gather | solution.py:92
  428.0 33.4 %all-gather.36.cloned.1.call-done = bf16[384,1536]{0,1:T(8,128)(2,1)} async-done(((bf16[384,192]{0,1:T(8,128)(2,1)}), bf16[384,1536]{0,1:T(8,128)(2,1)}) %all-gather.36.cloned.1.call-update) | async-done | bytes 1179664 | tf_op jit(solution)/shard_map/all_gather | solution.py:202
  472.5 38.5 %reduce-scatter.57.cloned.1.call-done = bf16[384,1025]{1,0:T(8,128)(2,1)} async-done(((bf16[1536,1025]{1,0:T(8,128)(2,1)}), bf16[384,1025]{1,0:T(8,128)(2,1)}) %reduce-scatter.57.cloned.1.call-update) | async-done | bytes 787216
  514.9 10.1 all-reduce.9
  527.6 65.6 %all-gather.40.cloned.1.call-done = bf16[1536,1536]{1,0:T(8,128)(2,1)} async-done(((bf16[192,1536]{1,0:T(8,128)(2,1)}), bf16[1536,1536]{1,0:T(8,128)(2,1)}) %all-gather.40.cloned.1.call-update) | async-done | bytes 4718608 | tf_op jit(solution)/shard_map/all_gather | solution.py:199
  593.1 28.8 %all-gather.38.cloned.1.call-done = bf16[1025,1536]{1,0:T(8,128)(2,1)} async-done(((bf16[1025,384]{1,0:T(8,128)(2,1)}), bf16[1025,1536]{1,0:T(8,128)(2,1)}) %all-gather.38.cloned.1.call-update) | async-done | bytes 3148816 | tf_op jit(solution)/shard_map/all_gather | solution.py:92
  631.7 72.2 %all-gather.42.cloned.1.call-done = bf16[1536,1536]{1,0:T(8,128)(2,1)} async-done(((bf16[192,1536]{1,0:T(8,128)(2,1)}), bf16[1536,1536]{1,0:T(8,128)(2,1)}) %all-gather.42.cloned.1.call-update) | async-done | bytes 4718608 | tf_op jit(solution)/shard_map/all_gather | solution.py:200
  703.9 11.4 multiply_convert_fusion.2
  715.3 68.6 %all-gather.44.cloned.1.call-done = bf16[1536,1536]{0,1:T(8,128)(2,1)} async-done(((bf16[1536,192]{0,1:T(8,128)(2,1)}), bf16[1536,1536]{0,1:T(8,128)(2,1)}) %all-gather.44.cloned.1.call-update) | async-done | bytes 4718608 | tf_op jit(solution)/shard_map/all_gather | solution.py:203
  798.7 38.7 %reduce-scatter.59.cloned.1.call-done = bf16[384,1025]{1,0:T(8,128)(2,1)} async-done(((bf16[1536,1025]{1,0:T(8,128)(2,1)}), bf16[384,1025]{1,0:T(8,128)(2,1)}) %reduce-scatter.59.cloned.1.call-update) | async-done | bytes 787216
  842.1 28.7 %all-gather.46.cloned.1.call-done = bf16[1025,1536]{1,0:T(8,128)(2,1)} async-done(((bf16[1025,384]{1,0:T(8,128)(2,1)}), bf16[1025,1536]{1,0:T(8,128)(2,1)}) %all-gather.46.cloned.1.call-update) | async-done | bytes 3148816 | tf_op jit(solution)/shard_map/all_gather | solution.py:102
  870.8 12.5 multiply_convert_fusion
  906.7 40.6 %reduce-scatter.61.cloned.1.call-done = bf16[384,1025]{1,0:T(8,128)(2,1)} async-done(((bf16[1536,1025]{1,0:T(8,128)(2,1)}), bf16[384,1025]{1,0:T(8,128)(2,1)}) %reduce-scatter.61.cloned.1.call-update) | async-done | bytes 787216
  966.5 29.8 %all-gather.48.cloned.1.call-done = bf16[1025,1536]{1,0:T(8,128)(2,1)} async-done(((bf16[1025,384]{1,0:T(8,128)(2,1)}), bf16[1025,1536]{1,0:T(8,128)(2,1)}) %all-gather.48.cloned.1.call-update) | async-done | bytes 3148816 | tf_op jit(solution)/shard_map/all_gather | solution.py:102
  1024.2 40.5 %reduce-scatter.63.cloned.1.call-done = bf16[384,1025]{1,0:T(8,128)(2,1)} async-done(((bf16[1536,1025]{1,0:T(8,128)(2,1)}), bf16[384,1025]{1,0:T(8,128)(2,1)}) %reduce-scatter.63.cloned.1.call-update) | async-done | bytes 787216
  1081.8 10.3 convolution_convert_fusion
  1092.2 10.6 convolution_convert_fusion.1
  1102.8 10.4 convolution_convert_fusion.2
  1155.3 29.6 %fusion.36 = f32[1,1025,6,64]{1,3,2,0:T(8,128)} fusion(f32[6,1025,1025]{1,2,0:T(8,128)} %get-tuple-element.237, f32[6,1025]{1,0:T(8,128)S(1)} %log_add_fusion, bf16[1025,6,64]{0,2,1:T(8,128)(2,1)S(1)} %bitcast.170, bf16[1025,6,64]{0,2,1:T(8,128)(2,1)} %bitcast.186, bf16[1025,6,32]{0,2,1:T(8,128)(2,1)S(1)} %copy-done.14, ...), kind=kOutput, calls=%fused_computation.48 | convolution fusion | flops 2467134976 | bytes 29175600 | tf_op jit(solution)/shard_map/while/body/eval_jaxpr/hqk,khd->qhd/dot_general | solution.py:136
  1186.2 30.5 %fusion.41 = f32[1,1025,6,64]{1,3,2,0:T(8,128)} fusion(f32[6,1025,1025]{1,2,0:T(8,128)} %get-tuple-element.237, f32[6,1025]{1,0:T(8,128)S(1)} %log_add_fusion, bf16[1025,6,64]{0,2,1:T(8,128)(2,1)S(1)} %bitcast.171, bf16[1025,6,64]{0,2,1:T(8,128)(2,1)} %bitcast.187, bf16[1025,6,32]{0,2,1:T(8,128)(2,1)S(1)} %copy-done.12, ...), kind=kOutput, calls=%fused_computation.49 | convolution fusion | flops 2467134976 | bytes 29175600 | tf_op jit(solution)/shard_map/while/body/eval_jaxpr/hqk,qhd->khd/dot_general | solution.py:139
  1229.1 12.1 fusion.48
  1261.0 41.3 %psum.97 = f32[]{:T(128)} all-reduce(f32[]{:T(128)} %get-tuple-element.180), channel_id=1, replica_groups=mesh['row'=4,'col'=8] {'row','col'}, use_global_device_ids=true, to_apply=%region_20.21 | all-reduce | flops 1 | bytes 8 | tf_op jit(solution)/shard_map/psum | solution.py:243
  1312.9 97.1 %reduce-scatter.49.cloned.1.call-done = bf16[192,1536]{1,0:T(8,128)(2,1)} async-done(((bf16[1536,1536]{1,0:T(8,128)(2,1)}), bf16[192,1536]{1,0:T(8,128)(2,1)}) %reduce-scatter.49.cloned.1.call-update) | async-done | bytes 589840 | tf_op jit(solution)/shard_map/reduce_scatter | solution.py:365
  1412.2 23.4 %reduce-scatter.67.cloned.1.call-done = bf16[384,130]{1,0:T(8,128)(2,1)} async-done(((bf16[1536,130]{1,0:T(8,128)(2,1)}), bf16[384,130]{1,0:T(8,128)(2,1)}) %reduce-scatter.67.cloned.1.call-update) | async-done | bytes 99856
  1437.3 65.7 %reduce-scatter.71.cloned.1.call-done = bf16[192,384]{1,0:T(8,128)(2,1)} async-done(((bf16[1536,384]{1,0:T(8,128)(2,1)}), bf16[192,384]{1,0:T(8,128)(2,1)}) %reduce-scatter.71.cloned.1.call-update) | async-done | bytes 147472
  1504.9 64.5 %reduce-scatter.69.cloned.1.call-done = bf16[192,384]{1,0:T(8,128)(2,1)} async-done(((bf16[1536,384]{1,0:T(8,128)(2,1)}), bf16[192,384]{1,0:T(8,128)(2,1)}) %reduce-scatter.69.cloned.1.call-update) | async-done | bytes 147472
  1571.3 64.7 %reduce-scatter.47.cloned.1.call-done = bf16[384,192]{0,1:T(8,128)(2,1)} async-done(((bf16[384,1536]{0,1:T(8,128)(2,1)}), bf16[384,192]{0,1:T(8,128)(2,1)}) %reduce-scatter.47.cloned.1.call-update) | async-done | bytes 147472 | tf_op jit(solution)/shard_map/reduce_scatter | solution.py:394
  1637.6 64.7 %reduce-scatter.45.cloned.1.call-done = bf16[192,384]{1,0:T(8,128)(2,1)} async-done(((bf16[1536,384]{1,0:T(8,128)(2,1)}), bf16[192,384]{1,0:T(8,128)(2,1)}) %reduce-scatter.45.cloned.1.call-update) | async-done | bytes 147472 | tf_op jit(solution)/shard_map/reduce_scatter | solution.py:356
  1704.1 64.5 %reduce-scatter.43.cloned.1.call-done = bf16[384,192]{0,1:T(8,128)(2,1)} async-done(((bf16[384,1536]{0,1:T(8,128)(2,1)}), bf16[384,192]{0,1:T(8,128)(2,1)}) %reduce-scatter.43.cloned.1.call-update) | async-done | bytes 147472 | tf_op jit(solution)/shard_map/reduce_scatter | solution.py:391
  1770.3 64.8 %reduce-scatter.37.cloned.1.call-done = bf16[192,384]{1,0:T(8,128)(2,1)} async-done(((bf16[1536,384]{1,0:T(8,128)(2,1)}), bf16[192,384]{1,0:T(8,128)(2,1)}) %reduce-scatter.37.cloned.1.call-update) | async-done | bytes 147472 | tf_op jit(solution)/shard_map/reduce_scatter | solution.py:347
  1836.7 64.7 %reduce-scatter.39.cloned.1.call-done = bf16[192,384]{1,0:T(8,128)(2,1)} async-done(((bf16[1536,384]{1,0:T(8,128)(2,1)}), bf16[192,384]{1,0:T(8,128)(2,1)}) %reduce-scatter.39.cloned.1.call-update) | async-done | bytes 147472 | tf_op jit(solution)/shard_map/reduce_scatter | solution.py:350
  1903.1 64.7 %reduce-scatter.41.cloned.1.call-done = bf16[192,384]{1,0:T(8,128)(2,1)} async-done(((bf16[1536,384]{1,0:T(8,128)(2,1)}), bf16[192,384]{1,0:T(8,128)(2,1)}) %reduce-scatter.41.cloned.1.call-update) | async-done | bytes 147472 | tf_op jit(solution)/shard_map/reduce_scatter | solution.py:353
  1969.5 40.4 %reduce-scatter.65.cloned.1.call-done = bf16[384,1025]{1,0:T(8,128)(2,1)} async-done(((bf16[1536,1025]{1,0:T(8,128)(2,1)}), bf16[384,1025]{1,0:T(8,128)(2,1)}) %reduce-scatter.65.cloned.1.call-update) | async-done | bytes 787216
  2014.6 21.6 %all-reduce.12 = (bf16[384]{0:T(512)(128)(2,1)S(1)}, bf16[384]{0:T(512)(128)(2,1)S(1)}, bf16[384]{0:T(512)(128)(2,1)S(1)}, bf16[384]{0:T(512)(128)(2,1)S(1)}, bf...) all-reduce(bf16[384]{0:T(512)(128)(2,1)S(1)} %get-tuple-element.178, ...), channel_id=20, replica_groups=mesh['row'=4,'col'=8] {'col'}, use_global_device_ids=true, to_apply=%region_51.52.clone | all-reduce | flops 2304 | bytes 9216
  2039.7 10.3 all-reduce.6
  (310 shorter events, 307.8 us)
Async XLA Ops:
  7.2 46.8 %all-gather.20.cloned.1.call-start = ((), (), s32[]{:S(2)}) async-start(), calls=%async_computation.19 | async-start | bytes 1327104 | tf_op jit(solution)/shard_map/all_gather | solution.py:195
  7.9 75.6 %all-gather.18.cloned.1.call-start = ((), (), s32[]{:S(2)}) async-start(), calls=%async_computation.18 | async-start | bytes 3962880 | tf_op jit(solution)/shard_map/all_gather | solution.py:92
  24.6 102.2 %all-gather.24.cloned.1.call-start = ((), (), s32[]{:S(2)}) async-start(), calls=%async_computation.21 | async-start | bytes 1327104 | tf_op jit(solution)/shard_map/all_gather | solution.py:194
  25.4 143.4 %all-gather.22.cloned.1.call-start = ((), (), s32[]{:S(2)}) async-start(), calls=%async_computation.20 | async-start | bytes 1327104 | tf_op jit(solution)/shard_map/all_gather | solution.py:193
  26.0 184.7 %all-gather.26.cloned.1.call-start = ((), (), s32[]{:S(2)}) async-start(), calls=%async_computation.22 | async-start | bytes 1327104 | tf_op jit(solution)/shard_map/all_gather | solution.py:201
  26.6 233.7 %reduce-scatter.55.cloned.1.call-start = ((), (), s32[]{:S(2)}) async-start(), calls=%async_computation.44 | async-start | bytes 4423680
  27.6 145.3 %copy-start.27 = (f32[1025,16]{0,1:T(8,128)}, f32[1025,16]{0,1:T(8,128)S(1)}, u32[]{:S(2)}) copy-start(f32[1025,16]{0,1:T(8,128)S(1)} %get-tuple-element.234) | copy-start | bytes 196804
  89.5 107.3 %copy-start.25 = (bf16[1025,384]{0,1:T(8,128)(2,1)}, bf16[1025,384]{0,1:T(8,128)(2,1)S(1)}, u32[]{:S(2)}) copy-start(bf16[1025,384]{0,1:T(8,128)(2,1)S(1)} %copy.81) | copy-start | bytes 2361604
  221.0 82.8 %all-gather.34.cloned.1.call-start = ((), (), s32[]{:S(2)}) async-start(), calls=%async_computation.26 | async-start | bytes 1327104 | tf_op jit(solution)/shard_map/all_gather | solution.py:197
  221.7 124.4 %all-gather.28.cloned.1.call-start = ((), (), s32[]{:S(2)}) async-start(), calls=%async_computation.23 | async-start | bytes 1327104 | tf_op jit(solution)/shard_map/all_gather | solution.py:198
  222.5 165.9 %all-gather.32.cloned.1.call-start = ((), (), s32[]{:S(2)}) async-start(), calls=%async_computation.25 | async-start | bytes 1327104 | tf_op jit(solution)/shard_map/all_gather | solution.py:196
  223.2 194.7 %all-gather.30.cloned.1.call-start = ((), (), s32[]{:S(2)}) async-start(), calls=%async_computation.24 | async-start | bytes 3962880 | tf_op jit(solution)/shard_map/all_gather | solution.py:92
  274.7 186.7 %all-gather.36.cloned.1.call-start = ((), (), s32[]{:S(2)}) async-start(), calls=%async_computation.27 | async-start | bytes 1327104 | tf_op jit(solution)/shard_map/all_gather | solution.py:202
  275.4 235.6 %reduce-scatter.57.cloned.1.call-start = ((), (), s32[]{:S(2)}) async-start(), calls=%async_computation.45 | async-start | bytes 4423680
  282.2 140.6 %copy-start.2 = (bf16[130,1536]{1,0:T(8,128)(2,1)}, bf16[130,1536]{1,0:T(8,128)(2,1)S(1)}, u32[]{:S(2)}) copy-start(bf16[130,1536]{1,0:T(8,128)(2,1)S(1)} %all_gather.70) | copy-start | bytes 1198084
  347.9 77.9 %copy-start.26 = (bf16[130,384]{0,1:T(8,128)(2,1)}, bf16[130,384]{0,1:T(8,128)(2,1)S(1)}, u32[]{:S(2)}) copy-start(bf16[130,384]{0,1:T(8,128)(2,1)S(1)} %copy.121) | copy-start | bytes 299524
  471.7 53.4 %copy-start.44 = (f32[384]{0:T(512)S(1)}, f32[384]{0:T(512)}, u32[]{:S(2)}) copy-start(f32[384]{0:T(512)} %param.27) | copy-start | bytes 4612
  471.7 53.4 %copy-start.48 = (f32[384]{0:T(512)S(1)}, f32[384]{0:T(512)}, u32[]{:S(2)}) copy-start(f32[384]{0:T(512)} %param.28) | copy-start | bytes 4612
  471.7 121.4 %all-gather.40.cloned.1.call-start = ((), (), s32[]{:S(2)}) async-start(), calls=%async_computation.29 | async-start | bytes 5308416 | tf_op jit(solution)/shard_map/all_gather | solution.py:199
  472.4 149.5 %all-gather.38.cloned.1.call-start = ((), (), s32[]{:S(2)}) async-start(), calls=%async_computation.28 | async-start | bytes 3962880 | tf_op jit(solution)/shard_map/all_gather | solution.py:92
  526.3 177.5 %all-gather.42.cloned.1.call-start = ((), (), s32[]{:S(2)}) async-start(), calls=%async_computation.30 | async-start | bytes 5308416 | tf_op jit(solution)/shard_map/all_gather | solution.py:200
  526.9 257.0 %all-gather.44.cloned.1.call-start = ((), (), s32[]{:S(2)}) async-start(), calls=%async_computation.31 | async-start | bytes 5308416 | tf_op jit(solution)/shard_map/all_gather | solution.py:203
  527.5 309.8 %reduce-scatter.59.cloned.1.call-start = ((), (), s32[]{:S(2)}) async-start(), calls=%async_computation.46 | async-start | bytes 4423680
  798.6 72.2 %all-gather.46.cloned.1.call-start = ((), (), s32[]{:S(2)}) async-start(), calls=%async_computation.32 | async-start | bytes 3962880 | tf_op jit(solution)/shard_map/all_gather | solution.py:102
  842.0 105.3 %reduce-scatter.61.cloned.1.call-start = ((), (), s32[]{:S(2)}) async-start(), calls=%async_computation.47 | async-start | bytes 4423680
  906.7 89.6 %all-gather.48.cloned.1.call-start = ((), (), s32[]{:S(2)}) async-start(), calls=%async_computation.33 | async-start | bytes 3962880 | tf_op jit(solution)/shard_map/all_gather | solution.py:102
  966.4 98.3 %reduce-scatter.63.cloned.1.call-start = ((), (), s32[]{:S(2)}) async-start(), calls=%async_computation.48 | async-start | bytes 4423680
  1024.2 119.1 %all-gather.50.cloned.1.call-start = ((), (), s32[]{:S(2)}) async-start(), calls=%async_computation.34 | async-start | bytes 3962880 | tf_op jit(solution)/shard_map/all_gather | solution.py:102
  1081.7 221.5 %reduce-scatter.53.cloned.1.call-start = ((), (), s32[]{:S(2)}) async-start(), calls=%async_computation.43 | async-start | bytes 5308416 | tf_op jit(solution)/shard_map/reduce_scatter | solution.py:397
  1092.1 218.5 %reduce-scatter.51.cloned.1.call-start = ((), (), s32[]{:S(2)}) async-start(), calls=%async_computation.42 | async-start | bytes 5308416 | tf_op jit(solution)/shard_map/reduce_scatter | solution.py:368
  1102.8 307.2 %reduce-scatter.49.cloned.1.call-start = ((), (), s32[]{:S(2)}) async-start(), calls=%async_computation.41 | async-start | bytes 5308416 | tf_op jit(solution)/shard_map/reduce_scatter | solution.py:365
  1113.2 322.4 %reduce-scatter.67.cloned.1.call-start = ((), (), s32[]{:S(2)}) async-start(), calls=%async_computation.50 | async-start | bytes 983040
  1128.3 374.7 %reduce-scatter.71.cloned.1.call-start = ((), (), s32[]{:S(2)}) async-start(), calls=%async_computation.52 | async-start | bytes 1327104
  1130.3 439.1 %reduce-scatter.69.cloned.1.call-start = ((), (), s32[]{:S(2)}) async-start(), calls=%async_computation.51 | async-start | bytes 1327104
  1132.2 503.7 %reduce-scatter.47.cloned.1.call-start = ((), (), s32[]{:S(2)}) async-start(), calls=%async_computation.40 | async-start | bytes 1327104 | tf_op jit(solution)/shard_map/reduce_scatter | solution.py:394
  1137.8 564.4 %reduce-scatter.45.cloned.1.call-start = ((), (), s32[]{:S(2)}) async-start(), calls=%async_computation.39 | async-start | bytes 1327104 | tf_op jit(solution)/shard_map/reduce_scatter | solution.py:356
  1143.2 625.4 %reduce-scatter.43.cloned.1.call-start = ((), (), s32[]{:S(2)}) async-start(), calls=%async_computation.38 | async-start | bytes 1327104 | tf_op jit(solution)/shard_map/reduce_scatter | solution.py:391
  1148.6 686.5 %reduce-scatter.37.cloned.1.call-start = ((), (), s32[]{:S(2)}) async-start(), calls=%async_computation.35 | async-start | bytes 1327104 | tf_op jit(solution)/shard_map/reduce_scatter | solution.py:347
  1222.4 679.0 %reduce-scatter.39.cloned.1.call-start = ((), (), s32[]{:S(2)}) async-start(), calls=%async_computation.36 | async-start | bytes 1327104 | tf_op jit(solution)/shard_map/reduce_scatter | solution.py:350
  1229.0 738.8 %reduce-scatter.41.cloned.1.call-start = ((), (), s32[]{:S(2)}) async-start(), calls=%async_computation.37 | async-start | bytes 1327104 | tf_op jit(solution)/shard_map/reduce_scatter | solution.py:353
  1244.5 765.4 %reduce-scatter.65.cloned.1.call-start = ((), (), s32[]{:S(2)}) async-start(), calls=%async_computation.49 | async-start | bytes 4423680
  1305.4 398.5 %copy-start.8 = (bf16[384,1025]{1,0:T(8,128)(2,1)S(1)}, bf16[384,1025]{1,0:T(8,128)(2,1)}, u32[]{:S(2)}) copy-start(bf16[384,1025]{1,0:T(8,128)(2,1)} %reduce-scatter.63.cloned.1.call-done) | copy-start | bytes 2361604
  1504.0 508.0 %copy-start.38 = (f32[1025]{0:T(1024)S(1)}, f32[1025]{0:T(1024)}, u32[]{:S(2)}) copy-start(f32[1025]{0:T(1024)} %copy-done.37) | copy-start | bytes 12304
  1504.0 508.0 %copy-start.40 = (f32[1025]{0:T(1024)S(1)}, f32[1025]{0:T(1024)}, u32[]{:S(2)}) copy-start(f32[1025]{0:T(1024)} %copy-done.39) | copy-start | bytes 12304
  1504.1 508.0 %copy-start.42 = (f32[384]{0:T(512)S(1)}, f32[384]{0:T(512)}, u32[]{:S(2)}) copy-start(f32[384]{0:T(512)} %param.23) | copy-start | bytes 4612
  1704.1 310.5 %copy-start.45 = (bf16[384]{0:T(512)(128)(2,1)S(1)}, bf16[384]{0:T(512)(128)(2,1)}, u32[]{:S(2)}) copy-start(bf16[384]{0:T(512)(128)(2,1)} %get-tuple-element.174) | copy-start | bytes 2308
  1704.1 310.5 %copy-start.46 = (bf16[384]{0:T(512)(128)(2,1)S(1)}, bf16[384]{0:T(512)(128)(2,1)}, u32[]{:S(2)}) copy-start(bf16[384]{0:T(512)(128)(2,1)} %get-tuple-element.176) | copy-start | bytes 2308
  1704.1 345.9 %copy-start.4 = (f32[1025,384]{1,0:T(8,128)S(1)}, f32[1025,384]{1,0:T(8,128)}, u32[]{:S(2)}) copy-start(f32[1025,384]{1,0:T(8,128)} %get-tuple-element.209) | copy-start | bytes 4723204
  (47 other events, 774.9 us)
Sparse Core Ops, SparseCore 0:
  10.2 43.7 all-gather.19
  56.1 27.3 all-gather.17
  85.8 41.0 all-gather.23
  128.9 39.8 all-gather.21
  170.8 39.8 all-gather.25
  221.1 39.1 reduce-scatter.54
  262.7 41.0 all-gather.33
  306.2 39.8 all-gather.27
  348.5 39.8 all-gather.31
  390.4 27.3 all-gather.29
  420.3 41.0 all-gather.35
  471.8 39.1 reduce-scatter.56
  513.2 79.8 all-gather.39
  595.1 26.7 all-gather.37
  623.9 79.8 all-gather.41
  705.9 78.0 all-gather.43
  798.7 38.5 reduce-scatter.58
  842.1 28.6 all-gather.45
  906.8 40.4 reduce-scatter.60
  966.6 29.6 all-gather.47
  1024.3 40.4 reduce-scatter.62
  1081.8 29.6 all-gather.49
  1115.6 95.4 reduce-scatter.52
  1215.0 95.5 reduce-scatter.50
  1314.8 95.1 reduce-scatter.48
  1412.5 23.0 reduce-scatter.66
  1438.8 64.1 reduce-scatter.70
  1506.4 62.9 reduce-scatter.68
  1572.8 63.0 reduce-scatter.46
  1639.1 63.0 reduce-scatter.44
  1705.7 62.9 reduce-scatter.42
  1772.0 63.0 reduce-scatter.36
  1838.3 63.0 reduce-scatter.38
  1904.8 62.9 reduce-scatter.40
  1970.4 39.4 reduce-scatter.64
where the time goes:
time: 2060 us
  waiting for transfers between devices  1480 us (72%)
  matrix products  295 us (14%)
  blocking collectives  133 us (6%)
  local copies, waits for them, and re-layouts  69.1 us (3%)
  other arithmetic  62.9 us (3%)
    unnamed x44, waiting for transfers between devices  397 us
    reduce_scatter x1, waiting for transfers between devices, body(): lax.psum_scatter(part_gate.astype(jnp.bfloat16), 'col', scatter_dimension...  97.1 us
    all_gather x3, waiting for transfers between devices, spread_rows(): return lax.all_gather(low_rows, 'row', axis=1, tiled=True)  87.9 us
    all_gather x1, waiting for transfers between devices, body(): lax.all_gather(shards[7], 'col', axis=0, tiled=True)  72.2 us
    all_gather x1, waiting for transfers between devices, body(): lax.all_gather(shards[10], 'col', axis=1, tiled=True)  68.6 us
    all_gather x1, waiting for transfers between devices, body(): lax.all_gather(shards[6], 'col', axis=0, tiled=True)  65.6 us
    reduce_scatter x1, waiting for transfers between devices, body(): lax.psum_scatter(part_query.astype(jnp.bfloat16), 'col', scatter_dimensio...  64.8 us
    reduce_scatter x1, waiting for transfers between devices, body(): lax.psum_scatter(part_value.astype(jnp.bfloat16), 'col', scatter_dimensio...  64.7 us
  transfers between devices with their start and end apart: 35, of which 33 were waited for; matrix products, arithmetic and copies ran while one was open for 14% of the time, Pallas kernels for 0%

commit v1 on v0

v1 whole, which is shorter than its diff:
```python
import functools
import math

import jax, jax.numpy as jnp
from jax import lax
from jax.sharding import PartitionSpec as P
from jax.experimental import pallas as pl
from jax.experimental.pallas import tpu as pltpu

BF, F32 = jnp.bfloat16, jnp.float32
MESH = pl.DeviceIdType.MESH
TP = 1040
LEN = 1025
CLEN = 130
CP = 144
HEAD = 64
ROT = 32
EPSILON = 1e-06
CH = 208
NCH = TP // CH
SUB = 16


def nt(a, b):
    return lax.dot_general(a, b, (((1,), (1,)), ((), ())), preferred_element_type=F32)


def remote(src, dst, ssem, rsem, dev):
    return pltpu.make_async_remote_copy(src_ref=src, dst_ref=dst, send_sem=ssem, recv_sem=rsem, device_id=dev, device_id_type=MESH)


def ar_kernel(mode, wide, *refs):
    n_in = {"fwd": 5, "out": 4, "bwd": 5}[mode]
    n_out = {"fwd": 2, "out": 4, "bwd": 3}[mode]
    ins, outs, scr = refs[:n_in], refs[n_in:n_in + n_out], refs[n_in + n_out:]
    (ybuf, wbuf, acc, send_a, recv_a, p1, p2, buf1, buf2, low, lsem, s_a, r_a, s_b, r_b, s_c, r_c, s_d, r_d) = scr
    half = wide // 2
    r, col = lax.axis_index("row"), lax.axis_index("col")
    c = lax.rem(r, 2)
    o = 1 - c
    sib = (r + 1 - 2 * c, col)
    xi = lax.div(r, 2)
    par = (r + 2 - 4 * xi, col)

    y_hbm, w_hbm = ins[0], ins[1]
    ycp = pltpu.make_async_copy(y_hbm, ybuf, lsem.at[0])
    wcp = pltpu.make_async_copy(w_hbm, wbuf, lsem.at[1])
    ycp.start()
    wcp.start()
    b1 = pltpu.make_async_copy(ins[2], buf1, lsem.at[2])
    b1.start()
    if mode in ("out", "bwd"):
        b2 = pltpu.make_async_copy(ins[3], buf2, lsem.at[3])
        b2.start()

    barrier = pltpu.get_barrier_semaphore()
    pl.semaphore_signal(barrier, inc=1, device_id=sib, device_id_type=MESH)
    pl.semaphore_signal(barrier, inc=1, device_id=par, device_id_type=MESH)
    pl.semaphore_wait(barrier, 2)
    ycp.wait()
    wcp.wait()

    def rows_of(i):
        return pl.ds(pl.multiple_of(i * CH, 16), CH)

    def copy_a(i):
        return remote(send_a.at[rows_of(i)], recv_a.at[rows_of(i)], s_a.at[i], r_a.at[i], sib)

    def copy_b(i):
        return remote(p1.at[c, rows_of(i)], p2.at[c, rows_of(i)], s_b.at[i], r_b.at[i], par)

    def copy_c(i):
        return remote(p1.at[c, rows_of(i)], p1.at[c, rows_of(i)], s_c.at[i], r_c.at[i], sib)

    def copy_d(i):
        return remote(p2.at[c, rows_of(i)], p2.at[c, rows_of(i)], s_d.at[i], r_d.at[i], sib)

    w_mine = pl.ds(pl.multiple_of(c * half, 128), half)
    w_other = pl.ds(pl.multiple_of(o * half, 128), half)

    def step_b(i):
        copy_a(i).wait_recv()
        p1[c, rows_of(i)] = (acc[rows_of(i)] + recv_a[rows_of(i)].astype(F32)).astype(BF)
        copy_b(i).start()
        copy_c(i).start()

    def first(i, carry):
        yc = ybuf[rows_of(i)]
        send_a[rows_of(i)] = nt(yc, wbuf[w_other]).astype(BF)
        copy_a(i).start()
        acc[rows_of(i)] = nt(yc, wbuf[w_mine])

        @pl.when(i > 0)
        def _():
            step_b(i - 1)

        return carry

    lax.fori_loop(0, NCH, first, 0)
    step_b(NCH - 1)
    b1.wait()
    if mode in ("out", "bwd"):
        b2.wait()

    gain = ins[{"fwd": 3, "out": 0, "bwd": 4}[mode]]
    if mode == "bwd":
        outs[2][...] = jnp.zeros_like(outs[2])
    if mode == "out":
        outs[3][...] = jnp.zeros_like(outs[3])

    def block(k, carry):
        rs = pl.ds(pl.multiple_of(k * SUB, SUB), SUB)
        tot = jnp.concatenate(
            [p1[0, rs].astype(F32) + p2[0, rs].astype(F32), p1[1, rs].astype(F32) + p2[1, rs].astype(F32)], axis=1
        )
        if mode == "fwd":
            x = buf1[rs] + tot
            buf1[rs] = x
            xc = x - jnp.sum(x, axis=1, keepdims=True) * (1.0 / wide)
            inv = lax.rsqrt(jnp.sum(xc * xc, axis=1, keepdims=True) * (1.0 / wide) + EPSILON)
            low[rs] = (xc * inv * gain[...] + ins[4][...]).astype(BF)
        if mode == "out":
            y = buf1[rs] + tot
            pos = k * SUB + lax.broadcasted_iota(jnp.int32, (SUB, wide), 0)
            res = jnp.where(pos < LEN, y - buf2[rs].astype(F32), 0.0)
            buf1[rs] = res
            low[rs] = res.astype(BF)
            send_a_full[rs] = y.astype(BF)
            sq = res * res
            outs[3][...] += sq[:8] + sq[8:]
        if mode == "bwd":
            x = buf2[rs]
            xc = x - jnp.sum(x, axis=1, keepdims=True) * (1.0 / wide)
            inv = lax.rsqrt(jnp.sum(xc * xc, axis=1, keepdims=True) * (1.0 / wide) + EPSILON)
            xh = xc * inv
            e = tot * gain[...]
            m1 = jnp.sum(e, axis=1, keepdims=True) * (1.0 / wide)
            m2 = jnp.sum(e * xh, axis=1, keepdims=True) * (1.0 / wide)
            gnew = buf1[rs] + inv * (e - m1 - xh * m2)
            buf1[rs] = gnew
            low[rs] = gnew.astype(BF)
            dx = tot * xh
            outs[2][0] += dx[:8] + dx[8:]
            outs[2][1] += tot[:8] + tot[8:]
        return carry

    per = CH // SUB
    send_a_full = ybuf if mode == "out" else None

    def out_copies(i):
        cps = [
            pltpu.make_async_copy(buf1.at[rows_of(i)], outs[0].at[rows_of(i)], lsem.at[4 + 2 * i]),
            pltpu.make_async_copy(low.at[rows_of(i)], outs[1].at[rows_of(i)], lsem.at[5 + 2 * i]),
        ]
        return cps

    def second(i, carry):
        copy_b(i).wait_recv()
        copy_d(i).start()

        @pl.when(i > 0)
        def _():
            finish(i - 1)

        return carry

    def finish(i):
        remote(p1.at[o, rows_of(i)], p1.at[o, rows_of(i)], s_c.at[i], r_c.at[i], sib).wait_recv()
        remote(p2.at[o, rows_of(i)], p2.at[o, rows_of(i)], s_d.at[i], r_d.at[i], sib).wait_recv()
        lax.fori_loop(i * per, (i + 1) * per, block, 0)
        for cp in out_copies(i):
            cp.start()

    lax.fori_loop(0, NCH, second, 0)
    finish(NCH - 1)

    def drain(i, carry):
        copy_a(i).wait_send()
        copy_b(i).wait_send()
        copy_c(i).wait_send()
        copy_d(i).wait_send()
        for cp in out_copies(i):
            cp.wait()
        return carry

    lax.fori_loop(0, NCH, drain, 0)
    if mode == "out":
        width = wide // 4
        cp = pltpu.make_async_copy(
            ybuf.at[:, pl.ds(pl.multiple_of(r * width, 128), width)], outs[2], lsem.at[0]
        )
        cp.start()
        cp.wait()


def ar_call(mode, cid, args, k, wide):
    vm = pl.BlockSpec(memory_space=pltpu.VMEM)
    hb = pl.BlockSpec(memory_space=pl.ANY)
    sd = jax.ShapeDtypeStruct
    outs = [sd((TP, wide), F32), sd((TP, wide), BF)]
    ospec = [hb, hb]
    if mode == "out":
        outs += [sd((TP, wide // 4), BF), sd((8, wide), F32)]
        ospec += [hb, vm]
    if mode == "bwd":
        outs += [sd((2, 8, wide), F32)]
        ospec += [vm]
    ispec = {"fwd": [hb, hb, hb, vm, vm], "out": [hb, hb, hb, hb], "bwd": [hb, hb, hb, hb, vm]}[mode]
    half = wide // 2
    ncopies = pltpu.SemaphoreType.DMA((NCH,))
    return pl.pallas_call(
        functools.partial(ar_kernel, mode, wide),
        out_shape=outs,
        in_specs=ispec,
        out_specs=ospec,
        scratch_shapes=[
            pltpu.VMEM((TP, k), BF),
            pltpu.VMEM((wide, k), BF),
            pltpu.VMEM((TP, half), F32),
            pltpu.VMEM((TP, half), BF),
            pltpu.VMEM((TP, half), BF),
            pltpu.VMEM((2, TP, half), BF),
            pltpu.VMEM((2, TP, half), BF),
            pltpu.VMEM((TP, wide), F32),
            pltpu.VMEM((TP, wide), BF if mode == "out" else F32) if mode != "fwd" else pltpu.VMEM((8, 128), F32),
            pltpu.VMEM((TP, wide), BF),
            pltpu.SemaphoreType.DMA((4 + 2 * NCH,)),
        ] + [ncopies] * 8,
        compiler_params=pltpu.CompilerParams(collective_id=cid, has_side_effects=True, vmem_limit_bytes=60 << 20),
        name=f"ar_{mode}_{cid}",
    )(*args)


NEG = -1e30


def nn(a, b):
    return jnp.dot(a, b, preferred_element_type=F32)


def lanes(shape):
    return lax.broadcasted_iota(jnp.int32, shape, len(shape) - 1)


def head_mask(value, which):
    lane = lanes(value.shape)
    keep = (lane < HEAD) if which == 0 else (lane >= HEAD)
    return jnp.where(keep, value, jnp.zeros_like(value))


def attend_rows(q_ref, q_off, k_ref, k_off, v_ref, v_off, keys, valid, out_ref, lse_ref, heads):
    def rows_step(i, carry):
        rows = pl.ds(pl.multiple_of(i * CH, 16), CH)
        lse = jnp.zeros((CH, 128), F32)
        for pair in range(heads // 2):
            qp = q_ref[rows, q_off + 128 * pair:q_off + 128 * (pair + 1)]
            kp = k_ref[:, k_off + 128 * pair:k_off + 128 * (pair + 1)]
            vp = v_ref[:, v_off + 128 * pair:v_off + 128 * (pair + 1)]
            mixed = []
            for which in range(2):
                s = nt(head_mask(qp, which), kp)
                s = jnp.where(lanes((1, keys)) < valid, s, NEG)
                top = jnp.max(s, axis=1, keepdims=True)
                e = jnp.exp(s - top)
                total = jnp.sum(e, axis=1, keepdims=True)
                mixed.append(nn(e.astype(BF), vp) / total)
                lse = jnp.where(lanes(lse.shape) == 2 * pair + which, top + jnp.log(total), lse)
            both = jnp.where(lanes(mixed[0].shape) < HEAD, mixed[0], mixed[1])
            out_ref[rows, 128 * pair:128 * (pair + 1)] = both.astype(BF)
        lse_ref[rows] = lse
        return carry

    lax.fori_loop(0, TP // CH, rows_step, 0)


def attend_back(q_ref, q_off, k_ref, k_off, v_ref, v_off, keys, kblock, valid, do_ref, out_ref, lse_ref, lse_t, delta_t, dqt, emit_q, emit_kv, heads):
    queries = q_ref.shape[0]
    lse_t[...] = lse_ref[...].T
    delta = jnp.zeros((queries, 128), F32)
    for pair in range(heads // 2):
        cols = slice(128 * pair, 128 * (pair + 1))
        prod = do_ref[:, cols].astype(F32) * out_ref[:, cols].astype(F32)
        for which in range(2):
            one = jnp.sum(head_mask(prod, which), axis=1, keepdims=True)
            delta = jnp.where(lanes(delta.shape) == 2 * pair + which, one, delta)
    delta_t[...] = delta.T
    for pair in range(heads // 2):
        qc = slice(q_off + 128 * pair, q_off + 128 * (pair + 1))
        kc = slice(k_off + 128 * pair, k_off + 128 * (pair + 1))
        vc = slice(v_off + 128 * pair, v_off + 128 * (pair + 1))
        oc = slice(128 * pair, 128 * (pair + 1))
        dqt[...] = jnp.zeros_like(dqt)

        def keys_step(j, carry):
            rows = pl.ds(pl.multiple_of(j * kblock, 16), kblock)
            kb, vb = k_ref[rows, kc], v_ref[rows, vc]
            dks, dvs = [], []
            for which in range(2):
                h = 2 * pair + which
                km = head_mask(kb, which)
                p = jnp.exp(nt(km, q_ref[:, qc]) - lse_t[h:h + 1])
                if keys != valid:
                    pos = j * kblock + lax.broadcasted_iota(jnp.int32, (kblock, 1), 0)
                    p = jnp.where(pos < valid, p, 0.0)
                dp = nt(head_mask(vb, which), do_ref[:, oc])
                ds = (p * (dp - delta_t[h:h + 1])).astype(BF)
                dvs.append(nn(p.astype(BF), do_ref[:, oc]))
                dks.append(nn(ds, q_ref[:, qc]))
                dqt[...] += nn(km.T, ds)
            low = lanes(dks[0].shape) < HEAD
            emit_kv(pair, rows, jnp.where(low, dks[0], dks[1]), jnp.where(low, dvs[0], dvs[1]))
            return carry

        lax.fori_loop(0, keys // kblock, keys_step, 0)
        emit_q(pair, dqt[...].T)


def rotate_lanes(u, cos, sin_low, sin_high):
    width = u.shape[-1]
    return u * cos + pltpu.roll(u, width - ROT // 2, u.ndim - 1) * sin_low + pltpu.roll(u, ROT // 2, u.ndim - 1) * sin_high


def qkv_kernel(wide, f, x_ref, g_ref, b_ref, w_ref, cos_ref, lo_ref, hi_ref, h_ref, x0_ref, qkv_ref, a_ref, lse_ref):
    def norm(i, carry):
        rows = pl.ds(pl.multiple_of(i * SUB, SUB), SUB)
        x = x_ref[rows].astype(F32)
        x0_ref[rows] = x
        xc = x - jnp.sum(x, axis=1, keepdims=True) * (1.0 / wide)
        inv = lax.rsqrt(jnp.sum(xc * xc, axis=1, keepdims=True) * (1.0 / wide) + EPSILON)
        h_ref[rows] = (xc * inv * g_ref[...] + b_ref[...]).astype(BF)
        return carry

    lax.fori_loop(0, TP // SUB, norm, 0)

    def project(i, carry):
        rows = pl.ds(pl.multiple_of(i * CH, 16), CH)
        cos, lo, hi = cos_ref[rows], lo_ref[rows], hi_ref[rows]
        valid = i * CH + lax.broadcasted_iota(jnp.int32, (CH, 1), 0) < LEN
        res = nn(h_ref[rows], w_ref[...])
        for part in range(3):
            for pair in range(f // 128):
                at = slice(part * f + pair * 128, part * f + (pair + 1) * 128)
                u = res[:, at]
                if part < 2:
                    u = rotate_lanes(u, cos, lo, hi).astype(BF)
                else:
                    u = u.astype(BF)
                if part == 0:
                    u = u * HEAD ** (-0.5)
                qkv_ref[rows, at] = u
        return carry

    lax.fori_loop(0, TP // CH, project, 0)
    attend_rows(qkv_ref, 0, qkv_ref, f, qkv_ref, 2 * f, TP, LEN, a_ref, lse_ref, f // HEAD)


def vspec():
    return pl.BlockSpec(memory_space=pltpu.VMEM)


def qkv_call(x, g, b, w, tables):
    wide, f = x.shape[1], w.shape[1] // 3
    sd = jax.ShapeDtypeStruct
    return pl.pallas_call(
        functools.partial(qkv_kernel, wide, f),
        out_shape=[sd((TP, wide), BF), sd((TP, wide), F32), sd((TP, 3 * f), BF), sd((TP, f), BF), sd((TP, 128), F32)],
        in_specs=[vspec()] * 7,
        out_specs=[vspec()] * 5,
        compiler_params=pltpu.CompilerParams(vmem_limit_bytes=60 << 20),
        name="qkv_attend",
    )(x, g, b, w, *tables)


def self_back_kernel(f, do_ref, w_ref, qkv_ref, a_ref, lse_ref, cos_ref, lo_ref, hi_ref, out_ref, da, lse_t, delta_t, dqt):
    da[...] = nn(do_ref[...], w_ref[...]).astype(BF)

    def emit_q(pair, dq):
        out_ref[:, 128 * pair:128 * (pair + 1)] = rotate_lanes(dq * HEAD ** (-0.5), cos_ref[...], -lo_ref[...], -hi_ref[...]).astype(BF)

    def emit_kv(pair, rows, dk, dv):
        out_ref[rows, f + 128 * pair:f + 128 * (pair + 1)] = rotate_lanes(dk, cos_ref[rows], -lo_ref[rows], -hi_ref[rows]).astype(BF)
        out_ref[rows, 2 * f + 128 * pair:2 * f + 128 * (pair + 1)] = dv.astype(BF)

    attend_back(qkv_ref, 0, qkv_ref, f, qkv_ref, 2 * f, TP, CH, LEN, da, a_ref, lse_ref, lse_t, delta_t, dqt, emit_q, emit_kv, f // HEAD)


def self_back_call(do, w, qkv, a, lse, tables):
    f = a.shape[1]
    return pl.pallas_call(
        functools.partial(self_back_kernel, f),
        out_shape=jax.ShapeDtypeStruct((TP, 3 * f), BF),
        in_specs=[vspec()] * 8,
        out_specs=vspec(),
        scratch_shapes=[pltpu.VMEM((TP, f), BF), pltpu.VMEM((128, TP), F32), pltpu.VMEM((128, TP), F32), pltpu.VMEM((128, TP), F32)],
        compiler_params=pltpu.CompilerParams(vmem_limit_bytes=60 << 20),
        name="self_back",
    )(do, w, qkv, a, lse, *tables)


def cross_kernel(f, h_ref, cond_ref, wq_ref, wkv_ref, cq_ref, ckv_ref, c_ref, lse_ref):
    ckv_ref[...] = nn(cond_ref[...], wkv_ref[...]).astype(BF)

    def project(i, carry):
        rows = pl.ds(pl.multiple_of(i * CH, 16), CH)
        cq_ref[rows] = nn(h_ref[rows], wq_ref[...]).astype(BF) * HEAD ** (-0.5)
        return carry

    lax.fori_loop(0, TP // CH, project, 0)
    attend_rows(cq_ref, 0, ckv_ref, 0, ckv_ref, f, CP, CLEN, c_ref, lse_ref, f // HEAD)


def cross_call(h, cond, wq, wkv):
    f = wq.shape[1]
    sd = jax.ShapeDtypeStruct
    return pl.pallas_call(
        functools.partial(cross_kernel, f),
        out_shape=[sd((TP, f), BF), sd((CP, 2 * f), BF), sd((TP, f), BF), sd((TP, 128), F32)],
        in_specs=[vspec()] * 4,
        out_specs=[vspec()] * 4,
        compiler_params=pltpu.CompilerParams(vmem_limit_bytes=60 << 20),
        name="cross_attend",
    )(h, cond, wq, wkv)


def cross_back_kernel(f, do_ref, w_ref, cq_ref, ckv_ref, c_ref, lse_ref, dq_ref, dkv_ref, dc, lse_t, delta_t, dqt):
    dc[...] = nn(do_ref[...], w_ref[...]).astype(BF)

    def emit_q(pair, dq):
        dq_ref[:, 128 * pair:128 * (pair + 1)] = (dq * HEAD ** (-0.5)).astype(BF)

    def emit_kv(pair, rows, dk, dv):
        dkv_ref[rows, 128 * pair:128 * (pair + 1)] = dk.astype(BF)
        dkv_ref[rows, f + 128 * pair:f + 128 * (pair + 1)] = dv.astype(BF)

    attend_back(cq_ref, 0, ckv_ref, 0, ckv_ref, f, CP, CP, CLEN, dc, c_ref, lse_ref, lse_t, delta_t, dqt, emit_q, emit_kv, f // HEAD)


def cross_back_call(do, w, cq, ckv, c, lse):
    f = c.shape[1]
    sd = jax.ShapeDtypeStruct
    return pl.pallas_call(
        functools.partial(cross_back_kernel, f),
        out_shape=[sd((TP, f), BF), sd((CP, 2 * f), BF)],
        in_specs=[vspec()] * 6,
        out_specs=[vspec()] * 2,
        scratch_shapes=[pltpu.VMEM((TP, f), BF), pltpu.VMEM((128, TP), F32), pltpu.VMEM((128, TP), F32), pltpu.VMEM((128, TP), F32)],
        compiler_params=pltpu.CompilerParams(vmem_limit_bytes=60 << 20),
        name="cross_back",
    )(do, w, cq, ckv, c, lse)


def tn(left, right):
    return lax.dot_general(left, right, (((0,), (0,)), ((), ())), preferred_element_type=F32)


def rotary_lanes():
    half_size = ROT // 2
    position = jnp.arange(TP, dtype=F32)
    frequency = jnp.exp(jnp.arange(half_size, dtype=F32) * (-2.0 * math.log(10000.0) / ROT))
    angles = position[:, None] * frequency[None, :]
    cos, sin = jnp.cos(angles), jnp.sin(angles)
    one, zero = jnp.ones((TP, HEAD - ROT), F32), jnp.zeros((TP, half_size), F32)
    rest = jnp.zeros((TP, HEAD - ROT), F32)
    tile = lambda *xs: jnp.concatenate(xs + xs, axis=1)
    return tile(cos, cos, one), tile(-sin, zero, rest), tile(zero, sin, rest)


def gather_cols(block):
    return lax.all_gather(block, "row", axis=1, tiled=True)


def own_cols(full, width):
    return lax.dynamic_slice_in_dim(full, lax.axis_index("row") * width, width, axis=1)


def pad_rows(block, rows):
    return jnp.pad(block, ((0, rows - block.shape[0]), (0, 0)))


def body(
    latents,
    conditioning,
    teacher,
    gain_attn,
    bias_attn,
    gain_cross,
    bias_cross,
    gain_mlp,
    bias_mlp,
    w_query,
    w_key,
    w_value,
    w_out,
    w_cross_query,
    w_cross_key,
    w_cross_value,
    w_cross_out,
    w_gate,
    w_up,
    w_down,
):

    wide = latents.shape[1] * lax.axis_size("row")
    F = latents.shape[1]
    FFL = w_gate.shape[1]
    small = jnp.stack([gain_attn, bias_attn, gain_cross, bias_cross, gain_mlp, bias_mlp])
    g1, b1, g2, b2, g3, b3 = jnp.split(gather_cols(small), 6, axis=0)
    x0_low = gather_cols(pad_rows(latents, TP))
    cond_full = gather_cols(pad_rows(conditioning, CP))
    teacher_full = gather_cols(pad_rows(teacher, TP))
    tables = rotary_lanes()
    gather_w = lambda *ws: lax.all_gather(jnp.concatenate(ws, axis=1), "col", axis=0, tiled=True)
    w1 = gather_w(w_query, w_key, w_value)
    w2 = gather_w(w_out.T, w_cross_query, w_cross_key, w_cross_value, w_cross_out.T)
    w3 = gather_w(w_gate, w_up, w_down.T)
    full_out, full_cquery, full_ckv, full_cout = w2[:, :F], w2[:, F:2 * F], w2[:, 2 * F:4 * F], w2[:, 4 * F:]
    full_gate_up, full_down = w3[:, :2 * FFL], w3[:, 2 * FFL:]

    h1, x0, qkv, a, lse1 = qkv_call(x0_low, g1, b1, w1, tables)
    x1, h2 = ar_call("fwd", 0, (a, full_out, x0, g2, b2), F, wide)
    cq, ckv, c, lse2 = cross_call(h2, cond_full, full_cquery, full_ckv)
    x2, h3 = ar_call("fwd", 1, (c, full_cout, x1, g3, b3), F, wide)
    gate_values = nn(h3, full_gate_up[:, :FFL])
    up_values = nn(h3, full_gate_up[:, FFL:])
    hidden = (jax.nn.silu(gate_values) * up_values).astype(BF)
    res, dm, outputs, squares = ar_call("out", 2, (hidden, full_down, x2, teacher_full), FFL, wide)
    count = LEN * wide * lax.axis_size("col")
    loss_part = jnp.sum(squares) / count
    grad_hidden = nn(dm, full_down)
    sigmoid_gate = jax.nn.sigmoid(gate_values)
    grad_gate = (
        grad_hidden * up_values * sigmoid_gate * (1.0 + gate_values * (1.0 - sigmoid_gate))
    ).astype(BF)
    grad_up = (grad_hidden * gate_values * sigmoid_gate).astype(BF)
    grad_gu = jnp.concatenate([grad_gate, grad_up], axis=1)
    scatter_w = lambda *gs: lax.psum_scatter(
        jnp.concatenate([g.astype(BF) for g in gs], axis=1), "col", scatter_dimension=0, tiled=True
    ).astype(F32)
    r3 = scatter_w(tn(h3, grad_gu), tn(dm, hidden))
    gs2, dco, sums3 = ar_call("bwd", 3, (grad_gu, full_gate_up, res, x2, g3), 2 * FFL, wide)
    grad_cq, grad_ckv = cross_back_call(dco, full_cout, cq, ckv, c, lse2)
    grad_conditioning = lax.psum_scatter(
        nt(grad_ckv, full_ckv)[:CLEN].astype(BF), "row", scatter_dimension=1, tiled=True
    )
    gs1, do, sums2 = ar_call("bwd", 4, (grad_cq, full_cquery, gs2, x1, g2), F, wide)
    r2 = scatter_w(tn(do, a), tn(h2, grad_cq), tn(cond_full, grad_ckv), tn(dco, c))
    grad_qkv = self_back_call(do, full_out, qkv, a, lse1, tables)
    r1 = scatter_w(tn(h1, grad_qkv))
    _, glat, sums1 = ar_call("bwd", 5, (grad_qkv, w1, gs1, x0, g1), 3 * F, wide)
    grad_latents = own_cols(glat, F)[:LEN]
    sums = jnp.concatenate([sums1, sums2, sums3]).sum(axis=1)
    sums, loss = lax.psum((own_cols(sums, F), loss_part), "col")
    width = F // lax.axis_size("col")
    vectors = lax.dynamic_slice_in_dim(sums, lax.axis_index("col") * width, width, axis=1)
    gq, gk, gv = jnp.split(r1, 3, axis=1)
    go, gcq, gck, gcv, gco = jnp.split(r2, 5, axis=1)
    ggate, gup, gdown = jnp.split(r3, 3, axis=1)
    return (
        outputs[:LEN], loss, grad_latents, grad_conditioning, gq, gk, gv, go.T, gcq, gck, gcv, gco.T,
        ggate, gup, gdown.T, vectors[0], vectors[1], vectors[2], vectors[3], vectors[4], vectors[5],
    )


def solution(mesh):
    in_specs = (
        P("col", "row"),
        P("col", "row"),
        P("col", "row"),
        P("row"),
        P("row"),
        P("row"),
        P("row"),
        P("row"),
        P("row"),
        P("col", "row"),
        P("col", "row"),
        P("col", "row"),
        P("row", "col"),
        P("col", "row"),
        P("col", "row"),
        P("col", "row"),
        P("row", "col"),
        P("col", "row"),
        P("col", "row"),
        P("row", "col"),
    )
    out_specs = (
        P("col", "row"),
        P(),
        P("col", "row"),
        P("col", "row"),
        P("col", "row"),
        P("col", "row"),
        P("col", "row"),
        P("row", "col"),
        P("col", "row"),
        P("col", "row"),
        P("col", "row"),
        P("row", "col"),
        P("col", "row"),
        P("col", "row"),
        P("row", "col"),
        P(("row", "col")),
        P(("row", "col")),
        P(("row", "col")),
        P(("row", "col")),
        P(("row", "col")),
        P(("row", "col")),
    )
    return jax.shard_map(body, mesh=mesh, in_specs=in_specs, out_specs=out_specs, check_vma=False)
```

time: 2060 us -> 1120 us (0.54)
  waiting for transfers between devices: 1480 us -> 477 us
  Pallas kernels: 0 us -> 405 us
  matrix products: 295 us -> 73.5 us
  blocking collectives: 133 us -> 56 us
  other arithmetic: 62.9 us -> 22.6 us
    pallas_call x0 -> x10, Pallas kernels: none -> 405 us  [the longest x6 313 us: ar_call(): pl.pallas_call(functools.partial(ar_kernel, mode, wide), out_shape=outs,...]
    all_gather x17 -> x5, waiting for transfers between devices: 592 us -> 213 us  [the longest x3 207 us: body(): lax.all_gather(jnp.concatenate(ws, axis=1), 'col', axis=0, tiled=True)]
    unnamed x44 -> x11, waiting for transfers between devices: 397 us -> 38.2 us
    reduce_scatter x9 -> x2, waiting for transfers between devices: 490 us -> 227 us  [body(): lax.psum_scatter(jnp.concatenate([g.astype(BF) for g in gs], axis=1), 'co...]
    dot_general x44 -> x11, matrix products: 295 us -> 73.5 us  [the longest x7 41.4 us: tn(): lax.dot_general(left, right, (((0,), (0,)), ((), ())), preferred_element_...]
    psum x7 -> x1, blocking collectives: 105 us -> 39.2 us  [body(): sums, loss = lax.psum((own_cols(sums, F), loss_part), 'col')]
    convert_element_type x22 -> x2, other arithmetic: 35.6 us -> 2.14 us  [body(): scatter_w = lambda *gs: lax.psum_scatter(jnp.concatenate([g.astype(BF) fo...]
    unnamed x141 -> x79, local copies, waits for them, and re-layouts: 59.7 us -> 28.5 us
  transfers between devices with their start and end apart: 35 -> 9, of which waited for: 33 -> 7; matrix products, arithmetic and copies ran while one was open for 14% -> 11% of each run, Pallas kernels for 0% -> 26%
where the time goes in v1:
time: 1120 us
  waiting for transfers between devices  477 us (43%)
  Pallas kernels  405 us (36%)
  matrix products  73.5 us (7%)
  local copies, waits for them, and re-layouts  66.6 us (6%)
  blocking collectives  56 us (5%)
  other arithmetic  22.6 us (2%)
  between operations  15.4 us (1%)
    pallas_call x6, Pallas kernels, ar_call(): pl.pallas_call(functools.partial(ar_kernel, mode, wide), out_shape=outs,...  313 us
    reduce_scatter x2, waiting for transfers between devices, body(): lax.psum_scatter(jnp.concatenate([g.astype(BF) for g in gs], axis=1), 'co...  227 us
    all_gather x3, waiting for transfers between devices, body(): lax.all_gather(jnp.concatenate(ws, axis=1), 'col', axis=0, tiled=True)  207 us
    dot_general x7, matrix products, tn(): lax.dot_general(left, right, (((0,), (0,)), ((), ())), preferred_element_...  41.4 us
    psum x1, blocking collectives, body(): sums, loss = lax.psum((own_cols(sums, F), loss_part), 'col')  39.2 us
    pallas_call x1, Pallas kernels, qkv_call(): pl.pallas_call(functools.partial(qkv_kernel, wide, f), out_shape=[sd((TP,...  38.9 us
    unnamed x11, waiting for transfers between devices  38.2 us
    pallas_call x1, Pallas kernels, self_back_call(): pl.pallas_call(functools.partial(self_back_kernel, f), out_shape=jax.Shap...  32.3 us
  transfers between devices with their start and end apart: 9, of which 7 were waited for; matrix products, arithmetic and copies ran while one was open for 11% of the time, Pallas kernels for 26%

profile of v1, /device:TPU:0, one launch (start us, length us, event | category | flops | bytes accessed | tf_op | source)
XLA Modules:
  0.0 1117.6 jit_solution(11882966065301856800)
XLA Ops:
  7.3 2.2 pad.11
  9.6 1.9 pad_maximum_fusion.4
  17.3 2.0 fusion.4
  19.4 1.8 concatenate.32.lo_ref
  21.2 1.8 concatenate.33.hi_ref
  23.0 1.8 concatenate.31.cos_ref
  24.8 6.4 all_gather.22
  31.2 10.3 all_gather.25.cond_ref
  42.2 2.2 all-gather.6.cloned.1.call-done.x_ref
  44.4 68.0 %all-gather.8.cloned.1.call-done.w_ref.refs_1_ = bf16[1536,1152]{1,0:T(8,128)(2,1)} async-done(((bf16[192,1152]{1,0:T(8,128)(2,1)}), bf16[1536,1152]{1,0:T(8,128)(2,1)}) %all-gather.8.cloned.1.call-update) | async-done | bytes 3538960 | tf_op jit(solution)/shard_map/all_gather | solution.py:512
  112.3 38.9 %qkv_attend.1 = (bf16[1040,1536]{1,0:T(8,128)(2,1)}, f32[1040,1536]{1,0:T(8,128)}, bf16[1040,1152]{1,0:T(8,128)(2,1)}, bf16[1040,384]{1,0:T(8,128)(2,1)}, f32[1040,128]{1,0:T(8,128)}) custom-call(bf16[1040,1536]{1,0:T(8,128)(2,1)} %all-gather.6.cloned.1.call-done.x_ref, f32[1,1536]{1,0:T(1,128)} %get-tuple-element.139.g_ref.refs_4_, ...), custom_call_target="tpu_custom_call" | custom-call | tf_op jit(solution)/shard_map/qkv_attend/pallas_call | solution.py:364
  151.3 56.8 %all-gather.10.cloned.1.call-done = bf16[1536,1920]{1,0:T(8,128)(2,1)} async-done(((bf16[192,1920]{1,0:T(8,128)(2,1)}), bf16[1536,1920]{1,0:T(8,128)(2,1)}) %all-gather.10.cloned.1.call-update) | async-done | bytes 5898256 | tf_op jit(solution)/shard_map/all_gather | solution.py:512
  208.1 3.9 fusion.11
  212.0 47.9 %ar_fwd_0.1 = (f32[1040,1536]{1,0:T(8,128)}, bf16[1040,1536]{1,0:T(8,128)(2,1)}) custom-call(bf16[1040,384]{1,0:T(8,128)(2,1)} %get-tuple-element.48.refs_0_.a_ref, bf16[1536,384]{1,0:T(8,128)(2,1)} %get-tuple-element.123.refs_1_.w_ref, f32[1040,1536]{1,0:T(8,128)} %get-tuple-element.49.refs_2_.refs_3_, f32[1,1536]{1,0:T(1,128)} %get-tuple-element.137.refs_3_.refs_4_, ...), custom_call_target="tpu_custom_call" | custom-call | tf_op jit(solution)/shard_map/ar_fwd_0/pallas_call | solution.py:211
  260.0 3.3 slice.73.wkv_ref
  263.2 11.9 %cross_attend.1 = (bf16[1040,384]{1,0:T(8,128)(2,1)}, bf16[144,768]{1,0:T(8,128)(2,1)}, bf16[1040,384]{1,0:T(8,128)(2,1)}, f32[1040,128]{1,0:T(8,128)}) custom-call(bf16[1040,1536]{1,0:T(8,128)(2,1)} %get-tuple-element.50.h_ref, bf16[144,1536]{1,0:T(8,128)(2,1)} %all_gather.25.cond_ref, bf16[1536,384]{1,0:T(8,128)(2,1)} %get-tuple-element.122.wq_ref.refs_1_, ...), custom_call_target="tpu_custom_call" | custom-call | tf_op jit(solution)/shard_map/cross_attend/pallas_call | solution.py:415
  275.1 47.0 %ar_fwd_1.1 = (f32[1040,1536]{1,0:T(8,128)}, bf16[1040,1536]{1,0:T(8,128)(2,1)}) custom-call(bf16[1040,384]{1,0:T(8,128)(2,1)} %get-tuple-element.51.refs_0_.c_ref, bf16[1536,384]{1,0:T(8,128)(2,1)} %get-tuple-element.121.refs_1_.w_ref, f32[1040,1536]{1,0:T(8,128)} %get-tuple-element.52.refs_2_.refs_3_, f32[1,1536]{1,0:T(1,128)} %get-tuple-element.135.refs_3_.refs_4_, ...), custom_call_target="tpu_custom_call" | custom-call | tf_op jit(solution)/shard_map/ar_fwd_1/pallas_call | solution.py:211
  322.2 81.8 %all-gather.12.cloned.1.call-done = bf16[1536,4608]{1,0:T(8,128)(2,1)} async-done(((bf16[192,4608]{1,0:T(8,128)(2,1)}), bf16[1536,4608]{1,0:T(8,128)(2,1)}) %all-gather.12.cloned.1.call-update) | async-done | bytes 14155792 | tf_op jit(solution)/shard_map/all_gather | solution.py:512
  404.0 4.7 slice.77.refs_1_
  408.7 7.2 fusion.2
  416.0 2.6 copy-done.32
  418.6 10.1 multiply_convert_fusion.2
  428.7 3.7 all-gather.14.cloned.1.call-done.refs_3_
  432.4 48.3 %ar_out_2.1 = (f32[1040,1536]{1,0:T(8,128)}, bf16[1040,1536]{1,0:T(8,128)(2,1)}, bf16[1040,384]{1,0:T(8,128)(2,1)}, f32[8,1536]{1,0:T(8,128)}) custom-call(bf16[1040,1536]{1,0:T(8,128)(2,1)} %get-tuple-element.149.refs_0_, bf16[1536,1536]{1,0:T(8,128)(2,1)} %slice.77.refs_1_, f32[1040,1536]{1,0:T(8,128)} %get-tuple-element.54.refs_2_.refs_3_, ...), custom_call_target="tpu_custom_call" | custom-call | tf_op jit(solution)/shard_map/ar_out_2/pallas_call | solution.py:211
  480.7 12.1 %multiply_convert_fusion.1 = (bf16[1040,1536]{1,0:T(8,128)(2,1)S(1)}, bf16[1040,1536]{1,0:T(8,128)(2,1)S(1)}) fusion(f32[1040,1536]{1,0:T(8,128)} %copy-done.32, f32[1040,1536]{1,0:T(8,128)} %get-tuple-element.150, bf16[1040,1536]{1,0:T(8,128)(2,1)} %get-tuple-element.57, bf16[1536,4608]{1,0:T(8,128)(2,1)} %all-gather.12.cloned.1.call-done), kind=kOutput, calls=%fused_computation.6 | convolution fusion | flops 4928102400 | bytes 27082752 | tf_op jit(solution)/shard_map/dot_general | solution.py:238
  495.5 3.4 pad_maximum_fusion.1.refs_0_
  498.9 8.1 slice.78.refs_1_
  507.0 61.5 %ar_bwd_3.1 = (f32[1040,1536]{1,0:T(8,128)}, bf16[1040,1536]{1,0:T(8,128)(2,1)}, f32[2,8,1536]{2,1,0:T(8,128)}) custom-call(bf16[1040,3072]{1,0:T(8,128)(2,1)} %pad_maximum_fusion.1.refs_0_, bf16[1536,3072]{1,0:T(8,128)(2,1)} %slice.78.refs_1_, f32[1040,1536]{1,0:T(8,128)} %get-tuple-element.58.refs_2_, f32[1040,1536]{1,0:T(8,128)} %get-tuple-element.54.refs_2_.refs_3_, ...), custom_call_target="tpu_custom_call" | custom-call | tf_op jit(solution)/shard_map/ar_bwd_3/pallas_call | solution.py:211
  568.5 9.5 cross_back.1
  578.1 2.7 fusion.7
  582.0 54.4 %ar_bwd_4.1 = (f32[1040,1536]{1,0:T(8,128)}, bf16[1040,1536]{1,0:T(8,128)(2,1)}, f32[2,8,1536]{2,1,0:T(8,128)}) custom-call(bf16[1040,384]{1,0:T(8,128)(2,1)} %get-tuple-element.63.refs_0_, bf16[1536,384]{1,0:T(8,128)(2,1)} %get-tuple-element.122.wq_ref.refs_1_, f32[1040,1536]{1,0:T(8,128)} %get-tuple-element.64.refs_2_, ...), custom_call_target="tpu_custom_call" | custom-call | tf_op jit(solution)/shard_map/ar_bwd_4/pallas_call | solution.py:211
  636.4 32.3 %self_back.1.refs_0_ = bf16[1040,1152]{1,0:T(8,128)(2,1)} custom-call(bf16[1040,1536]{1,0:T(8,128)(2,1)} %get-tuple-element.65.do_ref, bf16[1536,384]{1,0:T(8,128)(2,1)} %get-tuple-element.123.refs_1_.w_ref, bf16[1040,1152]{1,0:T(8,128)(2,1)} %get-tuple-element.66.qkv_ref, bf16[1040,384]{1,0:T(8,128)(2,1)} %get-tuple-element.48.refs_0_.a_ref, ...), custom_call_target="tpu_custom_call" | custom-call | tf_op jit(solution)/shard_map/self_back/pallas_call | solution.py:389
  668.7 8.4 convolution_convert_fusion.2
  679.0 3.8 convolution_convert_fusion.4
  686.7 3.0 pad_maximum_fusion.2
  689.7 8.6 copy.56
  698.3 1.8 copy-done.2
  700.2 8.6 convolution_convert_fusion.1
  708.8 16.3 %convolution_convert_fusion = bf16[1536,3072]{1,0:T(8,128)(2,1)S(1)} fusion(bf16[1040,1536]{1,0:T(8,128)(2,1)} %get-tuple-element.53, bf16[1040,1536]{1,0:T(8,128)(2,1)} %copy-done.6, bf16[1040,1536]{1,0:T(8,128)(2,1)} %copy-done.5), kind=kOutput, calls=%fused_computation.1 | convolution fusion | flops 9832169472 | bytes 19021824 | tf_op jit(solution)/shard_map/dot_general | solution.py:453
  725.0 7.2 pad_maximum_fusion
  734.4 53.7 %ar_bwd_5.1 = (f32[1040,1536]{1,0:T(8,128)}, bf16[1040,1536]{1,0:T(8,128)(2,1)}, f32[2,8,1536]{2,1,0:T(8,128)}) custom-call(bf16[1040,1152]{1,0:T(8,128)(2,1)} %self_back.1.refs_0_, bf16[1536,1152]{1,0:T(8,128)(2,1)} %all-gather.8.cloned.1.call-done.w_ref.refs_1_, f32[1040,1536]{1,0:T(8,128)} %get-tuple-element.68.refs_2_, ...), custom_call_target="tpu_custom_call" | custom-call | tf_op jit(solution)/shard_map/ar_bwd_5/pallas_call | solution.py:211
  789.1 39.2 %all-reduce.3 = (f32[]{:T(128)}, f32[6,384]{1,0:T(8,128)S(1)}) all-reduce(f32[]{:T(128)S(6)} %div.9, f32[6,384]{1,0:T(8,128)S(1)} %constant_dynamic-slice_fusion.1), channel_id=1, replica_groups=mesh['row'=4,'col'=8] {'col'}, use_global_device_ids=true, to_apply=%region_1.2 | all-reduce | flops 2305 | bytes 18440 | tf_op jit(solution)/shard_map/psum | solution.py:552
  829.9 2.1 constant_dynamic-slice_fusion.2
  833.7 2.0 fusion.14
  835.7 38.1 %reduce-scatter.15.cloned.1.call-done = bf16[192,1920]{1,0:T(8,128)(2,1)} async-done(((bf16[1536,1920]{1,0:T(8,128)(2,1)}), bf16[192,1920]{1,0:T(8,128)(2,1)}) %reduce-scatter.15.cloned.1.call-update) | async-done | bytes 737296
  880.2 226.7 %reduce-scatter.11.cloned.1.call-done = bf16[192,4608]{1,0:T(8,128)(2,1)} async-done(((bf16[1536,4608]{1,0:T(8,128)(2,1)}), bf16[192,4608]{1,0:T(8,128)(2,1)}) %reduce-scatter.11.cloned.1.call-update) | async-done | bytes 1769488 | tf_op jit(solution)/shard_map/reduce_scatter | solution.py:536
  1106.9 2.0 convert_element_type.57
  1108.9 1.9 fusion.12
  (125 shorter events, 28.2 us)
Async XLA Ops:
  7.2 4.4 copy-start.17
  7.2 4.4 copy-start.18
  7.2 4.4 copy-start.19
  7.2 7.3 copy-start.13
  7.2 7.3 copy-start.14
  7.2 7.3 copy-start.15
  7.3 37.1 %all-gather.6.cloned.1.call-start = ((), (), s32[]{:S(2)}) async-start(), calls=%async_computation.4 | async-start | bytes 3993600 | tf_op jit(solution)/shard_map/all_gather | solution.py:469
  9.6 102.8 %all-gather.8.cloned.1.call-start = ((), (), s32[]{:S(2)}) async-start(), calls=%async_computation.5 | async-start | bytes 3981312 | tf_op jit(solution)/shard_map/all_gather | solution.py:512
  11.5 196.6 %all-gather.10.cloned.1.call-start = ((), (), s32[]{:S(2)}) async-start(), calls=%async_computation.6 | async-start | bytes 6635520 | tf_op jit(solution)/shard_map/all_gather | solution.py:512
  11.6 4.5 copy-start.11
  13.6 0.9 copy-start.9
  14.5 389.5 %all-gather.12.cloned.1.call-start = ((), (), s32[]{:S(2)}) async-start(), calls=%async_computation.7 | async-start | bytes 15925248 | tf_op jit(solution)/shard_map/all_gather | solution.py:512
  14.6 2.6 copy-start.24
  14.6 2.6 copy-start.25
  14.6 2.6 copy-start.26
  14.6 2.7 copy-start.27
  14.6 2.7 copy-start.28
  14.7 2.7 copy-start.29
  16.1 416.3 %all-gather.14.cloned.1.call-start = ((), (), s32[]{:S(2)}) async-start(), calls=%async_computation.8 | async-start | bytes 3993600 | tf_op jit(solution)/shard_map/all_gather | solution.py:469
  17.2 814.9 %reduce-scatter.13.cloned.1.call-start = ((), (), s32[]{:S(2)}) async-start(), calls=%async_computation.11 | async-start | bytes 983040
  19.4 3.5 copy-start.20
  322.2 86.6 %copy-start.30 = (bf16[1040,1536]{1,0:T(8,128)(2,1)S(1)}, bf16[1040,1536]{1,0:T(8,128)(2,1)}, u32[]{:S(2)}) copy-start(bf16[1040,1536]{1,0:T(8,128)(2,1)} %get-tuple-element.53) | copy-start | bytes 9584644
  415.9 2.6 copy-start.32
  492.8 1.7 copy-start.5
  492.9 2.6 copy-start.6
  582.0 251.7 %reduce-scatter.9.cloned.1.call-start = ((), (), s32[]{:S(2)}) async-start(), calls=%async_computation.9 | async-start | bytes 3981312 | tf_op jit(solution)/shard_map/reduce_scatter | solution.py:536
  636.4 32.3 %copy-start.31 = (bf16[1040,1536]{1,0:T(8,128)(2,1)S(1)}, bf16[1040,1536]{1,0:T(8,128)(2,1)}, u32[]{:S(2)}) copy-start(bf16[1040,1536]{1,0:T(8,128)(2,1)} %get-tuple-element.71) | copy-start | bytes 9584644
  677.0 1.0 copy-start.1
  677.0 1.1 copy-start.16
  677.0 2.0 copy-start.3
  677.1 196.7 %reduce-scatter.15.cloned.1.call-start = ((), (), s32[]{:S(2)}) async-start(), calls=%async_computation.12 | async-start | bytes 6635520
  679.0 3.8 copy-start.4
  679.0 3.8 copy-start.10
  682.8 1.9 copy-start.7
  682.8 2.1 copy-start.8
  698.2 1.9 copy-start.2
  698.3 408.6 %reduce-scatter.11.cloned.1.call-start = ((), (), s32[]{:S(2)}) async-start(), calls=%async_computation.10 | async-start | bytes 15925248 | tf_op jit(solution)/shard_map/reduce_scatter | solution.py:536
  732.3 0.8 copy-start.23
  734.4 53.7 %copy-start.21 = (f32[2,8,1536]{2,1,0:T(8,128)S(1)}, f32[2,8,1536]{2,1,0:T(8,128)}, u32[]{:S(2)}) copy-start(f32[2,8,1536]{2,1,0:T(8,128)} %get-tuple-element.74) | copy-start | bytes 294916
  734.4 53.7 %copy-start.22 = (f32[2,8,1536]{2,1,0:T(8,128)S(1)}, f32[2,8,1536]{2,1,0:T(8,128)}, u32[]{:S(2)}) copy-start(f32[2,8,1536]{2,1,0:T(8,128)} %get-tuple-element.73) | copy-start | bytes 294916
  734.4 94.0 %copy-start.12 = (bf16[1040,384]{1,0:T(8,128)(2,1)S(1)}, bf16[1040,384]{1,0:T(8,128)(2,1)}, u32[]{:S(2)}) copy-start(bf16[1040,384]{1,0:T(8,128)(2,1)} %get-tuple-element.55) | copy-start | bytes 2396164
  1106.9 2.0 copy-start
Sparse Core Ops, SparseCore 0:
  10.2 34.0 all-gather.5
  47.1 65.1 all-gather.7
  115.1 92.9 all-gather.9
  210.2 193.7 all-gather.11
  405.4 26.9 all-gather.13
  582.1 28.0 reduce-scatter.12
  677.2 79.8 reduce-scatter.8
  761.2 112.5 reduce-scatter.14
  877.9 228.9 reduce-scatter.10

commit v2 on v1

v2 whole, which is shorter than its diff:
```python
import functools
import math

import jax, jax.numpy as jnp
from jax import lax
from jax.sharding import PartitionSpec as P
from jax.experimental import pallas as pl
from jax.experimental.pallas import tpu as pltpu

BF, F32 = jnp.bfloat16, jnp.float32
MESH = pl.DeviceIdType.MESH
TP = 1040
LEN = 1025
CLEN = 130
CP = 144
HEAD = 64
ROT = 32
EPSILON = 1e-06
CH = 208
NCH = TP // CH
SUB = 16


def nt(a, b):
    return lax.dot_general(a, b, (((1,), (1,)), ((), ())), preferred_element_type=F32)


def remote(src, dst, ssem, rsem, dev):
    return pltpu.make_async_remote_copy(src_ref=src, dst_ref=dst, send_sem=ssem, recv_sem=rsem, device_id=dev, device_id_type=MESH)


def tn(left, right):
    return lax.dot_general(left, right, (((0,), (0,)), ((), ())), preferred_element_type=F32)


def row_stats(x, wide):
    xc = x - jnp.sum(x, axis=1, keepdims=True) * (1.0 / wide)
    inv = lax.rsqrt(jnp.sum(xc * xc, axis=1, keepdims=True) * (1.0 / wide) + EPSILON)
    return xc * inv, inv


def rotate_lanes(u, cos, sin_low, sin_high):
    width = u.shape[-1]
    return u * cos + pltpu.roll(u, width - ROT // 2, u.ndim - 1) * sin_low + pltpu.roll(u, ROT // 2, u.ndim - 1) * sin_high


def vspec():
    return pl.BlockSpec(memory_space=pltpu.VMEM)


def hspec():
    return pl.BlockSpec(memory_space=pl.ANY)


class Place:
    def __init__(self, n):
        self.n, self.outer = n, n // 2
        self.r, self.col = lax.axis_index("row"), lax.axis_index("col")
        self.c = lax.rem(self.r, 2)
        self.o = 1 - self.c
        self.xi = lax.div(self.r, 2)
        self.sib = (self.r + 1 - 2 * self.c, self.col)
        self.par = (self.r + 2 - 4 * self.xi, self.col)
        self.diag = (self.par[0] + 1 - 2 * self.c, self.col)
        self.zo, self.yi = lax.div(self.col, 2), lax.rem(self.col, 2)
        self.ypar = (self.r, self.col + 1 - 2 * self.yi)

    def zpeer(self, step):
        return lax.rem(self.zo + step, self.outer)

    def near(self, z):
        gap = z - self.zo
        return jnp.logical_and(gap < 3, gap > -3)

    def enter(self, with_cols, diagonal=False):
        barrier = pltpu.get_barrier_semaphore()
        pl.semaphore_signal(barrier, inc=1, device_id=self.sib, device_id_type=MESH)
        pl.semaphore_signal(barrier, inc=1, device_id=self.par, device_id_type=MESH)
        count = 2
        if diagonal:
            pl.semaphore_signal(barrier, inc=1, device_id=self.diag, device_id_type=MESH)
            count += 1
        if with_cols:
            pl.semaphore_signal(barrier, inc=1, device_id=self.ypar, device_id_type=MESH)

            def greet(step, carry):
                pl.semaphore_signal(barrier, inc=1, device_id=(self.r, 2 * self.zpeer(step) + self.yi), device_id_type=MESH)
                return carry

            lax.fori_loop(1, self.outer, greet, 0)
            count += self.outer
        pl.semaphore_wait(barrier, count)


class ColGather:
    def __init__(self, place, pieces, ahead, ssem, rsem, lsem):
        self.at, self.pieces, self.ahead, self.ssem, self.rsem, self.lsem = place, pieces, ahead, ssem, rsem, lsem
        self.line = place.outer == 4

    def rows(self, p, j):
        size = self.pieces[p][0].shape[0]
        return self.pieces[p][1].at[pl.ds(pl.multiple_of(j * size, 16), size)]

    def local(self, p):
        return pltpu.make_async_copy(self.pieces[p][0], self.rows(p, self.at.col), self.lsem.at[p])

    def send(self, p, slot, j, to, own=False):
        src = self.pieces[p][0] if own else self.rows(p, j)
        return remote(src, self.rows(p, j), self.ssem.at[p, slot], self.rsem.at[p, j], to)

    def across(self, p):
        return self.send(p, 0, self.at.col, self.at.ypar, own=True)

    def outward(self, p, step):
        at = self.at
        return self.send(p, step, at.col, (at.r, 2 * at.zpeer(step) + at.yi), own=True)

    def onward(self, p, step):
        at = self.at
        return self.send(p, at.outer - 1 + step, 2 * at.zpeer(at.outer - step) + at.yi, at.ypar)

    def steps(self, fn, source, far=False):
        at = self.at
        if far and not self.line:
            return

        def one(step):
            if not self.line:
                fn(step)
                return
            near = at.near(at.zpeer(at.outer - step) if source else at.zpeer(step))
            pl.when(jnp.logical_not(near) if far else near)(lambda: fn(step))

        each(1, at.outer, one)

    def relay(self, p, act):
        if not self.line:
            return
        at = self.at
        for mine, source, end in ((2, 0, 3), (1, 3, 0)):
            pl.when(at.zo == mine)(lambda: act(self.send(p, at.n - 1, 2 * source + at.yi, (at.r, 2 * end + at.yi))))

    def start(self, p):
        if p < len(self.pieces):
            self.local(p).start()
            self.across(p).start()
            self.steps(lambda step: self.outward(p, step).start(), False)

    def pass_on(self, p, far):
        def one(step):
            cp = self.onward(p, step)
            cp.wait_recv()
            cp.start()

        self.steps(one, True, far)

    def begin(self):
        for p in range(self.ahead):
            self.start(p)

    def advance(self, p):
        self.pass_on(p, False)
        self.relay(p, lambda cp: cp.start())
        self.start(p + self.ahead)
        if p > 0:
            self.pass_on(p - 1, True)
        if p == len(self.pieces) - 1:
            self.pass_on(p, True)

    def finish(self, p):
        at = self.at
        self.local(p).wait()
        self.across(p).wait_send()
        self.steps(lambda step: self.outward(p, step).wait_send(), False)
        each(0, at.outer, lambda z: self.send(p, 0, 2 * z + 1 - at.yi, at.ypar).wait_recv())
        self.steps(lambda step: self.onward(p, step).wait_send(), True)
        self.steps(lambda step: self.onward(p, step).wait_send(), True, far=True)
        self.relay(p, lambda cp: cp.wait_send())


def gather_sems(pieces, n):
    return [pltpu.SemaphoreType.DMA((pieces, n)), pltpu.SemaphoreType.DMA((pieces, n)), pltpu.SemaphoreType.DMA((pieces,))]


class ColScatter:
    def __init__(self, place, pieces, ahead, slots, bufs, sems):
        self.at, self.pieces, self.ahead, self.slots = place, pieces, ahead, slots
        self.ry, self.hb, self.rz, self.rl, self.ob, self.obt = bufs
        self.ls, self.sy, self.ryr, self.sz, self.rzr, self.rlr, self.os, self.credit = sems
        self.line = place.outer == 4
        self.size = self.hb.shape[2]

    def rows(self, p, j):
        return self.pieces[p][0].at[pl.ds(pl.multiple_of(j * self.size, 16), self.size)]

    def across(self, p, z):
        at = self.at
        return remote(
            self.rows(p, 2 * z + 1 - at.yi), self.ry.at[p % self.slots, z], self.sy.at[p, z], self.ryr.at[p, z], at.ypar
        )

    def own(self, p, z):
        return pltpu.make_async_copy(self.rows(p, 2 * z + self.at.yi), self.hb.at[p % self.slots, z], self.ls.at[p, z])

    def outward(self, p, z):
        at, s = self.at, p % self.slots
        return remote(self.hb.at[s, z], self.rz.at[s, at.zo], self.sz.at[p, z], self.rzr.at[p, at.zo], (at.r, 2 * z + at.yi))

    def detour(self, p, z):
        at, s = self.at, p % self.slots
        via = lax.div(at.zo, 3) + 1
        return remote(self.hb.at[s, z], self.rl.at[s], self.sz.at[p, z], self.rlr.at[p], (at.r, 2 * via + at.yi))

    def merging(self, z):
        zo = self.at.zo
        return jnp.logical_or(jnp.logical_and(zo == 1, z == 3), jnp.logical_and(zo == 2, z == 0))

    def arrives(self, zs):
        return self.at.near(zs)

    def blocks(self, fn):
        each(0, self.size // 48, lambda k: fn(pl.ds(pl.multiple_of(k * 48, 16), 48)))

    def begin(self):
        for p in range(self.ahead):
            self.start(p)

    def start(self, p):
        if p >= len(self.pieces):
            return
        if p >= self.slots:
            pl.semaphore_wait(self.credit.at[p - self.slots], self.at.outer)

        def one(z):
            self.across(p, z).start()
            self.own(p, z).start()

        each(0, self.at.outer, one)

    def reduce(self, p):
        at, s = self.at, p % self.slots

        def one(step):
            z = at.zpeer(step)
            self.own(p, z).wait()
            self.across(p, z).wait_recv()

            def add(rs):
                self.hb[s, z, rs] = (self.hb[s, z, rs].astype(F32) + self.ry[s, z, rs].astype(F32)).astype(BF)

            self.blocks(add)

            @pl.when(z != at.zo)
            def _():
                if not self.line:
                    self.outward(p, z).start()
                    return
                near = at.near(z)
                pl.when(jnp.logical_not(near))(lambda: self.detour(p, z).start())
                pl.when(jnp.logical_and(near, jnp.logical_not(self.merging(z))))(lambda: self.outward(p, z).start())

        each(1, at.outer + 1, one)

    def merge(self, p):
        if not self.line:
            return
        at, s = self.at, p % self.slots
        for mine, z, origin in ((1, 3, 0), (2, 0, 3)):
            @pl.when(at.zo == mine)
            def _():
                remote(self.rl.at[s], self.rl.at[s], self.sz.at[p, z], self.rlr.at[p], at.ypar).wait_recv()

                def add(rs):
                    self.hb[s, z, rs] = (self.hb[s, z, rs].astype(F32) + self.rl[s, rs].astype(F32)).astype(BF)

                self.blocks(add)
                self.outward(p, z).start()

    def result(self, p):
        flip = self.pieces[p][2]
        src = self.obt if flip else self.ob
        return pltpu.make_async_copy(src.at[p % 2], self.pieces[p][1], self.os.at[p])

    def finish(self, p):
        at, s = self.at, p % self.slots
        flip = self.pieces[p][2]
        if p >= 2:
            self.result(p - 2).wait()

        def first(rs):
            self.ob[p % 2, rs] = self.hb[s, at.zo, rs].astype(F32)

        self.blocks(first)

        def one(step):
            zs = at.zpeer(at.outer - step)

            def take():
                remote(self.rz.at[s, zs], self.rz.at[s, zs], self.sz.at[p, zs], self.rzr.at[p, zs], at.ypar).wait_recv()

                def add(rs):
                    self.ob[p % 2, rs] += self.rz[s, zs, rs].astype(F32)

                self.blocks(add)

            if self.line:
                pl.when(at.near(zs))(take)
            else:
                take()

        each(1, at.outer, one)
        if flip:
            self.obt[p % 2] = self.ob[p % 2].T
        self.result(p).start()

        def sent(z):
            self.across(p, z).wait_send()

            @pl.when(z != at.zo)
            def _():
                self.outward(p, z).wait_send()

        each(0, at.outer, sent)
        if p + self.slots < len(self.pieces):
            pl.semaphore_signal(self.credit.at[p], inc=1, device_id=at.ypar, device_id_type=MESH)
            each(
                1,
                at.outer,
                lambda step: pl.semaphore_signal(
                    self.credit.at[p], inc=1, device_id=(at.r, 2 * at.zpeer(step) + at.yi), device_id_type=MESH
                ),
            )

    def advance(self, p):
        if p < len(self.pieces):
            self.reduce(p)
        if 0 <= p - 1 < len(self.pieces):
            self.merge(p - 1)
        if 0 <= p - 2 < len(self.pieces):
            self.finish(p - 2)
        self.start(p + self.ahead)

    def complete(self):
        count = len(self.pieces)
        self.advance(count)
        self.advance(count + 1)
        for p in range(max(0, count - 2), count):
            self.result(p).wait()


def scatter_scratch(pieces, slots, n, f, rows):
    size, outer = rows // n, n // 2
    dma = pltpu.SemaphoreType.DMA
    block = lambda *lead: pltpu.VMEM(lead + (size, f), BF)
    return [
        block(slots, outer), block(slots, outer), block(slots, outer), block(slots),
        pltpu.VMEM((2, size, f), F32), pltpu.VMEM((2, f, size), F32),
    ], [
        dma((pieces, outer)), dma((pieces, outer)), dma((pieces, outer)), dma((pieces, outer)), dma((pieces, outer)),
        dma((pieces,)), dma((pieces,)), pltpu.SemaphoreType.REGULAR((pieces,)),
    ]


class RowGather:
    def __init__(self, place, pieces, ssem, rsem, lsem):
        self.at, self.pieces, self.ssem, self.rsem, self.lsem = place, pieces, ssem, rsem, lsem

    def cols(self, p, j):
        size = self.pieces[p][0].shape[1]
        return self.pieces[p][1].at[:, pl.ds(pl.multiple_of(j * size, 128), size)]

    def copies(self, p):
        at = self.at
        src, mine = self.pieces[p][0], self.cols(p, at.r)
        theirs = self.cols(p, at.par[0])
        return (
            pltpu.make_async_copy(src, mine, self.lsem.at[p]),
            remote(src, mine, self.ssem.at[p, 0], self.rsem.at[p, 0], at.sib),
            remote(src, mine, self.ssem.at[p, 1], self.rsem.at[p, 1], at.par),
            remote(theirs, theirs, self.ssem.at[p, 2], self.rsem.at[p, 2], at.sib),
        )

    def start(self, p):
        for cp in self.copies(p)[:3]:
            cp.start()

    def forward(self, p):
        local, near, far, on = self.copies(p)
        far.wait_recv()
        on.start()

    def finish(self, p):
        local, near, far, on = self.copies(p)
        local.wait()
        near.wait_recv()
        on.wait_recv()
        near.wait_send()
        far.wait_send()
        on.wait_send()


class RowReduce:
    def __init__(self, at, send_a, recv_a, acc, p1, p2, sems):
        self.at, self.send_a, self.recv_a, self.acc, self.p1, self.p2 = at, send_a, recv_a, acc, p1, p2
        self.s_a, self.r_a, self.s_b, self.r_b, self.s_c, self.r_c, self.s_d, self.r_d = sems
        self.half = p1.shape[2]

    def copy_a(self, i):
        rows = rows_of(i)
        return remote(self.send_a.at[rows], self.recv_a.at[rows], self.s_a.at[i], self.r_a.at[i], self.at.sib)

    def copy_b(self, i):
        rows, c = rows_of(i), self.at.c
        return remote(self.p1.at[c, rows], self.p2.at[c, rows], self.s_b.at[i], self.r_b.at[i], self.at.par)

    def copy_c(self, i, side):
        rows = rows_of(i)
        return remote(self.p1.at[side, rows], self.p1.at[side, rows], self.s_c.at[i], self.r_c.at[i], self.at.sib)

    def copy_d(self, i, side):
        rows = rows_of(i)
        return remote(self.p2.at[side, rows], self.p2.at[side, rows], self.s_d.at[i], self.r_d.at[i], self.at.sib)

    def partial(self, i, value, w):
        c, o, half = self.at.c, self.at.o, self.half
        self.send_a[rows_of(i)] = nt(value, w[pl.ds(pl.multiple_of(o * half, 128), half)]).astype(BF)
        self.copy_a(i).start()
        self.acc[lax.rem(i, 2)] = nt(value, w[pl.ds(pl.multiple_of(c * half, 128), half)])

    def swap(self, i):
        self.copy_a(i).wait_recv()
        self.p1[self.at.c, rows_of(i)] = (self.acc[lax.rem(i, 2)] + self.recv_a[rows_of(i)].astype(F32)).astype(BF)
        self.copy_b(i).start()
        self.copy_c(i, self.at.c).start()

    def share(self, i):
        self.copy_b(i).wait_recv()
        self.copy_d(i, self.at.c).start()

    def ready(self, i):
        self.copy_c(i, self.at.o).wait_recv()
        self.copy_d(i, self.at.o).wait_recv()

    def total(self, rs):
        p1, p2 = self.p1, self.p2
        return jnp.concatenate(
            [p1[0, rs].astype(F32) + p2[0, rs].astype(F32), p1[1, rs].astype(F32) + p2[1, rs].astype(F32)], axis=1
        )

    def drain(self, i):
        self.copy_a(i).wait_send()
        self.copy_b(i).wait_send()
        self.copy_c(i, self.at.c).wait_send()
        self.copy_d(i, self.at.c).wait_send()


def reduce_scratch(wide, both):
    half = wide // 2
    out = [
        pltpu.VMEM((TP, half), BF), pltpu.VMEM((TP, half), BF), pltpu.VMEM((2, CH, half), F32),
        pltpu.VMEM((2, TP, half), BF), pltpu.VMEM((2, TP, half), BF),
    ]
    if both:
        out.append(pltpu.VMEM((2, TP, half), BF))
    return out + [pltpu.SemaphoreType.DMA((NCH,))] * (16 if both else 8)


def rows_of(i):
    return pl.ds(pl.multiple_of(i * CH, 16), CH)


def each(low, high, fn):
    def body(i, carry):
        fn(i)
        return carry

    lax.fori_loop(low, high, body, 0)


def sub_blocks(i, fn):
    each(0, CH // SUB, lambda k: fn(k, pl.ds(pl.multiple_of(i * CH + k * SUB, SUB), SUB), pl.ds(pl.multiple_of(k * SUB, SUB), SUB)))


def mid_kernel(n, f, nbg, ahead, *refs):
    refs = list(refs)
    take = lambda count: [refs.pop(0) for _ in range(count)]
    a_hbm, x0_hbm, vecs, cond_ref, wo_hbm, wq_hbm, wk_hbm, wv_hbm, wc_hbm = take(9)
    bg_in = take(nbg)
    x1_out, h2_out, cq_ref, ckv_ref, c_ref, lse_ref, x2_out, h3_out = take(8)
    bg_out = take(nbg)
    a_buf, x0_buf, x_buf, low, wo, wq, wk, wv, wc, lsem, osem = take(11)
    send_a, recv_a, acc, p1, p2, p2b = take(6)
    sems = take(16)
    at = Place(n)
    wide = x_buf.shape[1]
    first = RowReduce(at, send_a, recv_a, acc, p1, p2, sems[:8])
    second = RowReduce(at, send_a, recv_a, acc, p1, p2b, sems[8:])
    gather = ColGather(at, list(zip(bg_in, bg_out)), ahead, *take(3)) if nbg else None
    loads = [
        pltpu.make_async_copy(src, dst, lsem.at[k])
        for k, (src, dst) in enumerate(
            ((a_hbm, a_buf), (wo_hbm, wo), (wk_hbm, wk), (wv_hbm, wv), (x0_hbm, x0_buf), (wq_hbm, wq), (wc_hbm, wc))
        )
    ]
    for cp in loads:
        cp.start()
    at.enter(nbg > 0)
    gather.begin()
    for cp in loads[:2]:
        cp.wait()

    def project(i):
        first.partial(i, a_buf[rows_of(i)], wo)
        pl.when(i > 0)(lambda: first.swap(i - 1))

    each(0, NCH, project)
    first.swap(NCH - 1)
    for cp in loads[2:]:
        cp.wait()
    ckv_ref[:, :f] = nn(cond_ref[...], wk[...]).astype(BF)
    ckv_ref[:, f:] = nn(cond_ref[...], wv[...]).astype(BF)

    def outs(i, main, lowest, which):
        return [
            pltpu.make_async_copy(x_buf.at[rows_of(i)], main.at[rows_of(i)], osem.at[which, 2 * i]),
            pltpu.make_async_copy(low.at[rows_of(i)], lowest.at[rows_of(i)], osem.at[which, 2 * i + 1]),
        ]

    def hook(slot):
        for k in range(nbg):
            pl.when(slot == k * 2 * NCH // nbg)(lambda: gather.advance(k))

    def cross(i):
        first.ready(i)

        def block(k, rs, ls):
            x = x0_buf[rs].astype(F32) + first.total(rs)
            x_buf[rs] = x
            low[rs] = (row_stats(x, wide)[0] * vecs[2:3] + vecs[3:4]).astype(BF)

        sub_blocks(i, block)
        for cp in outs(i, x1_out, h2_out, 0):
            cp.start()
        rows = rows_of(i)
        cq_ref[rows] = nn(low[rows], wq[...]).astype(BF) * HEAD ** (-0.5)
        attend_step(i, cq_ref, 0, ckv_ref, 0, ckv_ref, f, CP, CLEN, c_ref, lse_ref, f // HEAD)
        first.drain(i)
        second.partial(i, c_ref[rows], wc)
        pl.when(i > 0)(lambda: second.swap(i - 1))

    def step(i):
        first.share(i)
        pl.when(i > 0)(lambda: cross(i - 1))
        hook(i)

    each(0, NCH, step)
    cross(NCH - 1)
    second.swap(NCH - 1)

    def last(i):
        second.ready(i)
        for cp in outs(i, x1_out, h2_out, 0):
            cp.wait()

        def block(k, rs, ls):
            x = x_buf[rs] + second.total(rs)
            x_buf[rs] = x
            low[rs] = (row_stats(x, wide)[0] * vecs[4:5] + vecs[5:6]).astype(BF)

        sub_blocks(i, block)
        for cp in outs(i, x2_out, h3_out, 1):
            cp.start()

    def step_two(i):
        second.share(i)
        pl.when(i > 0)(lambda: last(i - 1))
        hook(NCH + i)

    each(0, NCH, step_two)
    last(NCH - 1)
    for k in range(nbg):
        gather.finish(k)

    def end(i):
        second.drain(i)
        for cp in outs(i, x2_out, h3_out, 1):
            cp.wait()

    each(0, NCH, end)


def mid_call(cid, n, a, x0, vecs, cond, wo, wq, wk, wv, wc, bg, ahead=4):
    f, wide, nbg = a.shape[1], x0.shape[1], len(bg)
    sd = jax.ShapeDtypeStruct
    dma = pltpu.SemaphoreType.DMA
    weight = lambda: pltpu.VMEM((wide, f), BF)
    return pl.pallas_call(
        functools.partial(mid_kernel, n, f, nbg, ahead),
        out_shape=[
            sd((TP, wide), F32), sd((TP, wide), BF), sd((TP, f), BF), sd((CP, 2 * f), BF), sd((TP, f), BF), sd((TP, 128), F32),
            sd((TP, wide), F32), sd((TP, wide), BF),
        ] + [sd((n * b.shape[0], b.shape[1]), BF) for b in bg],
        in_specs=[hspec()] * 2 + [vspec()] * 2 + [hspec()] * (5 + nbg),
        out_specs=[hspec()] * 2 + [vspec()] * 4 + [hspec()] * (2 + nbg),
        scratch_shapes=[
            pltpu.VMEM((TP, f), BF), pltpu.VMEM((TP, wide), BF), pltpu.VMEM((TP, wide), F32), pltpu.VMEM((TP, wide), BF),
            weight(), weight(), weight(), weight(), weight(), dma((7,)), dma((2, 2 * NCH)),
        ] + reduce_scratch(wide, True) + (gather_sems(nbg, n) if nbg else []),
        compiler_params=pltpu.CompilerParams(collective_id=cid, has_side_effects=True, vmem_limit_bytes=60 << 20),
        name="mid",
    )(a, x0, vecs, cond, wo, wq, wk, wv, wc, *bg)


NEG = -1e30


def nn(a, b):
    return jnp.dot(a, b, preferred_element_type=F32)


def lanes(shape):
    return lax.broadcasted_iota(jnp.int32, shape, len(shape) - 1)


def head_mask(value, which):
    lane = lanes(value.shape)
    keep = (lane < HEAD) if which == 0 else (lane >= HEAD)
    return jnp.where(keep, value, jnp.zeros_like(value))


def attend_step(i, q_ref, q_off, k_ref, k_off, v_ref, v_off, keys, valid, out_ref, lse_ref, heads, hook=None):
    rows = rows_of(i)
    lse = jnp.zeros((CH, 128), F32)
    for pair in range(heads // 2):
        qp = q_ref[rows, q_off + 128 * pair:q_off + 128 * (pair + 1)]
        kp = k_ref[:, k_off + 128 * pair:k_off + 128 * (pair + 1)]
        vp = v_ref[:, v_off + 128 * pair:v_off + 128 * (pair + 1)]
        mixed = []
        for which in range(2):
            s = nt(head_mask(qp, which), kp)
            s = jnp.where(lanes((1, keys)) < valid, s, NEG)
            top = jnp.max(s, axis=1, keepdims=True)
            e = jnp.exp(s - top)
            total = jnp.sum(e, axis=1, keepdims=True)
            mixed.append(nn(e.astype(BF), vp) / total)
            lse = jnp.where(lanes(lse.shape) == 2 * pair + which, top + jnp.log(total), lse)
        both = jnp.where(lanes(mixed[0].shape) < HEAD, mixed[0], mixed[1])
        out_ref[rows, 128 * pair:128 * (pair + 1)] = both.astype(BF)
        if hook is not None:
            hook(pair)
    lse_ref[rows] = lse


def attend_back(q_ref, q_off, k_ref, k_off, v_ref, v_off, keys, kblock, valid, do_ref, out_ref, lse_ref, lse_t, delta_t, dqt, emit_q, emit_kv, heads, hook=None):
    queries = q_ref.shape[0]
    lse_t[...] = lse_ref[...].T
    delta = jnp.zeros((queries, 128), F32)
    for pair in range(heads // 2):
        cols = slice(128 * pair, 128 * (pair + 1))
        prod = do_ref[:, cols].astype(F32) * out_ref[:, cols].astype(F32)
        for which in range(2):
            one = jnp.sum(head_mask(prod, which), axis=1, keepdims=True)
            delta = jnp.where(lanes(delta.shape) == 2 * pair + which, one, delta)
    delta_t[...] = delta.T
    for pair in range(heads // 2):
        qc = slice(q_off + 128 * pair, q_off + 128 * (pair + 1))
        kc = slice(k_off + 128 * pair, k_off + 128 * (pair + 1))
        vc = slice(v_off + 128 * pair, v_off + 128 * (pair + 1))
        oc = slice(128 * pair, 128 * (pair + 1))
        dqt[...] = jnp.zeros_like(dqt)

        def keys_step(j, carry):
            rows = pl.ds(pl.multiple_of(j * kblock, 16), kblock)
            kb, vb = k_ref[rows, kc], v_ref[rows, vc]
            dks, dvs = [], []
            for which in range(2):
                h = 2 * pair + which
                km = head_mask(kb, which)
                p = jnp.exp(nt(km, q_ref[:, qc]) - lse_t[h:h + 1])
                if keys != valid:
                    pos = j * kblock + lax.broadcasted_iota(jnp.int32, (kblock, 1), 0)
                    p = jnp.where(pos < valid, p, 0.0)
                dp = nt(head_mask(vb, which), do_ref[:, oc])
                ds = (p * (dp - delta_t[h:h + 1])).astype(BF)
                dvs.append(nn(p.astype(BF), do_ref[:, oc]))
                dks.append(nn(ds, q_ref[:, qc]))
                dqt[...] += nn(km.T, ds)
            low = lanes(dks[0].shape) < HEAD
            emit_kv(pair, rows, jnp.where(low, dks[0], dks[1]), jnp.where(low, dvs[0], dvs[1]))
            if hook is not None:
                hook(pair, j)
            return carry

        lax.fori_loop(0, keys // kblock, keys_step, 0)
        emit_q(pair, dqt[...].T)


def rotate_lanes(u, cos, sin_low, sin_high):
    width = u.shape[-1]
    return u * cos + pltpu.roll(u, width - ROT // 2, u.ndim - 1) * sin_low + pltpu.roll(u, ROT // 2, u.ndim - 1) * sin_high


def front_kernel(n, f, nbg, ahead, *refs):
    refs = list(refs)
    take = lambda count: [refs.pop(0) for _ in range(count)]
    lat, teach, cond, small = take(4)
    cos_ref, lo_ref, hi_ref = take(3)
    shards = take(3 + nbg)
    x_ref, h_ref, qkv_ref, a_ref, lse_ref, small_ref, teach_ref, cond_ref = take(8)
    fulls = take(3 + nbg)
    rows_sems, col_sems = take(3), take(3)
    at = Place(n)
    wide = x_ref.shape[1]
    rowg = RowGather(at, [(lat, x_ref), (small, small_ref), (cond, cond_ref), (teach, teach_ref)], *rows_sems)
    colg = ColGather(at, list(zip(shards, fulls)), ahead, *col_sems)
    at.enter(True)
    rowg.start(0)
    rowg.start(1)
    colg.begin()
    rowg.forward(0)
    rowg.forward(1)
    colg.advance(0)
    rowg.finish(0)
    rowg.finish(1)
    rowg.start(2)
    rowg.start(3)

    def norm(i, carry):
        rows = pl.ds(pl.multiple_of(i * SUB, SUB), SUB)
        h_ref[rows] = (row_stats(x_ref[rows].astype(F32), wide)[0] * small_ref[0:1] + small_ref[1:2]).astype(BF)
        return carry

    lax.fori_loop(0, TP // SUB, norm, 0)
    for k in (1, 2):
        colg.advance(k)
    rowg.forward(2)

    for part in range(3):
        colg.finish(part)
        if part > 0:
            colg.advance(part + 2)

        def project(i, carry):
            rows = pl.ds(pl.multiple_of(i * CH, 16), CH)
            cos, lo, hi = cos_ref[rows], lo_ref[rows], hi_ref[rows]
            res = nn(h_ref[rows], fulls[part][...])
            for pair in range(f // 128):
                u = res[:, pair * 128:(pair + 1) * 128]
                if part < 2:
                    u = rotate_lanes(u, cos, lo, hi).astype(BF)
                else:
                    u = u.astype(BF)
                if part == 0:
                    u = u * HEAD ** (-0.5)
                qkv_ref[rows, part * f + pair * 128:part * f + (pair + 1) * 128] = u
            return carry

        lax.fori_loop(0, TP // CH, project, 0)

    def attend(i):
        def hook(pair):
            for k in range(5, 3 + nbg):
                pl.when(i * 3 + pair == (k - 5) * 15 // (nbg - 2))(lambda: colg.advance(k))

        attend_step(i, qkv_ref, 0, qkv_ref, f, qkv_ref, 2 * f, TP, LEN, a_ref, lse_ref, f // HEAD, hook)

    each(0, NCH, attend)
    rowg.forward(3)
    for k in range(3, 3 + nbg):
        colg.finish(k)
    rowg.finish(2)
    rowg.finish(3)


def front_call(cid, n, lat, teach, cond, small, tables, shards, ahead=4):
    f, nbg = shards[0].shape[1], len(shards) - 3
    wide = 4 * f
    sd = jax.ShapeDtypeStruct
    fulls = [sd((n * s.shape[0], s.shape[1]), BF) for s in shards]
    return pl.pallas_call(
        functools.partial(front_kernel, n, f, nbg, ahead),
        out_shape=[
            sd((TP, wide), BF), sd((TP, wide), BF), sd((TP, 3 * f), BF), sd((TP, f), BF), sd((TP, 128), F32),
            sd((8, wide), F32), sd((TP, wide), BF), sd((CP, wide), BF),
        ] + fulls,
        in_specs=[hspec()] * 4 + [vspec()] * 3 + [hspec()] * len(shards),
        out_specs=[vspec()] * 6 + [hspec()] * 2 + [vspec()] * 3 + [hspec()] * nbg,
        scratch_shapes=[pltpu.SemaphoreType.DMA((4, 3)), pltpu.SemaphoreType.DMA((4, 3)), pltpu.SemaphoreType.DMA((4,))] + gather_sems(len(shards), n),
        compiler_params=pltpu.CompilerParams(collective_id=cid, has_side_effects=True, vmem_limit_bytes=60 << 20),
        name="front",
    )(lat, teach, cond, small, *tables, *shards)


def mlp_kernel(n, f, nbg, *refs):
    refs = list(refs)
    take = lambda count: [refs.pop(0) for _ in range(count)]
    parts = 4
    h_hbm, x_hbm, t_hbm = take(3)
    gates, ups = take(parts), take(parts)
    downs = take(parts - nbg)
    bg_in = take(nbg)
    res_out, y_out, sq_ref, dg_out, du_out, gw_out = take(6)
    (h, wg, wu, wd, hid, sg, tt, dm, acc, send_a, recv_a, p1, p2, xbuf, tbuf, rbuf, ybuf, stage) = take(18)
    (wsem, hsem, xsem, tsem, rsem, ysem, dsem, gsem, s_a, r_a, s_b, r_b, s_c, r_c, s_d, r_d) = take(16)
    at = Place(n)
    wide = h.shape[1]
    half = wide // 2
    c, o, sib, par = at.c, at.o, at.sib, at.par
    col = lambda k: slice(k * f, (k + 1) * f)
    gather = ColGather(at, [(b, wd.at[:, col(parts - nbg + k)]) for k, b in enumerate(bg_in)], nbg, *take(3)) if nbg else None

    hcp = pltpu.make_async_copy(h_hbm, h, hsem.at[0])
    hcp.start()
    loads = []
    for k in range(parts):
        loads.append(pltpu.make_async_copy(gates[k], wg.at[:, col(k)], wsem.at[k]))
        loads.append(pltpu.make_async_copy(ups[k], wu.at[:, col(k)], wsem.at[parts + k]))
    late = [pltpu.make_async_copy(d, wd.at[:, col(k)], wsem.at[2 * parts + k]) for k, d in enumerate(downs)]
    for cp in loads + late:
        cp.start()
    at.enter(nbg > 0)
    if nbg:
        gather.begin()
    hcp.wait()
    sq_ref[...] = jnp.zeros_like(sq_ref)

    def rows_of(i):
        return pl.ds(pl.multiple_of(i * CH, 16), CH)

    def slot_in(i):
        return [
            pltpu.make_async_copy(x_hbm.at[rows_of(i)], xbuf.at[lax.rem(i, 2)], xsem.at[lax.rem(i, 2)]),
            pltpu.make_async_copy(t_hbm.at[rows_of(i)], tbuf.at[lax.rem(i, 2)], tsem.at[lax.rem(i, 2)]),
        ]

    def copy_a(i):
        return remote(send_a.at[rows_of(i)], recv_a.at[rows_of(i)], s_a.at[i], r_a.at[i], sib)

    def copy_b(i):
        return remote(p1.at[c, rows_of(i)], p2.at[c, rows_of(i)], s_b.at[i], r_b.at[i], par)

    def copy_c(i, side):
        return remote(p1.at[side, rows_of(i)], p1.at[side, rows_of(i)], s_c.at[i], r_c.at[i], sib)

    def copy_d(i, side):
        return remote(p2.at[side, rows_of(i)], p2.at[side, rows_of(i)], s_d.at[i], r_d.at[i], sib)

    for k in range(parts):
        loads[2 * k].wait()
        loads[2 * k + 1].wait()

        def hidden(i, carry):
            rows = rows_of(i)
            gate = nn(h[rows], wg[:, col(k)])
            up = nn(h[rows], wu[:, col(k)])
            sig = jax.nn.sigmoid(gate)
            act = gate * sig
            hid[rows, col(k)] = (act * up).astype(BF)
            sg[rows, col(k)] = act.astype(BF)
            tt[rows, col(k)] = (up * sig * (1.0 + gate * (1.0 - sig))).astype(BF)
            return carry

        lax.fori_loop(0, NCH, hidden, 0)
    for cp in late:
        cp.wait()
    for k in range(nbg):
        gather.advance(k)
    for k in range(nbg):
        gather.finish(k)
    for i in range(2):
        for cp in slot_in(i):
            cp.start()

    w_mine = pl.ds(pl.multiple_of(c * half, 128), half)
    w_other = pl.ds(pl.multiple_of(o * half, 128), half)

    def step_b(i):
        copy_a(i).wait_recv()
        p1[c, rows_of(i)] = (acc[rows_of(i)] + recv_a[rows_of(i)].astype(F32)).astype(BF)
        copy_b(i).start()
        copy_c(i, c).start()

    def first(i, carry):
        yc = hid[rows_of(i)]
        send_a[rows_of(i)] = nt(yc, wd[w_other]).astype(BF)
        copy_a(i).start()
        acc[rows_of(i)] = nt(yc, wd[w_mine])

        @pl.when(i > 0)
        def _():
            step_b(i - 1)

        return carry

    lax.fori_loop(0, NCH, first, 0)
    step_b(NCH - 1)
    per = CH // SUB

    def outs_of(i):
        slot = lax.rem(i, 2)
        return [
            pltpu.make_async_copy(rbuf.at[slot], res_out.at[rows_of(i)], rsem.at[slot]),
            pltpu.make_async_copy(ybuf.at[slot], y_out.at[rows_of(i)], ysem.at[slot]),
        ]

    def grads_of(i):
        return [
            pltpu.make_async_copy(sg.at[rows_of(i)], du_out.at[rows_of(i)], dsem.at[2 * i]),
            pltpu.make_async_copy(tt.at[rows_of(i)], dg_out.at[rows_of(i)], dsem.at[2 * i + 1]),
        ]

    def finish(i):
        slot = lax.rem(i, 2)
        copy_c(i, o).wait_recv()
        copy_d(i, o).wait_recv()
        for cp in slot_in(i):
            cp.wait()

        @pl.when(i >= 2)
        def _():
            for cp in outs_of(i - 2):
                cp.wait()

        def block(k, carry):
            rs = pl.ds(pl.multiple_of(i * CH + k * SUB, SUB), SUB)
            ls = pl.ds(pl.multiple_of(k * SUB, SUB), SUB)
            tot = jnp.concatenate(
                [p1[0, rs].astype(F32) + p2[0, rs].astype(F32), p1[1, rs].astype(F32) + p2[1, rs].astype(F32)], axis=1
            )
            y = xbuf[slot, ls] + tot
            pos = i * CH + k * SUB + lax.broadcasted_iota(jnp.int32, (SUB, wide), 0)
            res = jnp.where(pos < LEN, y - tbuf[slot, ls].astype(F32), 0.0)
            rbuf[slot, ls] = res
            dm[rs] = res.astype(BF)
            ybuf[slot, ls] = y.astype(BF)
            sq = res * res
            sq_ref[...] += sq[:8] + sq[8:]
            return carry

        lax.fori_loop(0, per, block, 0)
        for cp in outs_of(i):
            cp.start()

        @pl.when(i < NCH - 2)
        def _():
            for cp in slot_in(i + 2):
                cp.start()

        for k in range(parts):
            dh = nn(dm[rows_of(i)], wd[:, col(k)])
            tt[rows_of(i), col(k)] = (dh * tt[rows_of(i), col(k)].astype(F32)).astype(BF)
            sg[rows_of(i), col(k)] = (dh * sg[rows_of(i), col(k)].astype(F32)).astype(BF)
        for cp in grads_of(i):
            cp.start()

    def second(i, carry):
        copy_b(i).wait_recv()
        copy_d(i, c).start()

        @pl.when(i > 0)
        def _():
            finish(i - 1)

        return carry

    lax.fori_loop(0, NCH, second, 0)
    finish(NCH - 1)

    block_rows = stage.shape[1]
    steps = wide // block_rows

    def stored(q, j):
        rows = pl.ds(pl.multiple_of(j * block_rows, 128), block_rows)
        slot = lax.rem(j, 2)
        return pltpu.make_async_copy(stage.at[slot], gw_out.at[rows, q * parts * f:(q + 1) * parts * f], gsem.at[slot])

    for q, (left, right) in enumerate(((h, tt), (h, sg), (dm, hid))):
        def grad(j, carry):
            at_cols = pl.ds(pl.multiple_of(j * block_rows, 128), block_rows)

            @pl.when(j >= 2)
            def _():
                stored(q, j - 2).wait()

            stage[lax.rem(j, 2)] = tn(left[:, at_cols], right[...]).astype(BF)
            stored(q, j).start()
            return carry

        lax.fori_loop(0, steps, grad, 0)
        stored(q, steps - 2).wait()
        stored(q, steps - 1).wait()

    def drain(i, carry):
        copy_a(i).wait_send()
        copy_b(i).wait_send()
        copy_c(i, c).wait_send()
        copy_d(i, c).wait_send()
        for cp in grads_of(i):
            cp.wait()
        return carry

    lax.fori_loop(0, NCH, drain, 0)
    for i in range(NCH - 2, NCH):
        for cp in outs_of(i):
            cp.wait()


def mlp_call(cid, n, h, x, teach, gates, ups, downs, bg):
    wide, f = h.shape[1], gates[0].shape[1]
    half, nbg = wide // 2, len(bg)
    sd = jax.ShapeDtypeStruct
    dma = pltpu.SemaphoreType.DMA
    full = lambda: pltpu.VMEM((TP, wide), BF)
    weight = lambda: pltpu.VMEM((wide, 4 * f), BF)
    scratch = [full(), weight(), weight(), weight(), full(), full(), full(), full()] + [
        pltpu.VMEM((TP, half), F32),
        pltpu.VMEM((TP, half), BF),
        pltpu.VMEM((TP, half), BF),
        pltpu.VMEM((2, TP, half), BF),
        pltpu.VMEM((2, TP, half), BF),
        pltpu.VMEM((2, CH, wide), F32),
        pltpu.VMEM((2, CH, wide), BF),
        pltpu.VMEM((2, CH, wide), F32),
        pltpu.VMEM((2, CH, wide), BF),
        pltpu.VMEM((2, 256, wide), BF),
        dma((12,)), dma((1,)), dma((2,)), dma((2,)), dma((2,)), dma((2,)), dma((2 * NCH,)), dma((2,)),
    ] + [dma((NCH,))] * 8
    if nbg:
        scratch += gather_sems(nbg, n)
    return pl.pallas_call(
        functools.partial(mlp_kernel, n, f, nbg),
        out_shape=[
            sd((TP, wide), F32), sd((TP, wide), BF), sd((8, wide), F32), sd((TP, 4 * f), BF), sd((TP, 4 * f), BF), sd((wide, 12 * f), BF),
        ],
        in_specs=[hspec()] * (3 + 8 + len(downs) + nbg),
        out_specs=[hspec(), hspec(), vspec(), hspec(), hspec(), hspec()],
        scratch_shapes=scratch,
        compiler_params=pltpu.CompilerParams(collective_id=cid, has_side_effects=True, vmem_limit_bytes=62 << 20),
        name="mlp",
    )(h, x, teach, *gates, *ups, *downs, *bg)


def norm_back(tot, x, prior, gain, wide):
    xh, inv = row_stats(x, wide)
    e = tot * gain
    m1 = jnp.sum(e, axis=1, keepdims=True) * (1.0 / wide)
    m2 = jnp.sum(e * xh, axis=1, keepdims=True) * (1.0 / wide)
    return prior + inv * (e - m1 - xh * m2), tot * xh


def fold(ref, at, value):
    ref[at] += value[:8] + value[8:]


def mid_back_kernel(n, f, npieces, ahead, slots, *refs):
    refs = list(refs)
    take = lambda count: [refs.pop(0) for _ in range(count)]
    dg_hbm, du_hbm, res_hbm, x2_hbm, x1_hbm, part_hbm, vecs, cq_ref, ckv_ref, c_ref, lse_ref, wc_hbm, wq_hbm = take(13)
    w_hbm = take(8)
    dco_out, dcq_ref, dckv_ref, g1_out, do_out, sums_ref = take(6)
    piece_out = take(2)
    ybuf, wbuf, g, low, xs, wc, wq, dkv, dc, lsem, wsem, xsem, osem = take(13)
    send_a, recv_a, acc, p1, p2, p2b = take(6)
    sems = take(16)
    bufs, rsems = take(6), take(8)
    at = Place(n)
    wide = g.shape[1]
    ffl = dg_hbm.shape[1]
    first = RowReduce(at, send_a, recv_a, acc, p1, p2, sems[:8])
    second = RowReduce(at, send_a, recv_a, acc, p1, p2b, sems[8:])
    made = [
        (part_hbm.at[:, k * f:(k + 1) * f], piece_out[k // 4].at[:, k % 4 * f:(k % 4 + 1) * f], False) for k in range(npieces)
    ]
    scatter = ColScatter(at, made, ahead, slots, bufs, rsems)
    loads = [
        pltpu.make_async_copy(dg_hbm, ybuf.at[:, :ffl], lsem.at[0]),
        pltpu.make_async_copy(du_hbm, ybuf.at[:, ffl:], lsem.at[1]),
    ] + [pltpu.make_async_copy(w_hbm[k], wbuf.at[:, k * f:(k + 1) * f], wsem.at[k]) for k in range(8)]
    rest = [
        pltpu.make_async_copy(src, dst, lsem.at[2 + k])
        for k, (src, dst) in enumerate(((res_hbm, g), (wc_hbm, wc), (wq_hbm, wq)))
    ]
    for cp in loads + rest:
        cp.start()

    def stream(src, i):
        slot = lax.rem(i, 2)
        return pltpu.make_async_copy(src.at[rows_of(i)], xs.at[slot], xsem.at[slot])

    stream(x2_hbm, 0).start()
    stream(x2_hbm, 1).start()
    at.enter(True)
    scatter.begin()
    for cp in loads:
        cp.wait()

    def project(i):
        first.partial(i, ybuf[rows_of(i)], wbuf)
        pl.when(i > 0)(lambda: first.swap(i - 1))

    each(0, NCH, project)
    first.swap(NCH - 1)
    for cp in rest:
        cp.wait()
    sums_ref[...] = jnp.zeros_like(sums_ref)
    dkv[...] = jnp.zeros_like(dkv)

    def hook(slot):
        for k in range(npieces):
            pl.when(slot == k * 2 * NCH // npieces + 1)(lambda: scatter.advance(k))

    def outs(i, which):
        lowest = (dco_out, do_out)[which]
        cps = [pltpu.make_async_copy(low.at[rows_of(i)], lowest.at[rows_of(i)], osem.at[which, i])]
        if which == 1:
            cps.append(pltpu.make_async_copy(g.at[rows_of(i)], g1_out.at[rows_of(i)], osem.at[2, i]))
        return cps

    def cross(i):
        first.ready(i)
        stream(x2_hbm, i).wait()
        slot = lax.rem(i, 2)

        def block(k, rs, ls):
            tot = first.total(rs)
            new, dx = norm_back(tot, xs[slot, ls], g[rs], vecs[4:5], wide)
            g[rs] = new
            low[rs] = new.astype(BF)
            fold(sums_ref, 0, dx)
            fold(sums_ref, 1, tot)

        sub_blocks(i, block)
        pl.when(i < NCH - 2)(lambda: stream(x2_hbm, i + 2).start())

        @pl.when(i >= NCH - 2)
        def _():
            pltpu.make_async_copy(x1_hbm.at[rows_of(i + 2 - NCH)], xs.at[slot], xsem.at[slot]).start()

        for cp in outs(i, 0):
            cp.start()
        rows = rows_of(i)
        dc[...] = nn(low[rows], wc[...]).astype(BF)
        lse_t = lse_ref[rows].T
        delta = jnp.zeros((CH, 128), F32)
        for pair in range(f // 128):
            cols = slice(128 * pair, 128 * (pair + 1))
            prod = dc[:, cols].astype(F32) * c_ref[rows, cols].astype(F32)
            for which in range(2):
                one = jnp.sum(head_mask(prod, which), axis=1, keepdims=True)
                delta = jnp.where(lanes(delta.shape) == 2 * pair + which, one, delta)
        delta_t = delta.T
        valid = lax.broadcasted_iota(jnp.int32, (CP, 1), 0) < CLEN
        for pair in range(f // 128):
            cols = slice(128 * pair, 128 * (pair + 1))
            vcols = slice(f + 128 * pair, f + 128 * (pair + 1))
            kb, vb, qc, doc = ckv_ref[:, cols], ckv_ref[:, vcols], cq_ref[rows, cols], dc[:, cols]
            dks, dvs, dqt = [], [], None
            for which in range(2):
                h = 2 * pair + which
                km = head_mask(kb, which)
                p = jnp.where(valid, jnp.exp(nt(km, qc) - lse_t[h:h + 1]), 0.0)
                dp = nt(head_mask(vb, which), doc)
                ds = (p * (dp - delta_t[h:h + 1])).astype(BF)
                dvs.append(nn(p.astype(BF), doc))
                dks.append(nn(ds, qc))
                part = nn(km.T, ds)
                dqt = part if dqt is None else dqt + part
            left = lanes(dks[0].shape) < HEAD
            dkv[:, cols] += jnp.where(left, dks[0], dks[1])
            dkv[:, vcols] += jnp.where(left, dvs[0], dvs[1])
            dcq_ref[rows, cols] = (dqt.T * HEAD ** (-0.5)).astype(BF)
        first.drain(i)
        second.partial(i, dcq_ref[rows], wq)
        pl.when(i > 0)(lambda: second.swap(i - 1))

    def step(i):
        first.share(i)
        pl.when(i > 0)(lambda: cross(i - 1))
        hook(i)

    each(0, NCH, step)
    cross(NCH - 1)
    second.swap(NCH - 1)
    dckv_ref[...] = dkv[...].astype(BF)

    def last(i):
        second.ready(i)
        slot = lax.rem(i + NCH, 2)
        cp = pltpu.make_async_copy(x1_hbm.at[rows_of(i)], xs.at[slot], xsem.at[slot])
        cp.wait()
        for cp in outs(i, 0):
            cp.wait()

        def block(k, rs, ls):
            tot = second.total(rs)
            new, dx = norm_back(tot, xs[slot, ls], g[rs], vecs[2:3], wide)
            g[rs] = new
            low[rs] = new.astype(BF)
            fold(sums_ref, 2, dx)
            fold(sums_ref, 3, tot)

        sub_blocks(i, block)

        @pl.when(i < NCH - 2)
        def _():
            pltpu.make_async_copy(x1_hbm.at[rows_of(i + 2)], xs.at[slot], xsem.at[slot]).start()

        for cp in outs(i, 1):
            cp.start()

    def step_two(i):
        second.share(i)
        pl.when(i > 0)(lambda: last(i - 1))
        hook(NCH + i)

    each(0, NCH, step_two)
    last(NCH - 1)
    scatter.complete()

    def end(i):
        second.drain(i)
        for cp in outs(i, 1):
            cp.wait()

    each(0, NCH, end)


def mid_back_call(cid, n, dg, du, res, x2, x1, part, vecs, cq, ckv, c, lse, wc, wq, ws, npieces=5, ahead=3, slots=5):
    wide, f, ffl = res.shape[1], cq.shape[1], dg.shape[1]
    size = wide // n
    sd = jax.ShapeDtypeStruct
    dma = pltpu.SemaphoreType.DMA
    bufs, sems = scatter_scratch(npieces, slots, n, f, wide)
    return pl.pallas_call(
        functools.partial(mid_back_kernel, n, f, npieces, ahead, slots),
        out_shape=[
            sd((TP, wide), BF), sd((TP, f), BF), sd((CP, 2 * f), BF), sd((TP, wide), F32), sd((TP, wide), BF), sd((4, 8, wide), F32),
            sd((size, ffl), F32), sd((size, (npieces - 4) * f), F32),
        ],
        in_specs=[hspec()] * 6 + [vspec()] * 5 + [hspec()] * 10,
        out_specs=[hspec(), vspec(), vspec(), hspec(), hspec(), vspec()] + [hspec()] * 2,
        scratch_shapes=[
            pltpu.VMEM((TP, 2 * ffl), BF), pltpu.VMEM((wide, 2 * ffl), BF), pltpu.VMEM((TP, wide), F32), pltpu.VMEM((TP, wide), BF),
            pltpu.VMEM((2, CH, wide), F32), pltpu.VMEM((wide, f), BF), pltpu.VMEM((wide, f), BF), pltpu.VMEM((CP, 2 * f), F32),
            pltpu.VMEM((CH, f), BF), dma((5,)), dma((8,)), dma((2,)), dma((3, NCH)),
        ] + reduce_scratch(wide, True) + bufs + sems,
        compiler_params=pltpu.CompilerParams(collective_id=cid, has_side_effects=True, vmem_limit_bytes=63 << 20),
        name="mid_back",
    )(dg, du, res, x2, x1, part, vecs, cq, ckv, c, lse, wc, wq, *ws)


def end_kernel(n, f, low, ahead, slots, *refs):
    refs = list(refs)
    take = lambda count: [refs.pop(0) for _ in range(count)]
    do_hbm, h1_hbm, h2_hbm, dco_hbm, x0_hbm, g1_hbm, part_hbm, vecs_hbm, sums_hbm = take(9)
    wo_hbm, wck_hbm, wcv_hbm = take(3)
    w1_hbm = take(3)
    qkv_ref, a_ref, lse_ref, cos_ref, lo_ref, hi_ref, c_ref, dcq_ref, dckv_ref, cond_ref, sq_ref = take(11)
    lat_ref, gcond_ref, vec_ref = take(3)
    up_out, down_out = take(2)
    square_out = take(8)
    (xa, xb, wt, w1, da, dqkv, lse_t, delta_t, dqt, gbuf, x0, xo, go, g1, tot, send_a, recv_a, acc, send_b, recv_b) = take(20)
    st, back, st_t, sx, cpart, crecv, vb, vr, vz, sums_own = take(10)
    lsem, wsem, s_a, r_a, s_b, r_b, s_x, r_x, s_c, r_c, s_v, r_v = take(12)
    bufs, rsems = take(6), take(8)
    at = Place(n)
    r, c, o = at.r, at.c, at.o
    wide = xa.shape[1]
    own = pl.ds(pl.multiple_of(r * f, 128), f)
    made = [(part_hbm.at[:, k * f:(k + 1) * f], up_out.at[:, (k - low) * f:(k - low + 1) * f], False) for k in range(low, 8)]
    made += [(part_hbm.at[:, k * f:(k + 1) * f], down_out.at[(k - 8) * f:(k - 7) * f], True) for k in range(8, 12)]
    flips = (True, True, False, False, False, False, False, False)
    made += [(gbuf.at[k], square_out[k], flips[k]) for k in range(8)]
    scatter = ColScatter(at, made, ahead, slots, bufs, rsems)
    load = lambda src, dst, k: pltpu.make_async_copy(src, dst, lsem.at[k])
    do_cp, h2_cp, wo_cp = load(do_hbm, xa, 0), load(h2_hbm, xb, 1), load(wo_hbm, wt, 2)
    others = [
        load(x0_hbm, x0, 3), load(x0_hbm.at[:, own], xo, 4), load(vecs_hbm.at[:, own], go, 5), load(g1_hbm.at[:, own], g1, 6),
        load(sums_hbm.at[:, :, own], sums_own, 7),
    ] + [pltpu.make_async_copy(w1_hbm[k], w1.at[:, k * f:(k + 1) * f], wsem.at[k]) for k in range(3)]
    for cp in [do_cp, wo_cp, h2_cp] + others:
        cp.start()
    at.enter(True, diagonal=True)
    scatter.begin()

    def weight_grad(slot, left, right):
        def one(j):
            cols = pl.ds(pl.multiple_of(j * 512, 128), 512)
            gbuf[slot, cols] = tn(left[:, cols], right).astype(BF)

        each(0, wide // 512, one)

    do_cp.wait()
    wo_cp.wait()
    each(0, NCH, lambda i: da.__setitem__(rows_of(i), nn(xa[rows_of(i)], wt[...]).astype(BF)))
    weight_grad(0, xa, a_ref[...])
    dco_cp, wck_cp = load(dco_hbm, xa, 0), load(wck_hbm, wt, 2)
    dco_cp.start()
    wck_cp.start()

    def emit_q(pair, dq):
        dqkv[:, 128 * pair:128 * (pair + 1)] = rotate_lanes(dq * HEAD ** (-0.5), cos_ref[...], -lo_ref[...], -hi_ref[...]).astype(BF)

    def emit_kv(pair, rows, dk, dv):
        dqkv[rows, f + 128 * pair:f + 128 * (pair + 1)] = rotate_lanes(dk, cos_ref[rows], -lo_ref[rows], -hi_ref[rows]).astype(BF)
        dqkv[rows, 2 * f + 128 * pair:2 * f + 128 * (pair + 1)] = dv.astype(BF)

    def hook(pair, j):
        pl.when(j == 4)(lambda: scatter.advance(pair))

    attend_back(qkv_ref, 0, qkv_ref, f, qkv_ref, 2 * f, TP, CH, LEN, da, a_ref, lse_ref, lse_t, delta_t, dqt, emit_q, emit_kv, f // HEAD, hook)
    step = f // 128

    dco_cp.wait()
    h2_cp.wait()
    weight_grad(1, xa, c_ref[...])
    weight_grad(2, xb, dcq_ref[...])
    h1_cp = load(h1_hbm, xb, 1)
    h1_cp.start()
    wck_cp.wait()
    dck, dcv = dckv_ref[:, :f], dckv_ref[:, f:]
    for j in range(4):
        cpart[j] = nt(dck, wt[j * f:(j + 1) * f])
    wcv_cp = load(wcv_hbm, wt, 2)
    wcv_cp.start()
    weight_grad(3, cond_ref, dck)
    weight_grad(4, cond_ref, dcv)
    scatter.advance(step)
    wcv_cp.wait()
    for j in range(4):
        crecv[j] = (cpart[j] + nt(dcv, wt[j * f:(j + 1) * f])).astype(BF)
    peers = (at.sib, at.par, at.diag)
    cond_cps = [
        remote(crecv.at[peers[k][0]], crecv.at[4 + k], s_c.at[k], r_c.at[k], peers[k]) for k in range(3)
    ]
    for cp in cond_cps:
        cp.start()
    h1_cp.wait()
    for k in range(3):
        weight_grad(5 + k, xb, dqkv[:, k * f:(k + 1) * f])
    for cp in others:
        cp.wait()
    scatter.advance(step + 1)

    wblock = lambda j: w1[pl.ds(pl.multiple_of(j * f, 128), f)]

    def copy_a(i):
        return remote(send_a.at[rows_of(i)], recv_a.at[rows_of(i)], s_a.at[i], r_a.at[i], at.sib)

    def copy_b(i):
        return remote(send_b.at[rows_of(i)], recv_b.at[rows_of(i)], s_b.at[i], r_b.at[i], at.par)

    def swap(i):
        copy_a(i).wait_recv()
        both = acc[lax.rem(i, 2)] + recv_a[rows_of(i)].astype(F32)
        left, right = both[:, :f], both[:, f:]
        tot[rows_of(i)] = jnp.where(at.xi == 0, left, right)
        send_b[rows_of(i)] = jnp.where(at.xi == 0, right, left).astype(BF)
        copy_b(i).start()

    def project(i):
        y = dqkv[rows_of(i)]
        send_a[rows_of(i), :f] = nt(y, wblock(o)).astype(BF)
        send_a[rows_of(i), f:] = nt(y, wblock(2 + o)).astype(BF)
        copy_a(i).start()
        acc[lax.rem(i, 2), :, :f] = nt(y, wblock(c))
        acc[lax.rem(i, 2), :, f:] = nt(y, wblock(2 + c))
        pl.when(i > 0)(lambda: swap(i - 1))

    each(0, NCH, project)
    swap(NCH - 1)
    vr[...] = jnp.zeros_like(vr)

    def sums_of(i):
        copy_b(i).wait_recv()

        def block(k, rs, ls):
            x = x0[rs].astype(F32)
            mean = jnp.sum(x, axis=1, keepdims=True) * (1.0 / wide)
            xc = x - mean
            inv = lax.rsqrt(jnp.sum(xc * xc, axis=1, keepdims=True) * (1.0 / wide) + EPSILON)
            t = tot[rs] + recv_b[rs].astype(F32)
            tot[rs] = t
            xh = (xo[rs].astype(F32) - mean) * inv
            e = t * go[0:1]
            dx = t * xh
            lane = lanes((SUB, 128))
            first = jnp.sum(e, axis=1, keepdims=True)
            cross = jnp.sum(e * xh, axis=1, keepdims=True)
            st[rs] = jnp.where(lane == 0, first, jnp.where(lane == 1, cross, jnp.where(lane == 2, mean, inv)))
            fold(vr, 0, dx)
            fold(vr, 1, t)

        sub_blocks(i, block)

    each(0, NCH, sums_of)
    st_t[...] = st[...].T
    sx[0] = st_t[:8]
    stat_cps = [remote(sx.at[0], sx.at[1 + k], s_x.at[k], r_x.at[k], peers[k]) for k in range(3)]
    for cp in stat_cps:
        cp.start()
    total = lambda x: jnp.sum(x, axis=0, keepdims=True)
    error = jnp.sum(total(sq_ref[...]), axis=1, keepdims=True)
    vb[0:1] = total(vr[0])
    vb[1:2] = total(vr[1])
    vb[2:3] = total(sums_own[2])
    vb[3:4] = total(sums_own[3])
    vb[4:5] = total(sums_own[0])
    vb[5:6] = total(sums_own[1])
    vb[6:8] = jnp.broadcast_to(error, (2, f))
    pair_cp = remote(vb, vz.at[at.outer], s_v.at[at.outer], r_v.at[at.outer], at.ypar)
    pair_cp.start()
    scatter.advance(step + 2)
    for cp in cond_cps:
        cp.wait_recv()
    gcond_ref[...] = (
        crecv[r].astype(F32) + crecv[4].astype(F32) + crecv[5].astype(F32) + crecv[6].astype(F32)
    ).astype(BF)
    for cp in stat_cps:
        cp.wait_recv()
    st_t[:8] = sx[0] + sx[1] + sx[2] + sx[3]
    pair_cp.wait()
    vz[at.zo] = vb[...] + vz[at.outer]

    def vec_out(step):
        return remote(vz.at[at.zo], vz.at[at.zo], s_v.at[step], r_v.at[at.zo], (r, 2 * at.zpeer(step) + at.yi))

    each(1, at.outer, lambda step: vec_out(step).start())
    back[...] = st_t[...].T

    def last(i):
        def block(k, rs, ls):
            e = tot[rs] * go[0:1]
            sums, own_stats = back[rs], st[rs]
            first, cross = sums[:, 0:1] * (1.0 / wide), sums[:, 1:2] * (1.0 / wide)
            mean, inv = own_stats[:, 2:3], own_stats[:, 3:4]
            xh = (xo[rs].astype(F32) - mean) * inv
            lat_ref[rs] = (g1[rs] + inv * (e - first - xh * cross)).astype(BF)

        sub_blocks(i, block)

    each(0, NCH, last)
    for p in range(step + 3, len(made)):
        scatter.advance(p)

    def vec_in(step):
        zs = at.zpeer(at.outer - step)
        remote(vz.at[zs], vz.at[zs], s_v.at[step], r_v.at[zs], at.ypar).wait_recv()
        vb[...] += vz[zs]

    vb[...] = vz[at.zo]
    each(1, at.outer, vec_in)
    vec_ref[...] = vb[...]
    each(1, at.outer, lambda step: vec_out(step).wait_send())
    scatter.complete()
    for cp in stat_cps + cond_cps:
        cp.wait_send()

    def drain(i):
        copy_a(i).wait_send()
        copy_b(i).wait_send()

    each(0, NCH, drain)


def end_call(cid, n, do, h1, h2, dco, x0, g1, part, vecs, sums, wo, wck, wcv, w1, qkv, a, lse, tables, c, dcq, dckv, cond, sq, low=5, ahead=3, slots=5):
    wide, f = do.shape[1], a.shape[1]
    size, outer = wide // n, n // 2
    sd = jax.ShapeDtypeStruct
    dma = pltpu.SemaphoreType.DMA
    pieces = 12 - low + 8
    bufs, sems = scatter_scratch(pieces, slots, n, f, wide)
    square = lambda flip: sd((f, size) if flip else (size, f), F32)
    return pl.pallas_call(
        functools.partial(end_kernel, n, f, low, ahead, slots),
        out_shape=[sd((TP, f), BF), sd((CP, f), BF), sd((8, f), F32), sd((size, (8 - low) * f), F32), sd((4 * f, size), F32)]
        + [square(k < 2) for k in range(8)],
        in_specs=[hspec()] * 15 + [vspec()] * 11,
        out_specs=[vspec()] * 3 + [hspec()] * 10,
        scratch_shapes=[
            pltpu.VMEM((TP, wide), BF), pltpu.VMEM((TP, wide), BF), pltpu.VMEM((wide, f), BF), pltpu.VMEM((wide, 3 * f), BF),
            pltpu.VMEM((TP, f), BF), pltpu.VMEM((TP, 3 * f), BF), pltpu.VMEM((128, TP), F32), pltpu.VMEM((128, TP), F32),
            pltpu.VMEM((128, TP), F32), pltpu.VMEM((8, wide, f), BF), pltpu.VMEM((TP, wide), BF), pltpu.VMEM((TP, f), BF),
            pltpu.VMEM((8, f), F32), pltpu.VMEM((TP, f), F32), pltpu.VMEM((TP, f), F32), pltpu.VMEM((TP, 2 * f), BF),
            pltpu.VMEM((TP, 2 * f), BF), pltpu.VMEM((2, CH, 2 * f), F32), pltpu.VMEM((TP, f), BF), pltpu.VMEM((TP, f), BF),
            pltpu.VMEM((TP, 128), F32), pltpu.VMEM((TP, 128), F32), pltpu.VMEM((128, TP), F32), pltpu.VMEM((4, 8, TP), F32),
            pltpu.VMEM((4, CP, f), F32), pltpu.VMEM((7, CP, f), BF), pltpu.VMEM((8, f), F32), pltpu.VMEM((2, 8, f), F32),
            pltpu.VMEM((outer + 1, 8, f), F32), pltpu.VMEM((4, 8, f), F32),
            dma((8,)), dma((3,)), dma((NCH,)), dma((NCH,)), dma((NCH,)), dma((NCH,)), dma((3,)), dma((3,)), dma((3,)), dma((3,)),
            dma((outer + 1,)), dma((outer + 1,)),
        ] + bufs + sems,
        compiler_params=pltpu.CompilerParams(collective_id=cid, has_side_effects=True, vmem_limit_bytes=63 << 20),
        name="end",
    )(do, h1, h2, dco, x0, g1, part, vecs, sums, wo, wck, wcv, *w1, qkv, a, lse, *tables, c, dcq, dckv, cond, sq)


def rotary_lanes():
    half_size = ROT // 2
    position = jnp.arange(TP, dtype=F32)
    frequency = jnp.exp(jnp.arange(half_size, dtype=F32) * (-2.0 * math.log(10000.0) / ROT))
    angles = position[:, None] * frequency[None, :]
    cos, sin = jnp.cos(angles), jnp.sin(angles)
    one, zero = jnp.ones((TP, HEAD - ROT), F32), jnp.zeros((TP, half_size), F32)
    rest = jnp.zeros((TP, HEAD - ROT), F32)
    tile = lambda *xs: jnp.concatenate(xs + xs, axis=1)
    return tile(cos, cos, one), tile(-sin, zero, rest), tile(zero, sin, rest)


def pad_rows(block, rows):
    return jnp.pad(block, ((0, rows - block.shape[0]), (0, 0)))


def body(
    latents,
    conditioning,
    teacher,
    gain_attn,
    bias_attn,
    gain_cross,
    bias_cross,
    gain_mlp,
    bias_mlp,
    w_query,
    w_key,
    w_value,
    w_out,
    w_cross_query,
    w_cross_key,
    w_cross_value,
    w_cross_out,
    w_gate,
    w_up,
    w_down,
):

    F = latents.shape[1]
    wide = F * lax.axis_size("row")
    n = lax.axis_size("col")
    FFL = w_gate.shape[1]
    small = jnp.stack([gain_attn, bias_attn, gain_cross, bias_cross, gain_mlp, bias_mlp])
    pieces = lambda w: [w[:, k:k + F] for k in range(0, FFL, F)]
    gates, ups, downs = pieces(w_gate), pieces(w_up), pieces(w_down.T)
    tables = rotary_lanes()
    early = [w_query, w_key, w_value, w_out.T, w_cross_query, w_cross_key, w_cross_value, w_cross_out.T, gates[0], ups[0]]
    late = [gates[1], ups[1], gates[2], ups[2], gates[3], ups[3]] + downs
    (x0, h1, qkv, a, lse1, vecs, teacher_full, cond_full, wq, wk, wv, wo, wcq, wck, wcv, wco, *gu0) = front_call(
        0, n, pad_rows(latents, TP), pad_rows(teacher, TP), pad_rows(conditioning, CP), pad_rows(small, 8), tables, early
    )
    x1, h2, cq, ckv, c, lse2, x2, h3, *gu1 = mid_call(1, n, a, x0, vecs, cond_full, wo, wcq, wck, wcv, wco, late[:8])
    gu = gu0 + gu1
    full_gate, full_up = [gu[0], gu[2], gu[4], gu[6]], [gu[1], gu[3], gu[5], gu[7]]
    res, y_low, squares, dgate, dup, part_mlp = mlp_call(2, n, h3, x2, teacher_full, full_gate, full_up, gu[8:], late[8:])
    dco, dcq, dckv, g1, do, sums, grad_gate, grad_up_a = mid_back_call(
        3, n, dgate, dup, res, x2, x1, part_mlp, vecs, cq, ckv, c, lse2, wco, wcq, full_gate + full_up
    )
    (glat, gcond, vec, grad_up_b, grad_down, go, gco, gcq, gck, gcv, gq, gk, gv) = end_call(
        4, n, do, h1, h2, dco, x0, g1, part_mlp, vecs, sums, wo, wck, wcv, [wq, wk, wv], qkv, a, lse1, tables, c, dcq, dckv,
        cond_full, squares,
    )
    outputs = lax.dynamic_slice_in_dim(y_low, lax.axis_index("row") * F, F, axis=1)[:LEN]
    loss = vec[6, 0] / (LEN * wide * n)
    width = F // n
    vectors = lax.dynamic_slice_in_dim(vec, lax.axis_index("col") * width, width, axis=1)
    return (
        outputs, loss, glat[:LEN], gcond[:CLEN], gq, gk, gv, go, gcq, gck, gcv, gco,
        grad_gate, jnp.concatenate([grad_up_a, grad_up_b], axis=1), grad_down,
        vectors[0], vectors[1], vectors[2], vectors[3], vectors[4], vectors[5],
    )


def solution(mesh):
    in_specs = (
        P("col", "row"),
        P("col", "row"),
        P("col", "row"),
        P("row"),
        P("row"),
        P("row"),
        P("row"),
        P("row"),
        P("row"),
        P("col", "row"),
        P("col", "row"),
        P("col", "row"),
        P("row", "col"),
        P("col", "row"),
        P("col", "row"),
        P("col", "row"),
        P("row", "col"),
        P("col", "row"),
        P("col", "row"),
        P("row", "col"),
    )
    out_specs = (
        P("col", "row"),
        P(),
        P("col", "row"),
        P("col", "row"),
        P("col", "row"),
        P("col", "row"),
        P("col", "row"),
        P("row", "col"),
        P("col", "row"),
        P("col", "row"),
        P("col", "row"),
        P("row", "col"),
        P("col", "row"),
        P("col", "row"),
        P("row", "col"),
        P(("row", "col")),
        P(("row", "col")),
        P(("row", "col")),
        P(("row", "col")),
        P(("row", "col")),
        P(("row", "col")),
    )
    return jax.shard_map(body, mesh=mesh, in_specs=in_specs, out_specs=out_specs, check_vma=False)
```

time: 1120 us -> 740 us (0.66)
  waiting for transfers between devices: 477 us -> 0 us
  Pallas kernels: 405 us -> 702 us
  matrix products: 73.5 us -> 0 us
  blocking collectives: 56 us -> 0 us
  local copies, waits for them, and re-layouts: 66.6 us -> 29 us
  other arithmetic: 22.6 us -> 3.15 us
  between operations: 15.4 us -> 2.87 us
    pallas_call x10 -> x5, Pallas kernels: 405 us -> 702 us  [the longest x1 213 us: end_call(): pl.pallas_call(functools.partial(end_kernel, n, f, low, ahead, slots), ou...]
    reduce_scatter x2 -> x0, waiting for transfers between devices: 227 us -> none  [body(): lax.psum_scatter(jnp.concatenate([g.astype(BF) for g in gs], axis=1), 'co...]
    all_gather x5 -> x0, waiting for transfers between devices: 213 us -> none  [the longest x3 207 us: body(): lax.all_gather(jnp.concatenate(ws, axis=1), 'col', axis=0, tiled=True)]
    dot_general x11 -> x0, matrix products: 73.5 us -> none  [the longest x7 41.4 us: tn(): lax.dot_general(left, right, (((0,), (0,)), ((), ())), preferred_element_...]
    psum x1 -> x0, blocking collectives: 39.2 us -> none  [body(): sums, loss = lax.psum((own_cols(sums, F), loss_part), 'col')]
    unnamed x11 -> x0, waiting for transfers between devices: 38.2 us -> none
    unnamed x79 -> x58, local copies, waits for them, and re-layouts: 28.5 us -> 9.27 us
    all_gather x2 -> x0, blocking collectives: 16.7 us -> none  [gather_cols(): return lax.all_gather(block, 'row', axis=1, tiled=True)]
  transfers between devices with their start and end apart: 9 -> 0, of which waited for: 7 -> 0; matrix products, arithmetic and copies ran while one was open for 11% -> 0% of each run, Pallas kernels for 26% -> 0%
where the time goes in v2:
time: 740 us; the launch traced here: 737 us
  Pallas kernels  702 us (95%)
  local copies, waits for them, and re-layouts  29 us (4%)
    pallas_call x1, Pallas kernels, end_call(): pl.pallas_call(functools.partial(end_kernel, n, f, low, ahead, slots), ou...  213 us
    pallas_call x1, Pallas kernels, front_call(): pl.pallas_call(functools.partial(front_kernel, n, f, nbg, ahead), out_sha...  158 us
    pallas_call x1, Pallas kernels, mlp_call(): pl.pallas_call(functools.partial(mlp_kernel, n, f, nbg), out_shape=[sd((T...  113 us
    pallas_call x1, Pallas kernels, mid_back_call(): pl.pallas_call(functools.partial(mid_back_kernel, n, f, npieces, ahead, s...  110 us
    pallas_call x1, Pallas kernels, mid_call(): pl.pallas_call(functools.partial(mid_kernel, n, f, nbg, ahead), out_shape...  109 us

profile of v2, /device:TPU:0, one launch (start us, length us, event | category | flops | bytes accessed | tf_op | source)
XLA Modules:
  0.0 736.9 jit_solution(4347110091938360592)
XLA Ops:
  0.7 0.0 copy-start.3
  0.7 2.2 pad.15.refs_0_
  2.8 0.0 copy-done.3
  2.9 0.0 copy-start.20
  2.9 0.0 copy-start.21
  2.9 0.0 copy-start.22
  2.9 0.0 copy-start.23
  2.9 1.0 pad.16.refs_1_
  3.9 0.0 copy-done.16
  3.9 0.7 pad.17.refs_2_
  4.5 0.0 copy-done.18
  4.5 0.0 copy-done.19
  4.5 0.0 copy-done.20
  4.7 0.6 pad.18.refs_3_
  5.3 2.0 fusion
  7.3 2.3 concatenate.12.refs_4_.refs_18_
  9.7 1.8 concatenate.13.refs_5_.refs_19_
  11.5 1.8 concatenate.14.refs_6_.refs_20_
  13.2 0.0 copy-done.5
  13.2 1.0 fusion.4
  14.3 158.1 %front.1 = (bf16[1040,1536]{1,0:T(8,128)(2,1)}, bf16[1040,1536]{1,0:T(8,128)(2,1)}, bf16[1040,1152]{1,0:T(8,128)(2,1)}, bf16[1040,384]{1,0:T(8,128)(2,1)}, f32[1...) custom-call(bf16[1040,384]{1,0:T(8,128)(2,1)} %pad.15.refs_0_, ...), custom_call_target="tpu_custom_call" | custom-call | tf_op jit(solution)/shard_map/front/pallas_call | solution.py:780
  172.4 0.8 fusion.3
  173.2 108.9 %mid.1 = (f32[1040,1536]{1,0:T(8,128)}, bf16[1040,1536]{1,0:T(8,128)(2,1)}, bf16[1040,384]{1,0:T(8,128)(2,1)}, bf16[144,768]{1,0:T(8,128)(2,1)}, bf16[1040,384]{...) custom-call(bf16[1040,384]{1,0:T(8,128)(2,1)} %get-tuple-element.82., ...), custom_call_target="tpu_custom_call" | custom-call | tf_op jit(solution)/shard_map/mid/pallas_call | solution.py:597
  282.1 112.9 %mlp.1 = (f32[1040,1536]{1,0:T(8,128)}, bf16[1040,1536]{1,0:T(8,128)(2,1)}, f32[8,1536]{1,0:T(8,128)}, bf16[1040,1536]{1,0:T(8,128)(2,1)}, bf16[1040,1536]{1,0:T(8,128)(2,1)}, /*index=5*/bf16[1536,4608]{1,0:T(8,128)(2,1)}) custom-call(bf16[1040,1536]{1,0:T(8,128)(2,1)} %get-tuple-element.91.refs_0_, f32[1040,1536]{1,0:T(8,128)} %get-tuple-element.92.refs_1_.refs_3_, ...), custom_call_target="tpu_custom_call" | custom-call | tf_op jit(solution)/shard_map/mlp/pallas_call | solution.py:1030
  395.0 2.1 constant_dynamic-slice_fusion.1
  397.1 109.5 %mid_back.1 = (bf16[1040,1536]{1,0:T(8,128)(2,1)}, bf16[1040,384]{1,0:T(8,128)(2,1)}, bf16[144,768]{1,0:T(8,128)(2,1)}, f32[1040,1536]{1,0:T(8,128)}, bf16[1040,...) custom-call(bf16[1040,1536]{1,0:T(8,128)(2,1)} %get-tuple-element.105.refs_0_, ...), custom_call_target="tpu_custom_call" | custom-call | tf_op jit(solution)/shard_map/mid_back/pallas_call | solution.py:1234
  506.6 212.5 %end.1 = (bf16[1040,384]{1,0:T(8,128)(2,1)}, bf16[144,384]{1,0:T(8,128)(2,1)}, f32[8,384]{1,0:T(8,128)}, f32[192,1152]{1,0:T(8,128)}, f32[1536,192]{1,0:T(8,128)...) custom-call(bf16[1040,1536]{1,0:T(8,128)(2,1)} %get-tuple-element.11, ...), custom_call_target="tpu_custom_call" | custom-call | tf_op jit(solution)/shard_map/end/pallas_call | solution.py:1474
  719.2 1.2 slice.79
  721.1 2.1 slice.80
  723.2 0.7 slice.81
  723.9 0.9 copy.41
  724.7 0.0 copy-done.7
  724.7 0.9 copy.42
  725.6 1.2 pad_maximum_fusion
  726.8 0.7 copy-done
  727.5 1.5 copy.43
  728.9 0.8 constant_dynamic-slice_fusion
  729.8 0.5 slice_bitcast_fusion
  730.3 0.7 copy.51
  731.0 0.0 copy-done.14
  731.0 0.7 copy.52
  731.7 0.7 copy.53
  732.5 0.7 copy.54
  733.2 0.0 copy-done.11
  733.2 0.7 copy.55
  733.9 0.0 copy-done.10
  733.9 0.7 copy.56
  734.6 1.0 copy.57
  (43 shorter events, 0.2 us)
Async XLA Ops:
  0.7 2.2 copy-start.3
  2.8 1.0 copy-start.16
  2.8 1.7 copy-start.18
  2.8 1.7 copy-start.19
  2.9 1.7 copy-start.20
  2.9 1.7 copy-start.21
  2.9 1.7 copy-start.22
  2.9 1.7 copy-start.23
  11.5 1.8 copy-start.5
  11.5 1.8 copy-start.6
  14.3 158.1 %copy-start.4 = (bf16[1536,192]{0,1:T(8,128)(2,1)S(1)}, bf16[1536,192]{0,1:T(8,128)(2,1)}, u32[]{:S(2)}) copy-start(bf16[1536,192]{0,1:T(8,128)(2,1)} %param.39) | copy-start | bytes 1769476
  719.1 4.1 copy-start.17
  719.2 4.7 copy-start.8
  721.1 3.7 copy-start.7
  723.2 2.4 copy-start.2
  723.2 2.4 copy-start.9
  725.6 1.8 copy-start
  727.5 2.8 copy-start.15
  727.5 3.6 copy-start.14
  728.9 2.8 copy-start.13
  728.9 3.5 copy-start.12
  730.3 2.9 copy-start.11
  731.0 2.9 copy-start.10
  731.7 2.9 copy-start.1

commit v3 on v1

v3 whole, which is shorter than its diff:
```python
import functools
import math

import jax
import jax.numpy as jnp
import numpy as np
from jax import lax
from jax.sharding import PartitionSpec as P
from jax.experimental import pallas as pl
from jax.experimental.pallas import tpu as pltpu

BF, F32 = jnp.bfloat16, jnp.float32
MESH = pl.DeviceIdType.MESH
TP = 1040
LEN = 1025
CLEN = 130
CP = 144
HEAD = 64
ROT = 32
EPSILON = 1e-06
CH = 208
NCH = TP // CH
SUB = 16


def nt(a, b):
    return lax.dot_general(a, b, (((1,), (1,)), ((), ())), preferred_element_type=F32)


def remote(src, dst, ssem, rsem, dev):
    return pltpu.make_async_remote_copy(src_ref=src, dst_ref=dst, send_sem=ssem, recv_sem=rsem, device_id=dev, device_id_type=MESH)


def tn(left, right):
    return lax.dot_general(left, right, (((0,), (0,)), ((), ())), preferred_element_type=F32)


def row_stats(x, wide):
    xc = x - jnp.sum(x, axis=1, keepdims=True) * (1.0 / wide)
    inv = lax.rsqrt(jnp.sum(xc * xc, axis=1, keepdims=True) * (1.0 / wide) + EPSILON)
    return xc * inv, inv


def rotate_lanes(u, cos, sin_low, sin_high):
    width = u.shape[-1]
    return u * cos + pltpu.roll(u, width - ROT // 2, u.ndim - 1) * sin_low + pltpu.roll(u, ROT // 2, u.ndim - 1) * sin_high


def vspec():
    return pl.BlockSpec(memory_space=pltpu.VMEM)


def hspec():
    return pl.BlockSpec(memory_space=pl.ANY)


class Place:
    def __init__(self, n):
        self.n, self.outer = n, n // 2
        self.r, self.col = lax.axis_index("row"), lax.axis_index("col")
        self.c = lax.rem(self.r, 2)
        self.o = 1 - self.c
        self.xi = lax.div(self.r, 2)
        self.sib = (self.r + 1 - 2 * self.c, self.col)
        self.par = (self.r + 2 - 4 * self.xi, self.col)
        self.diag = (self.par[0] + 1 - 2 * self.c, self.col)
        self.zo, self.yi = lax.div(self.col, 2), lax.rem(self.col, 2)
        self.ypar = (self.r, self.col + 1 - 2 * self.yi)

    def zpeer(self, step):
        return lax.rem(self.zo + step, self.outer)

    def near(self, z):
        gap = z - self.zo
        return jnp.logical_and(gap < 3, gap > -3)

    def enter(self, with_cols, diagonal=False):
        barrier = pltpu.get_barrier_semaphore()
        pl.semaphore_signal(barrier, inc=1, device_id=self.sib, device_id_type=MESH)
        pl.semaphore_signal(barrier, inc=1, device_id=self.par, device_id_type=MESH)
        count = 2
        if diagonal:
            pl.semaphore_signal(barrier, inc=1, device_id=self.diag, device_id_type=MESH)
            count += 1
        if with_cols:
            pl.semaphore_signal(barrier, inc=1, device_id=self.ypar, device_id_type=MESH)

            def greet(step, carry):
                pl.semaphore_signal(barrier, inc=1, device_id=(self.r, 2 * self.zpeer(step) + self.yi), device_id_type=MESH)
                return carry

            lax.fori_loop(1, self.outer, greet, 0)
            count += self.outer
        pl.semaphore_wait(barrier, count)


class ColGather:
    def __init__(self, place, pieces, ahead, ssem, rsem, lsem):
        self.at, self.pieces, self.ahead, self.ssem, self.rsem, self.lsem = place, pieces, ahead, ssem, rsem, lsem
        self.line = place.outer == 4

    def rows(self, p, j):
        size = self.pieces[p][0].shape[0]
        return self.pieces[p][1].at[pl.ds(pl.multiple_of(j * size, 16), size)]

    def local(self, p):
        return pltpu.make_async_copy(self.pieces[p][0], self.rows(p, self.at.col), self.lsem.at[p])

    def send(self, p, slot, j, to, own=False):
        src = self.pieces[p][0] if own else self.rows(p, j)
        return remote(src, self.rows(p, j), self.ssem.at[p, slot], self.rsem.at[p, j], to)

    def across(self, p):
        return self.send(p, 0, self.at.col, self.at.ypar, own=True)

    def outward(self, p, step):
        at = self.at
        return self.send(p, step, at.col, (at.r, 2 * at.zpeer(step) + at.yi), own=True)

    def onward(self, p, step):
        at = self.at
        return self.send(p, at.outer - 1 + step, 2 * at.zpeer(at.outer - step) + at.yi, at.ypar)

    def steps(self, fn, source, far=False):
        at = self.at
        if far and not self.line:
            return

        def one(step):
            if not self.line:
                fn(step)
                return
            near = at.near(at.zpeer(at.outer - step) if source else at.zpeer(step))
            pl.when(jnp.logical_not(near) if far else near)(lambda: fn(step))

        each(1, at.outer, one)

    def relay(self, p, act):
        if not self.line:
            return
        at = self.at
        for mine, source, end in ((2, 0, 3), (1, 3, 0)):
            pl.when(at.zo == mine)(lambda: act(self.send(p, at.n - 1, 2 * source + at.yi, (at.r, 2 * end + at.yi))))

    def start(self, p):
        if p < len(self.pieces):
            self.local(p).start()
            self.across(p).start()
            self.steps(lambda step: self.outward(p, step).start(), False)

    def pass_on(self, p, far):
        def one(step):
            cp = self.onward(p, step)
            cp.wait_recv()
            cp.start()

        self.steps(one, True, far)

    def begin(self):
        for p in range(self.ahead):
            self.start(p)

    def advance(self, p, flush=True):
        self.pass_on(p, False)
        self.relay(p, lambda cp: cp.start())
        self.start(p + self.ahead)
        if flush and p > 0:
            self.pass_on(p - 1, True)
        if p == len(self.pieces) - 1:
            self.pass_on(p, True)

    def finish(self, p):
        at = self.at
        self.local(p).wait()
        self.across(p).wait_send()
        self.steps(lambda step: self.outward(p, step).wait_send(), False)
        each(0, at.outer, lambda z: self.send(p, 0, 2 * z + 1 - at.yi, at.ypar).wait_recv())
        self.steps(lambda step: self.onward(p, step).wait_send(), True)
        self.steps(lambda step: self.onward(p, step).wait_send(), True, far=True)
        self.relay(p, lambda cp: cp.wait_send())


def gather_sems(pieces, n):
    return [pltpu.SemaphoreType.DMA((pieces, n)), pltpu.SemaphoreType.DMA((pieces, n)), pltpu.SemaphoreType.DMA((pieces,))]


class ColScatter:
    def __init__(self, place, pieces, ahead, slots, bufs, sems):
        self.at, self.pieces, self.ahead, self.slots = place, pieces, ahead, slots
        self.ry, self.hb, self.rz, self.rl, self.ob = bufs
        self.ls, self.sy, self.ryr, self.sz, self.rzr, self.rlr, self.os, self.credit = sems
        self.line = place.outer == 4
        self.size = self.hb.shape[2]

    def rows(self, p, j):
        return self.pieces[p][0].at[pl.ds(pl.multiple_of(j * self.size, 16), self.size)]

    def across(self, p, z):
        at = self.at
        return remote(
            self.rows(p, 2 * z + 1 - at.yi), self.ry.at[p % self.slots, z], self.sy.at[p, z], self.ryr.at[p, z], at.ypar
        )

    def own(self, p, z):
        return pltpu.make_async_copy(self.rows(p, 2 * z + self.at.yi), self.hb.at[p % self.slots, z], self.ls.at[p, z])

    def outward(self, p, z):
        at, s = self.at, p % self.slots
        return remote(self.hb.at[s, z], self.rz.at[s, at.zo], self.sz.at[p, z], self.rzr.at[p, at.zo], (at.r, 2 * z + at.yi))

    def detour(self, p, z):
        at, s = self.at, p % self.slots
        via = lax.div(at.zo, 3) + 1
        return remote(self.hb.at[s, z], self.rl.at[s], self.sz.at[p, z], self.rlr.at[p], (at.r, 2 * via + at.yi))

    def merging(self, z):
        zo = self.at.zo
        return jnp.logical_or(jnp.logical_and(zo == 1, z == 3), jnp.logical_and(zo == 2, z == 0))

    def arrives(self, zs):
        return self.at.near(zs)

    def blocks(self, fn):
        each(0, self.size // 48, lambda k: fn(pl.ds(pl.multiple_of(k * 48, 16), 48)))

    def begin(self):
        for p in range(self.ahead):
            self.start(p)

    def start(self, p):
        if p >= len(self.pieces):
            return
        if p >= self.slots:
            pl.semaphore_wait(self.credit.at[p - self.slots], self.at.outer)

        def one(z):
            self.across(p, z).start()
            self.own(p, z).start()

        each(0, self.at.outer, one)

    def reduce(self, p):
        at, s = self.at, p % self.slots

        def one(step):
            z = at.zpeer(step)
            self.own(p, z).wait()
            self.across(p, z).wait_recv()

            def add(rs):
                self.hb[s, z, rs] = (self.hb[s, z, rs].astype(F32) + self.ry[s, z, rs].astype(F32)).astype(BF)

            self.blocks(add)

            @pl.when(z != at.zo)
            def _():
                if not self.line:
                    self.outward(p, z).start()
                    return
                near = at.near(z)
                pl.when(jnp.logical_not(near))(lambda: self.detour(p, z).start())
                pl.when(jnp.logical_and(near, jnp.logical_not(self.merging(z))))(lambda: self.outward(p, z).start())

        each(1, at.outer + 1, one)

    def merge(self, p):
        if not self.line:
            return
        at, s = self.at, p % self.slots
        for mine, z, origin in ((1, 3, 0), (2, 0, 3)):
            @pl.when(at.zo == mine)
            def _():
                remote(self.rl.at[s], self.rl.at[s], self.sz.at[p, z], self.rlr.at[p], at.ypar).wait_recv()

                def add(rs):
                    self.hb[s, z, rs] = (self.hb[s, z, rs].astype(F32) + self.rl[s, rs].astype(F32)).astype(BF)

                self.blocks(add)
                self.outward(p, z).start()

    def result(self, p):
        return pltpu.make_async_copy(self.ob.at[p % 2], self.pieces[p][1], self.os.at[p])

    def finish(self, p):
        at, s = self.at, p % self.slots
        if p >= 2:
            self.result(p - 2).wait()

        def first(rs):
            self.ob[p % 2, rs] = self.hb[s, at.zo, rs].astype(F32)

        self.blocks(first)

        def one(step):
            zs = at.zpeer(at.outer - step)

            def take():
                remote(self.rz.at[s, zs], self.rz.at[s, zs], self.sz.at[p, zs], self.rzr.at[p, zs], at.ypar).wait_recv()

                def add(rs):
                    self.ob[p % 2, rs] += self.rz[s, zs, rs].astype(F32)

                self.blocks(add)

            if self.line:
                pl.when(at.near(zs))(take)
            else:
                take()

        each(1, at.outer, one)
        self.result(p).start()

        def sent(z):
            self.across(p, z).wait_send()

            @pl.when(z != at.zo)
            def _():
                self.outward(p, z).wait_send()

        each(0, at.outer, sent)
        if p + self.slots < len(self.pieces):
            pl.semaphore_signal(self.credit.at[p], inc=1, device_id=at.ypar, device_id_type=MESH)
            each(
                1,
                at.outer,
                lambda step: pl.semaphore_signal(
                    self.credit.at[p], inc=1, device_id=(at.r, 2 * at.zpeer(step) + at.yi), device_id_type=MESH
                ),
            )

    def advance(self, p):
        if p < len(self.pieces):
            self.reduce(p)
        if 0 <= p - 1 < len(self.pieces):
            self.merge(p - 1)
        if 0 <= p - 2 < len(self.pieces):
            self.finish(p - 2)
        self.start(p + self.ahead)

    def complete(self):
        count = len(self.pieces)
        self.advance(count)
        self.advance(count + 1)
        for p in range(max(0, count - 2), count):
            self.result(p).wait()


def scatter_scratch(pieces, slots, n, f, rows):
    size, outer = rows // n, n // 2
    dma = pltpu.SemaphoreType.DMA
    block = lambda *lead: pltpu.VMEM(lead + (size, f), BF)
    return [
        block(slots, outer), block(slots, outer), block(slots, outer), block(slots),
        pltpu.VMEM((2, size, f), F32),
    ], [
        dma((pieces, outer)), dma((pieces, outer)), dma((pieces, outer)), dma((pieces, outer)), dma((pieces, outer)),
        dma((pieces,)), dma((pieces,)), pltpu.SemaphoreType.REGULAR((pieces,)),
    ]


class RowGather:
    def __init__(self, place, pieces, ssem, rsem, lsem):
        self.at, self.pieces, self.ssem, self.rsem, self.lsem = place, pieces, ssem, rsem, lsem

    def cols(self, p, j):
        size = self.pieces[p][0].shape[1]
        return self.pieces[p][1].at[:, pl.ds(pl.multiple_of(j * size, 128), size)]

    def copies(self, p):
        at = self.at
        src, mine = self.pieces[p][0], self.cols(p, at.r)
        theirs = self.cols(p, at.par[0])
        return (
            pltpu.make_async_copy(src, mine, self.lsem.at[p]),
            remote(src, mine, self.ssem.at[p, 0], self.rsem.at[p, 0], at.sib),
            remote(src, mine, self.ssem.at[p, 1], self.rsem.at[p, 1], at.par),
            remote(theirs, theirs, self.ssem.at[p, 2], self.rsem.at[p, 2], at.sib),
        )

    def start(self, p):
        for cp in self.copies(p)[:3]:
            cp.start()

    def forward(self, p):
        local, near, far, on = self.copies(p)
        far.wait_recv()
        on.start()

    def finish(self, p):
        local, near, far, on = self.copies(p)
        local.wait()
        near.wait_recv()
        on.wait_recv()
        near.wait_send()
        far.wait_send()
        on.wait_send()


class RowReduce:
    def __init__(self, at, send_a, recv_a, acc, p1, p2, sems, free, prior):
        self.free, self.prior = free, prior
        self.at, self.send_a, self.recv_a, self.acc, self.p1, self.p2 = at, send_a, recv_a, acc, p1, p2
        self.s_a, self.r_a, self.s_b, self.r_b, self.s_c, self.r_c, self.s_d, self.r_d = sems
        self.half = p1.shape[2]

    def copy_a(self, i):
        rows = rows_of(i)
        return remote(self.send_a.at[rows], self.recv_a.at[rows], self.s_a.at[i], self.r_a.at[i], self.at.sib)

    def copy_b(self, i):
        rows, c = rows_of(i), self.at.c
        return remote(self.p1.at[c, rows], self.p2.at[c, rows], self.s_b.at[i], self.r_b.at[i], self.at.par)

    def copy_c(self, i, side):
        rows = rows_of(i)
        return remote(self.p1.at[side, rows], self.p1.at[side, rows], self.s_c.at[i], self.r_c.at[i], self.at.sib)

    def copy_d(self, i, side):
        rows = rows_of(i)
        return remote(self.p2.at[side, rows], self.p2.at[side, rows], self.s_d.at[i], self.r_d.at[i], self.at.sib)

    def partial(self, i, terms):
        half = self.half

        def side(which):
            rows = pl.ds(pl.multiple_of(which * half, 128), half)
            return sum(nt(value, w[rows]) for value, w in terms)

        self.send_a[rows_of(i)] = side(self.at.o).astype(BF)
        self.copy_a(i).start()
        self.acc[lax.rem(i, 2)] = side(self.at.c)

    def swap(self, i):
        self.copy_a(i).wait_recv()
        self.p1[self.at.c, rows_of(i)] = (self.acc[lax.rem(i, 2)] + self.recv_a[rows_of(i)].astype(F32)).astype(BF)
        if self.prior is not None:
            pl.semaphore_wait(self.prior.free.at[i], 1)
        self.copy_b(i).start()
        self.copy_c(i, self.at.c).start()

    def share(self, i):
        self.copy_b(i).wait_recv()
        self.copy_d(i, self.at.c).start()

    def ready(self, i):
        self.copy_c(i, self.at.o).wait_recv()
        self.copy_d(i, self.at.o).wait_recv()

    def total(self, rs):
        p1, p2 = self.p1, self.p2
        return jnp.concatenate(
            [p1[0, rs].astype(F32) + p2[0, rs].astype(F32), p1[1, rs].astype(F32) + p2[1, rs].astype(F32)], axis=1
        )

    def drain(self, i):
        self.copy_a(i).wait_send()
        self.copy_b(i).wait_send()
        self.copy_c(i, self.at.c).wait_send()
        self.copy_d(i, self.at.c).wait_send()
        pl.semaphore_signal(self.free.at[i], inc=1, device_id=self.at.par, device_id_type=MESH)


def rows_of(i):
    return pl.ds(pl.multiple_of(i * CH, 16), CH)


def each(low, high, fn):
    def body(i, carry):
        fn(i)
        return carry

    lax.fori_loop(low, high, body, 0)


def sub_blocks(i, fn):
    each(0, CH // SUB, lambda k: fn(k, pl.ds(pl.multiple_of(i * CH + k * SUB, SUB), SUB), pl.ds(pl.multiple_of(k * SUB, SUB), SUB)))


NEG = -1e30


def nn(a, b):
    return jnp.dot(a, b, preferred_element_type=F32)


def lanes(shape):
    return lax.broadcasted_iota(jnp.int32, shape, len(shape) - 1)


def head_mask(value, which):
    lane = lanes(value.shape)
    keep = (lane < HEAD) if which == 0 else (lane >= HEAD)
    return jnp.where(keep, value, jnp.zeros_like(value))


def attend_step(i, q_ref, q_off, k_ref, k_off, v_ref, v_off, keys, valid, out_ref, lse_ref, heads, hook=None):
    rows = rows_of(i)
    lse = jnp.zeros((CH, 128), F32)
    for pair in range(heads // 2):
        qp = q_ref[rows, q_off + 128 * pair:q_off + 128 * (pair + 1)]
        kp = k_ref[:, k_off + 128 * pair:k_off + 128 * (pair + 1)]
        vp = v_ref[:, v_off + 128 * pair:v_off + 128 * (pair + 1)]
        mixed = []
        for which in range(2):
            s = nt(head_mask(qp, which), kp)
            s = jnp.where(lanes((1, keys)) < valid, s, NEG)
            top = jnp.max(s, axis=1, keepdims=True)
            e = jnp.exp(s - top)
            total = jnp.sum(e, axis=1, keepdims=True)
            mixed.append(nn(e.astype(BF), vp) / total)
            lse = jnp.where(lanes(lse.shape) == 2 * pair + which, top + jnp.log(total), lse)
        both = jnp.where(lanes(mixed[0].shape) < HEAD, mixed[0], mixed[1])
        out_ref[rows, 128 * pair:128 * (pair + 1)] = both.astype(BF)
        if hook is not None:
            hook(pair)
    lse_ref[rows] = lse


def attend_back(q_ref, q_off, k_ref, k_off, v_ref, v_off, keys, kblock, valid, do_ref, out_ref, lse_ref, lse_t, delta_t, dqt, emit_q, emit_kv, heads, hook=None):
    queries = q_ref.shape[0]
    lse_t[...] = lse_ref[...].T
    delta = jnp.zeros((queries, 128), F32)
    for pair in range(heads // 2):
        cols = slice(128 * pair, 128 * (pair + 1))
        prod = do_ref[:, cols].astype(F32) * out_ref[:, cols].astype(F32)
        for which in range(2):
            one = jnp.sum(head_mask(prod, which), axis=1, keepdims=True)
            delta = jnp.where(lanes(delta.shape) == 2 * pair + which, one, delta)
    delta_t[...] = delta.T
    for pair in range(heads // 2):
        qc = slice(q_off + 128 * pair, q_off + 128 * (pair + 1))
        kc = slice(k_off + 128 * pair, k_off + 128 * (pair + 1))
        vc = slice(v_off + 128 * pair, v_off + 128 * (pair + 1))
        oc = slice(128 * pair, 128 * (pair + 1))
        dqt[...] = jnp.zeros_like(dqt)

        def keys_step(j, carry):
            rows = pl.ds(pl.multiple_of(j * kblock, 16), kblock)
            kb, vb = k_ref[rows, kc], v_ref[rows, vc]
            dks, dvs = [], []
            for which in range(2):
                h = 2 * pair + which
                km = head_mask(kb, which)
                p = jnp.exp(nt(km, q_ref[:, qc]) - lse_t[h:h + 1])
                if keys != valid:
                    pos = j * kblock + lax.broadcasted_iota(jnp.int32, (kblock, 1), 0)
                    p = jnp.where(pos < valid, p, 0.0)
                dp = nt(head_mask(vb, which), do_ref[:, oc])
                ds = (p * (dp - delta_t[h:h + 1])).astype(BF)
                dvs.append(nn(p.astype(BF), do_ref[:, oc]))
                dks.append(nn(ds, q_ref[:, qc]))
                dqt[...] += nn(km.T, ds)
            low = lanes(dks[0].shape) < HEAD
            emit_kv(pair, rows, jnp.where(low, dks[0], dks[1]), jnp.where(low, dvs[0], dvs[1]))
            if hook is not None:
                hook(pair, j)
            return carry

        lax.fori_loop(0, keys // kblock, keys_step, 0)
        emit_q(pair, dqt[...].T)


def rotate_lanes(u, cos, sin_low, sin_high):
    width = u.shape[-1]
    return u * cos + pltpu.roll(u, width - ROT // 2, u.ndim - 1) * sin_low + pltpu.roll(u, ROT // 2, u.ndim - 1) * sin_high


def norm_back(tot, x, prior, gain, wide):
    xh, inv = row_stats(x, wide)
    e = tot * gain
    m1 = jnp.sum(e, axis=1, keepdims=True) * (1.0 / wide)
    m2 = jnp.sum(e * xh, axis=1, keepdims=True) * (1.0 / wide)
    return prior + inv * (e - m1 - xh * m2), tot * xh


def fold(ref, at, value):
    ref[at] += value[:8] + value[8:]


def local(src, dst, sem):
    return pltpu.make_async_copy(src, dst, sem)


def start_all(copies):
    for cp in copies:
        cp.start()


def wait_all(copies):
    for cp in copies:
        cp.wait()


def pad_into(dst, src, count):
    whole = count // 16 * 16
    dst[:whole] = src[:whole]
    left = count - whole
    rows = lax.broadcasted_iota(jnp.int32, (16, dst.shape[1]), 0)
    tile = jnp.zeros((16, dst.shape[1]), F32)
    for k in range(left):
        tile = jnp.where(rows == k, src[whole + k:whole + k + 1].astype(F32), tile)
    dst[whole:whole + 16] = tile.astype(dst.dtype)


def spread_tables(trig, cos, low, high):
    half = ROT // 2
    t = trig[...]
    lane = lanes(t.shape)
    place = lax.rem(lane, HEAD)
    first, second = place < half, jnp.logical_and(place >= half, place < ROT)
    both = lambda u: jnp.where(lane < HEAD, u, pltpu.roll(u, HEAD, 1))
    shift = lambda u: pltpu.roll(u, half, 1)
    back = lambda u: pltpu.roll(u, 128 - half, 1)
    c16, s16 = both(t), both(back(t))
    cos[...] = jnp.where(first, c16, jnp.where(second, shift(c16), 1.0))
    low[...] = jnp.where(first, -s16, 0.0)
    high[...] = jnp.where(second, shift(s16), 0.0)


def front_phase(k, gather):
    at, f, wide = k.at, k.f, k.wide
    dma = pltpu.SemaphoreType.DMA

    def run(latv, teachv, condv, latp, teachp, condp, smallv, trig, cos, low, high, x, h, qkv, a, lse, st, w, vec, ssem, lsem, sem):
        ins = [local(k.lat, latv, sem.at[0]), local(k.teach, teachv, sem.at[1]), local(k.cond, condv, sem.at[2]), local(k.trig, trig, sem.at[4])]
        start_all(ins)
        rowg = RowGather(at, [(latp, k.x0), (smallv, k.vecs), (condp, k.cond_full), (teachp, k.teach_full)], ssem, k.row_sem, lsem)
        ins[0].wait()
        pad_into(latp, latv, LEN)
        smallv[...] = jnp.zeros_like(smallv)
        for j in range(6):
            smallv[j, :] = k.small[j][...]
        at.enter(True, diagonal=True)
        rowg.start(0)
        rowg.start(1)
        gather.begin()
        wait_all(ins[1:3])
        pad_into(condp, condv, CLEN)
        pad_into(teachp, teachv, LEN)
        ins[3].wait()
        spread_tables(trig, cos, low, high)
        rowg.forward(0)
        rowg.forward(1)
        gather.advance(0)
        rowg.finish(0)
        rowg.finish(1)
        more = [local(k.x0, x, sem.at[0]), local(k.vecs, vec, sem.at[1])]
        start_all(more)
        rowg.start(2)
        rowg.start(3)
        wait_all(more)

        def norm(b):
            rows = pl.ds(pl.multiple_of(b * SUB, SUB), SUB)
            v = x[rows].astype(F32)
            mean = jnp.sum(v, axis=1, keepdims=True) * (1.0 / wide)
            xc = v - mean
            inv = lax.rsqrt(jnp.sum(xc * xc, axis=1, keepdims=True) * (1.0 / wide) + EPSILON)
            h[rows] = (xc * inv * vec[0:1] + vec[1:2]).astype(BF)
            st[rows] = jnp.where(lanes((SUB, 128)) == 2, mean, inv)

        each(0, TP // SUB, norm)
        outs = [local(h, k.h1, sem.at[2]), local(st, k.st1, sem.at[3])]
        start_all(outs)
        gather.advance(1)
        gather.advance(2)
        rowg.forward(2)
        fetch = lambda p: local(gather.pieces[p][1], w.at[p % 2], sem.at[4 + p % 2])
        gather.finish(0)
        fetch(0).start()
        for part in range(3):
            fetch(part).wait()
            if part < 2:
                if part == 1:
                    gather.pass_on(2, True)
                gather.finish(part + 1)
                fetch(part + 1).start()

            def project(i):
                rows = rows_of(i)
                c, lo, hi = cos[rows], low[rows], high[rows]
                res = nn(h[rows], w[part % 2])
                for pair in range(f // 128):
                    u = res[:, pair * 128:(pair + 1) * 128]
                    if part < 2:
                        u = rotate_lanes(u, c, lo, hi).astype(BF)
                    else:
                        u = u.astype(BF)
                    if part == 0:
                        u = u * HEAD ** (-0.5)
                    qkv[rows, part * f + pair * 128:part * f + (pair + 1) * 128] = u

            each(0, NCH, project)
        gather.advance(3, flush=False)

        def attend(i):
            def hook(pair):
                for p in range(4, k.front_pieces):
                    pl.when(i * 3 + pair == (p - 4) * 15 // (k.front_pieces - 4))(lambda: gather.advance(p))

            attend_step(i, qkv, 0, qkv, f, qkv, 2 * f, TP, LEN, a, lse, f // HEAD, hook)

        each(0, NCH, attend)
        last = [local(qkv, k.qkv, sem.at[0]), local(a, k.a, sem.at[1]), local(lse, k.lse1, sem.at[6])]
        start_all(last)
        rowg.forward(3)
        rowg.finish(2)
        rowg.finish(3)
        wait_all(outs + last)

    vm = pltpu.VMEM
    pl.run_scoped(
        run,
        latv=vm((LEN, f), BF), teachv=vm((LEN, f), BF), condv=vm((CLEN, f), BF), latp=vm((TP, f), BF), teachp=vm((TP, f), BF),
        condp=vm((CP, f), BF), smallv=vm((8, f), F32), trig=vm((TP, 128), F32), cos=vm((TP, 128), F32), low=vm((TP, 128), F32),
        high=vm((TP, 128), F32), x=vm((TP, wide), BF), h=vm((TP, wide), BF), qkv=vm((TP, 3 * f), BF), a=vm((TP, f), BF),
        lse=vm((TP, 128), F32), st=vm((TP, 128), F32), w=vm((2, wide, f), BF), vec=vm((8, wide), F32),
        ssem=dma((4, 3)), lsem=dma((4,)), sem=dma((7,)),
    )


def mid_phase(k, gather, first, second):
    at, f, wide = k.at, k.f, k.wide
    dma, vm = pltpu.SemaphoreType.DMA, pltpu.VMEM
    slots = list(range(k.front_pieces, k.mid_pieces))

    def run(a, x0, x, low, wo, wq, wk, wv, wc, cq, ckv, c, lse, cond, vec, acc, sem, osem, esem):
        first.acc, second.acc = acc, acc
        for p in range(3, 8):
            gather.finish(p)
        loads = [
            local(src, dst, sem.at[j])
            for j, (src, dst) in enumerate(
                ((k.a, a), (k.full[3], wo), (k.full[5], wk), (k.full[6], wv), (k.cond_full, cond), (k.x0, x0), (k.full[4], wq), (k.full[7], wc), (k.vecs, vec))
            )
        ]
        start_all(loads)
        wait_all(loads[:2])

        def project(i):
            first.partial(i, [(a[rows_of(i)], wo)])
            pl.when(i > 0)(lambda: first.swap(i - 1))

        each(0, NCH, project)
        first.swap(NCH - 1)
        wait_all(loads[2:])
        ckv[:, :f] = nn(cond[...], wk[...]).astype(BF)
        ckv[:, f:] = nn(cond[...], wv[...]).astype(BF)

        def outs(i, main, lowest, which):
            return [
                local(x.at[rows_of(i)], main.at[rows_of(i)], osem.at[which, 2 * i]),
                local(low.at[rows_of(i)], lowest.at[rows_of(i)], osem.at[which, 2 * i + 1]),
            ]

        def hook(slot):
            for j, p in enumerate(slots):
                pl.when(slot == j * 2 * NCH // len(slots))(lambda: gather.advance(p))

        def cross(i):
            first.ready(i)

            def block(b, rs, ls):
                v = x0[rs].astype(F32) + first.total(rs)
                x[rs] = v
                low[rs] = (row_stats(v, wide)[0] * vec[2:3] + vec[3:4]).astype(BF)

            sub_blocks(i, block)
            start_all(outs(i, k.x1, k.h2, 0))
            rows = rows_of(i)
            cq[rows] = nn(low[rows], wq[...]).astype(BF) * HEAD ** (-0.5)
            attend_step(i, cq, 0, ckv, 0, ckv, f, CP, CLEN, c, lse, f // HEAD)
            first.drain(i)
            second.partial(i, [(c[rows], wc)])
            pl.when(i > 0)(lambda: second.swap(i - 1))

        def step(i):
            first.share(i)
            pl.when(i > 0)(lambda: cross(i - 1))
            hook(i)

        each(0, NCH, step)
        cross(NCH - 1)
        second.swap(NCH - 1)
        ends = [local(cq, k.cq, esem.at[0]), local(ckv, k.ckv, esem.at[1]), local(c, k.c, esem.at[2]), local(lse, k.lse2, esem.at[3])]
        start_all(ends)

        def last(i):
            second.ready(i)
            wait_all(outs(i, k.x1, k.h2, 0))

            def block(b, rs, ls):
                v = x[rs] + second.total(rs)
                x[rs] = v
                low[rs] = (row_stats(v, wide)[0] * vec[4:5] + vec[5:6]).astype(BF)

            sub_blocks(i, block)
            start_all(outs(i, k.x2, k.h3, 1))

        def step_two(i):
            second.share(i)
            pl.when(i > 0)(lambda: last(i - 1))
            hook(NCH + i)

        each(0, NCH, step_two)
        last(NCH - 1)

        def end(i):
            second.drain(i)
            wait_all(outs(i, k.x2, k.h3, 1))

        each(0, NCH, end)
        wait_all(ends)

    weight = lambda: vm((wide, f), BF)
    pl.run_scoped(
        run,
        a=vm((TP, f), BF), x0=vm((TP, wide), BF), x=vm((TP, wide), F32), low=vm((TP, wide), BF), wo=weight(), wq=weight(), wk=weight(),
        wv=weight(), wc=weight(), cq=vm((TP, f), BF), ckv=vm((CP, 2 * f), BF), c=vm((TP, f), BF), lse=vm((TP, 128), F32),
        cond=vm((CP, wide), BF), vec=vm((8, wide), F32), acc=vm((2, CH, wide // 2), F32), sem=dma((9,)), osem=dma((2, 2 * NCH)), esem=dma((4,)),
    )


def mlp_phase(k, gather, red, nxt, h, hid, sg, tt, dm):
    at, f, wide = k.at, k.f, k.wide
    dma, vm = pltpu.SemaphoreType.DMA, pltpu.VMEM
    parts = k.parts
    col = lambda j: slice(j * f, (j + 1) * f)
    own = pl.ds(pl.multiple_of(at.r * f, 128), f)

    def run(wg, wu, wd, acc, xbuf, tbuf, sq, sem, wsem, xsem, tsem, rsem, ysem):
        red.acc, nxt.acc = acc, acc
        hcp = local(k.h3, h, sem.at[0])
        hcp.start()
        sq[...] = jnp.zeros_like(sq)

        def slot_in(i):
            s = lax.rem(i, 2)
            return [local(k.x2.at[rows_of(i)], xbuf.at[s], xsem.at[s]), local(k.teach_full.at[rows_of(i)], tbuf.at[s], tsem.at[s])]

        for i in range(2):
            start_all(slot_in(i))
        pending = list(range(k.mid_pieces, len(gather.pieces)))

        def fetch(p):
            q, j = (p - 8) % 2 if p < 16 else 2, (p - 8) // 2 if p < 16 else p - 16
            return local(gather.pieces[p][1], (wg, wu, wd)[q].at[:, col(j)], wsem.at[p - 8])

        done = [8]

        def bring(upto):
            while done[0] <= upto:
                while pending and pending[0] <= done[0] + 1:
                    gather.advance(pending.pop(0))
                gather.finish(done[0])
                fetch(done[0]).start()
                done[0] += 1

        bring(9)
        hcp.wait()
        for j in range(parts):
            if j < parts - 1:
                bring(11 + 2 * j)
            fetch(8 + 2 * j).wait()
            fetch(9 + 2 * j).wait()

            def hidden(i):
                rows = rows_of(i)
                gate = nn(h[rows], wg[:, col(j)])
                up = nn(h[rows], wu[:, col(j)])
                sig = jax.nn.sigmoid(gate)
                act = gate * sig
                hid[rows, col(j)] = (act * up).astype(BF)
                sg[rows, col(j)] = act.astype(BF)
                tt[rows, col(j)] = (up * sig * (1.0 + gate * (1.0 - sig))).astype(BF)

            each(0, NCH, hidden)
            if pending:
                gather.advance(pending.pop(0))
        bring(15 + parts)
        for j in range(parts):
            fetch(16 + j).wait()

        def project(i):
            red.partial(i, [(hid[rows_of(i)], wd)])
            pl.when(i > 0)(lambda: red.swap(i - 1))

        each(0, NCH, project)
        red.swap(NCH - 1)

        def outs_of(i):
            s = lax.rem(i, 2)
            return [local(xbuf.at[s], k.res.at[rows_of(i)], rsem.at[s]), local(tbuf.at[s, :, own], k.y.at[rows_of(i)], ysem.at[s])]

        def finish(i):
            s = lax.rem(i, 2)
            red.ready(i)

            @pl.when(i >= 1)
            def _():
                wait_all(outs_of(i - 1))
                pl.when(i < NCH - 1)(lambda: start_all(slot_in(i + 1)))

            wait_all(slot_in(i))

            def block(b, rs, ls):
                y = xbuf[s, ls] + red.total(rs)
                pos = i * CH + b * SUB + lax.broadcasted_iota(jnp.int32, (SUB, wide), 0)
                res = jnp.where(pos < LEN, y - tbuf[s, ls].astype(F32), 0.0)
                xbuf[s, ls] = res
                dm[rs] = res.astype(BF)
                tbuf[s, ls] = y.astype(BF)
                sq_ = res * res
                sq[...] += sq_[:8] + sq_[8:]

            sub_blocks(i, block)
            start_all(outs_of(i))
            rows = rows_of(i)
            for j in range(parts):
                dh = nn(dm[rows], wd[:, col(j)])
                tt[rows, col(j)] = (dh * tt[rows, col(j)].astype(F32)).astype(BF)
                sg[rows, col(j)] = (dh * sg[rows, col(j)].astype(F32)).astype(BF)
            red.drain(i)
            nxt.partial(i, [(tt[rows], wg), (sg[rows], wu)])
            pl.when(i > 0)(lambda: nxt.swap(i - 1))

        def step(i):
            red.share(i)
            pl.when(i > 0)(lambda: finish(i - 1))

        each(0, NCH, step)
        finish(NCH - 1)
        nxt.swap(NCH - 1)
        scp = local(sq, k.squares, sem.at[0])
        scp.start()
        wait_all(outs_of(NCH - 1))
        scp.wait()

    weight = lambda: vm((wide, parts * f), BF)
    pl.run_scoped(
        run,
        wg=weight(), wu=weight(), wd=weight(), acc=vm((2, CH, wide // 2), F32), xbuf=vm((2, CH, wide), F32), tbuf=vm((2, CH, wide), BF),
        sq=vm((8, wide), F32), sem=dma((1,)), wsem=dma((3 * parts,)), xsem=dma((2,)), tsem=dma((2,)),
        rsem=dma((2,)), ysem=dma((2,)),
    )


class Grads:
    def __init__(self, part, stage, sem, f):
        self.part, self.stage, self.sem, self.f = part, stage, sem, f

    def copy(self, p):
        return local(self.stage, self.part.at[:, p * self.f:(p + 1) * self.f], self.sem.at[p % 2])

    def make(self, p, left, right):
        wide = left.shape[1]

        def one(j):
            cols = pl.ds(pl.multiple_of(j * 512, 128), 512)
            self.stage[cols] = tn(left[:, cols], right()).astype(BF)

        each(0, wide // 512, one)
        self.copy(p).start()


def mid_back_phase(k, scatter, first, second, h, hid, sg, tt, dm):
    at, f, wide = k.at, k.f, k.wide
    dma, vm = pltpu.SemaphoreType.DMA, pltpu.VMEM

    def run(g, low, xs, wc, wq, dkv, dc, cq, ckv, c, lse, dcq, sums, vec, acc, stage, sem, xsem, osem, gsem):
        second.acc = acc
        grads = Grads(k.part, stage, gsem, f)
        rest = [
            local(src, dst, sem.at[j])
            for j, (src, dst) in enumerate(((k.res, g), (k.full[7], wc), (k.full[4], wq), (k.cq, cq), (k.ckv, ckv), (k.c, c), (k.lse2, lse), (k.vecs, vec)))
        ]
        start_all(rest)

        def stream(src, i, s):
            return local(src.at[rows_of(i)], xs.at[s], xsem.at[s])

        stream(k.x2, 0, 0).start()
        stream(k.x2, 1, 1).start()
        sums[...] = jnp.zeros_like(sums)
        dkv[...] = jnp.zeros_like(dkv)

        def make(p):
            q, j = p // 4, p % 4
            left, right = ((h, tt), (h, sg), (dm, hid))[q]
            grads.make(p, left, lambda: right[:, j * f:(j + 1) * f])

        for p in range(2):
            make(p)
            grads.copy(p).wait()
            scatter.start(p)
        wait_all(rest)

        def hook(slot):
            for p in range(2, 12):
                @pl.when(slot == p - 2)
                def _():
                    make(p)
                    grads.copy(p).wait()
                    if p < scatter.ahead:
                        scatter.start(p)

            for p in range(k.back_pieces):
                pl.when(slot == p * 2 * NCH // k.back_pieces + 1)(lambda: scatter.advance(p))

        def low_out(i, which):
            return local(low.at[lax.rem(i + which * NCH, 2)], (k.dco, k.do)[which].at[rows_of(i)], osem.at[which, i])

        def g_out(i):
            return local(g.at[rows_of(i)], k.g1.at[rows_of(i)], osem.at[2, i])

        valid = lambda: lax.broadcasted_iota(jnp.int32, (CP, 1), 0) < CLEN

        def cross(i):
            first.ready(i)
            s = lax.rem(i, 2)
            stream(k.x2, i, s).wait()
            pl.when(i >= 2)(lambda: low_out(i - 2, 0).wait())

            def block(b, rs, ls):
                tot = first.total(rs)
                new, dx = norm_back(tot, xs[s, ls], g[rs], vec[4:5], wide)
                g[rs] = new
                low[s, ls] = new.astype(BF)
                fold(sums, 0, dx)
                fold(sums, 1, tot)

            sub_blocks(i, block)
            pl.when(i < NCH - 2)(lambda: stream(k.x2, i + 2, s).start())
            pl.when(i >= NCH - 2)(lambda: stream(k.x1, i + 2 - NCH, s).start())
            low_out(i, 0).start()
            rows = rows_of(i)
            dc[...] = nn(low[s], wc[...]).astype(BF)
            lse_t = lse[rows].T
            delta = jnp.zeros((CH, 128), F32)
            for pair in range(f // 128):
                cols = slice(128 * pair, 128 * (pair + 1))
                prod = dc[:, cols].astype(F32) * c[rows, cols].astype(F32)
                for which in range(2):
                    one = jnp.sum(head_mask(prod, which), axis=1, keepdims=True)
                    delta = jnp.where(lanes(delta.shape) == 2 * pair + which, one, delta)
            delta_t = delta.T
            for pair in range(f // 128):
                cols = slice(128 * pair, 128 * (pair + 1))
                vcols = slice(f + 128 * pair, f + 128 * (pair + 1))
                kb, vb, qc, doc = ckv[:, cols], ckv[:, vcols], cq[rows, cols], dc[:, cols]
                dks, dvs, dqt = [], [], None
                for which in range(2):
                    hd = 2 * pair + which
                    km = head_mask(kb, which)
                    p = jnp.where(valid(), jnp.exp(nt(km, qc) - lse_t[hd:hd + 1]), 0.0)
                    dp = nt(head_mask(vb, which), doc)
                    ds = (p * (dp - delta_t[hd:hd + 1])).astype(BF)
                    dvs.append(nn(p.astype(BF), doc))
                    dks.append(nn(ds, qc))
                    part = nn(km.T, ds)
                    dqt = part if dqt is None else dqt + part
                left = lanes(dks[0].shape) < HEAD
                dkv[:, cols] += jnp.where(left, dks[0], dks[1])
                dkv[:, vcols] += jnp.where(left, dvs[0], dvs[1])
                dcq[rows, cols] = (dqt.T * HEAD ** (-0.5)).astype(BF)
            first.drain(i)
            second.partial(i, [(dcq[rows], wq)])
            pl.when(i > 0)(lambda: second.swap(i - 1))

        def step(i):
            first.share(i)
            pl.when(i > 0)(lambda: cross(i - 1))
            hook(i)

        each(0, NCH, step)
        cross(NCH - 1)
        second.swap(NCH - 1)
        ckv[...] = dkv[...].astype(BF)

        def last(i):
            second.ready(i)
            s = lax.rem(i + NCH, 2)
            stream(k.x1, i, s).wait()
            pl.when(i < 2)(lambda: low_out(NCH - 2 + i, 0).wait())
            pl.when(i >= 2)(lambda: low_out(i - 2, 1).wait())

            def block(b, rs, ls):
                tot = second.total(rs)
                new, dx = norm_back(tot, xs[s, ls], g[rs], vec[2:3], wide)
                g[rs] = new
                low[s, ls] = new.astype(BF)
                fold(sums, 2, dx)
                fold(sums, 3, tot)

            sub_blocks(i, block)
            pl.when(i < NCH - 2)(lambda: stream(k.x1, i + 2, s).start())
            low_out(i, 1).start()
            g_out(i).start()

        def step_two(i):
            second.share(i)
            pl.when(i > 0)(lambda: last(i - 1))
            hook(NCH + i)

        each(0, NCH, step_two)
        last(NCH - 1)
        ends = [local(dcq, k.dcq, sem.at[0]), local(ckv, k.dckv, sem.at[1]), local(sums, k.sums, sem.at[2])]
        start_all(ends)

        def end(i):
            second.drain(i)
            pl.when(i >= NCH - 2)(lambda: low_out(i, 1).wait())
            g_out(i).wait()

        each(0, NCH, end)
        wait_all(ends)

    pl.run_scoped(
        run,
        g=vm((TP, wide), F32), low=vm((2, CH, wide), BF), xs=vm((2, CH, wide), F32), wc=vm((wide, f), BF), wq=vm((wide, f), BF),
        dkv=vm((CP, 2 * f), F32), dc=vm((CH, f), BF), cq=vm((TP, f), BF), ckv=vm((CP, 2 * f), BF), c=vm((TP, f), BF),
        lse=vm((TP, 128), F32), dcq=vm((TP, f), BF), sums=vm((4, 8, wide), F32), vec=vm((8, wide), F32), acc=vm((2, CH, wide // 2), F32),
        stage=vm((wide, f), BF), sem=dma((8,)), xsem=dma((2,)), osem=dma((3, NCH)), gsem=dma((2,)),
    )


def end_phase(k, scatter):
    at, f, wide = k.at, k.f, k.wide
    dma, vm = pltpu.SemaphoreType.DMA, pltpu.VMEM
    r, c_, o = at.r, at.c, at.o
    own = pl.ds(pl.multiple_of(r * f, 128), f)
    send_a, recv_a = k.send_a, k.recv_a
    send_b, recv_b = k.p1.at[0, :, :f], k.p2.at[0, :, :f]

    def run(xa, xb, wt, w1, da, dqkv, lse_t, delta_t, dqt, stage, xo, go, g1, tot, acc, st, back, st_t, cpart, qkv, a, lse, trig,
            cos, low, high, c, dcq, dckv, cond, sums, sq, vr, vb, lat, gc, sem, gsem, s_c, s_x, s_v):
        grads = Grads(k.part, stage, gsem, f)
        names = {}

        def load(name, src, dst):
            names[name] = local(src, dst, sem.at[len(names)])
            names[name].start()

        load("do", k.do, xa)
        load("wo", k.full[3], wt)
        load("a", k.a, a)
        load("qkv", k.qkv, qkv)
        load("lse", k.lse1, lse)
        load("trig", k.trig, trig)
        load("h2", k.h2, xb)
        load("c", k.c, c)
        load("dcq", k.dcq, dcq)
        load("dckv", k.dckv, dckv)
        load("cond", k.cond_full, cond)
        rest = ["st", "xo", "go", "g1", "sums", "sq"]
        for name, src, dst in (
            ("st", k.st1, st), ("xo", k.x0.at[:, own], xo), ("go", k.vecs.at[:, own], go), ("g1", k.g1.at[:, own], g1),
            ("sums", k.sums.at[:, :, own], sums), ("sq", k.squares, sq),
        ):
            load(name, src, dst)
        for j in range(3):
            load(f"w{j}", k.full[j], w1.at[:, j * f:(j + 1) * f])
            rest.append(f"w{j}")

        def ready(*which):
            for name in which:
                names[name].wait()

        def make(p, left, right):
            grads.make(p, left, right)
            grads.copy(p).wait()

        ready("do", "wo", "a")

        def project_da(i):
            da[rows_of(i)] = nn(xa[rows_of(i)], wt[...]).astype(BF)

        each(0, NCH, project_da)
        make(12, xa, lambda: a[...])
        again = local(k.dco, xa, sem.at[0])
        again.start()
        wck_cp = local(k.full[5], wt, sem.at[1])
        wck_cp.start()
        ready("qkv", "lse", "trig")
        spread_tables(trig, cos, low, high)

        def emit_q(pair, dq):
            dqkv[:, 128 * pair:128 * (pair + 1)] = rotate_lanes(dq * HEAD ** (-0.5), cos[...], -low[...], -high[...]).astype(BF)

        def emit_kv(pair, rows, dk, dv):
            dqkv[rows, f + 128 * pair:f + 128 * (pair + 1)] = rotate_lanes(dk, cos[rows], -low[rows], -high[rows]).astype(BF)
            dqkv[rows, 2 * f + 128 * pair:2 * f + 128 * (pair + 1)] = dv.astype(BF)

        pairs = f // 128
        nxt = k.back_pieces

        def hook(pair, j):
            pl.when(j == 3)(lambda: scatter.advance(nxt + pair))

        attend_back(qkv, 0, qkv, f, qkv, 2 * f, TP, CH, LEN, da, a, lse, lse_t, delta_t, dqt, emit_q, emit_kv, f // HEAD, hook)
        nxt = nxt + pairs

        ready("h2", "c", "dcq", "dckv", "cond")
        again.wait()
        make(13, xa, lambda: c[...])
        make(14, xb, lambda: dcq[...])
        h1_cp = local(k.h1, xb, sem.at[0])
        h1_cp.start()
        make(15, cond, lambda: dckv[:, :f])
        make(16, cond, lambda: dckv[:, f:])
        scatter.advance(nxt)
        wck_cp.wait()
        for j in range(4):
            cpart[j] = nt(dckv[:, :f], wt[j * f:(j + 1) * f])
        wcv_cp = local(k.full[6], wt, sem.at[1])
        wcv_cp.start()
        h1_cp.wait()
        for j in range(3):
            make(17 + j, xb, lambda: dqkv[:, j * f:(j + 1) * f])
        scatter.advance(nxt + 1)
        wcv_cp.wait()
        crecv = k.crecv
        for j in range(4):
            crecv[j] = (cpart[j] + nt(dckv[:, f:], wt[j * f:(j + 1) * f])).astype(BF)
        peers = (at.sib, at.par, at.diag)
        cond_cps = [remote(crecv.at[peers[j][0]], crecv.at[4 + j], s_c.at[j], k.r_c.at[j], peers[j]) for j in range(3)]
        start_all(cond_cps)
        ready(*rest)

        wblock = lambda j: w1[pl.ds(pl.multiple_of(j * f, 128), f)]

        def copy_a(i):
            return remote(send_a.at[rows_of(i)], recv_a.at[rows_of(i)], k.e_sa.at[i], k.e_ra.at[i], at.sib)

        def copy_b(i):
            return remote(send_b.at[rows_of(i)], recv_b.at[rows_of(i)], k.e_sb.at[i], k.e_rb.at[i], at.par)

        def swap(i):
            copy_a(i).wait_recv()
            both = acc[lax.rem(i, 2)] + recv_a[rows_of(i)].astype(F32)
            left, right = both[:, :f], both[:, f:]
            tot[rows_of(i)] = jnp.where(at.xi == 0, left, right)
            send_b[rows_of(i)] = jnp.where(at.xi == 0, right, left).astype(BF)
            pl.semaphore_wait(k.last_sum.free.at[i], 1)
            copy_b(i).start()

        def project(i):
            y = dqkv[rows_of(i)]
            send_a[rows_of(i), :f] = nt(y, wblock(o)).astype(BF)
            send_a[rows_of(i), f:] = nt(y, wblock(2 + o)).astype(BF)
            copy_a(i).start()
            acc[lax.rem(i, 2), :, :f] = nt(y, wblock(c_))
            acc[lax.rem(i, 2), :, f:] = nt(y, wblock(2 + c_))
            pl.when(i > 0)(lambda: swap(i - 1))

        each(0, NCH, project)
        swap(NCH - 1)
        vr[...] = jnp.zeros_like(vr)
        scatter.advance(nxt + 2)

        def sums_of(i):
            copy_b(i).wait_recv()

            def block(b, rs, ls):
                t = tot[rs] + recv_b[rs].astype(F32)
                tot[rs] = t
                own_st = st[rs]
                mean, inv = own_st[:, 2:3], own_st[:, 3:4]
                xh = (xo[rs].astype(F32) - mean) * inv
                e = t * go[0:1]
                lane = lanes((SUB, 128))
                first = jnp.sum(e, axis=1, keepdims=True)
                cross = jnp.sum(e * xh, axis=1, keepdims=True)
                back[rs] = jnp.where(lane == 0, first, cross)
                fold(vr, 0, t * xh)
                fold(vr, 1, t)

            sub_blocks(i, block)

        each(0, NCH, sums_of)
        sx = k.sx
        st_t[...] = back[...].T
        sx[0] = st_t[:8]
        stat_cps = [remote(sx.at[0], sx.at[1 + j], s_x.at[j], k.r_x.at[j], peers[j]) for j in range(3)]
        start_all(stat_cps)
        total = lambda x: jnp.sum(x, axis=0, keepdims=True)
        error = jnp.sum(total(sq[...]), axis=1, keepdims=True)
        vb[0:1] = total(vr[0])
        vb[1:2] = total(vr[1])
        vb[2:3] = total(sums[2])
        vb[3:4] = total(sums[3])
        vb[4:5] = total(sums[0])
        vb[5:6] = total(sums[1])
        vb[6:8] = jnp.broadcast_to(error, (2, f))
        vz = k.vz
        pair_cp = remote(vb, vz.at[at.outer], s_v.at[at.outer], k.r_v.at[at.outer], at.ypar)
        pair_cp.start()
        scatter.advance(nxt + 3)
        for cp in cond_cps:
            cp.wait_recv()
        gc[...] = (crecv[r].astype(F32) + crecv[4].astype(F32) + crecv[5].astype(F32) + crecv[6].astype(F32)).astype(BF)
        for cp in stat_cps:
            cp.wait_recv()
        st_t[:8] = sx[0] + sx[1] + sx[2] + sx[3]
        back[...] = st_t[...].T
        pair_cp.wait()
        vz[at.zo] = vb[...] + vz[at.outer]

        def vec_out(step):
            return remote(vz.at[at.zo], vz.at[at.zo], s_v.at[step], k.r_v.at[at.zo], (r, 2 * at.zpeer(step) + at.yi))

        each(1, at.outer, lambda step: vec_out(step).start())

        def last(i):
            def block(b, rs, ls):
                e = tot[rs] * go[0:1]
                row_sums, own_st = back[rs], st[rs]
                first, cross = row_sums[:, 0:1] * (1.0 / wide), row_sums[:, 1:2] * (1.0 / wide)
                mean, inv = own_st[:, 2:3], own_st[:, 3:4]
                xh = (xo[rs].astype(F32) - mean) * inv
                lat[rs] = (g1[rs] + inv * (e - first - xh * cross)).astype(BF)

            sub_blocks(i, block)

        each(0, NCH, last)
        outs = [local(lat, k.glat, sem.at[0]), local(gc, k.gcond, sem.at[1])]
        start_all(outs)
        for p in range(nxt + 4, len(scatter.pieces)):
            scatter.advance(p)
        vb[...] = vz[at.zo]

        def vec_in(step):
            zs = at.zpeer(at.outer - step)
            remote(vz.at[zs], vz.at[zs], s_v.at[step], k.r_v.at[zs], at.ypar).wait_recv()
            vb[...] += vz[zs]

        each(1, at.outer, vec_in)
        vec_cp = local(vb, k.vec, sem.at[2])
        vec_cp.start()
        each(1, at.outer, lambda step: vec_out(step).wait_send())
        scatter.complete()
        for cp in stat_cps + cond_cps:
            cp.wait_send()

        def drain(i):
            copy_a(i).wait_send()
            copy_b(i).wait_send()

        each(0, NCH, drain)
        wait_all(outs + [vec_cp])

    tab = lambda: vm((TP, 128), F32)
    flip = lambda: vm((128, TP), F32)
    pl.run_scoped(
        run,
        xa=vm((TP, wide), BF), xb=vm((TP, wide), BF), wt=vm((wide, f), BF), w1=vm((wide, 3 * f), BF), da=vm((TP, f), BF),
        dqkv=vm((TP, 3 * f), BF), lse_t=flip(), delta_t=flip(), dqt=flip(), stage=vm((wide, f), BF), xo=vm((TP, f), BF),
        go=vm((8, f), F32), g1=vm((TP, f), F32), tot=vm((TP, f), F32), acc=vm((2, CH, 2 * f), F32), st=tab(), back=tab(), st_t=flip(),
        cpart=vm((4, CP, f), F32), qkv=vm((TP, 3 * f), BF), a=vm((TP, f), BF), lse=tab(), trig=tab(), cos=tab(), low=tab(), high=tab(),
        c=vm((TP, f), BF), dcq=vm((TP, f), BF), dckv=vm((CP, 2 * f), BF), cond=vm((CP, wide), BF), sums=vm((4, 8, f), F32),
        sq=vm((8, wide), F32), vr=vm((2, 8, f), F32), vb=vm((8, f), F32), lat=vm((TP, f), BF), gc=vm((CP, f), BF),
        sem=dma((24,)), gsem=dma((2,)), s_c=dma((3,)), s_x=dma((3,)), s_v=dma((k.outer + 1,)),
    )


class Names:
    pass


def layer_kernel(n, f, pieces, front_pieces, mid_pieces, back_pieces, ahead, s_ahead, slots, *refs):
    refs = list(refs)
    take = lambda count: [refs.pop(0) for _ in range(count)]
    k = Names()
    k.at, k.f, k.wide, k.outer = Place(n), f, 4 * f, n // 2
    k.front_pieces, k.mid_pieces, k.back_pieces = front_pieces, mid_pieces, back_pieces
    k.lat, k.teach, k.cond, k.trig = take(4)
    k.small = take(6)
    shards = take(11)
    k.y, k.glat, k.gcond, k.vec = take(4)
    gate_out, up_out, down_out = take(3)
    square_out = take(8)
    k.full = take(8)
    mlp_full = take(3)
    k.x0, k.vecs, k.cond_full, k.teach_full, k.h1, k.st1, k.qkv, k.a, k.lse1 = take(9)
    k.x1, k.h2, k.cq, k.ckv, k.c, k.lse2, k.x2, k.h3 = take(8)
    k.res, k.squares, k.g1, k.dco, k.do, k.dcq, k.dckv, k.sums, k.part = take(9)
    k.send_a, k.recv_a, k.p1, k.p2, k.sx, k.crecv, k.vz = take(7)
    sems = [take(8) for _ in range(5)]
    free = take(5)
    k.e_sa, k.e_ra, k.e_sb, k.e_rb, k.row_sem, k.r_c, k.r_x, k.r_v = take(8)
    gather_sem = take(3)
    bufs, scatter_sem = take(5), take(8)
    k.parts = shards[8].shape[1] // f
    col = lambda j: slice(j * f, (j + 1) * f)
    made = [(shards[j], k.full[j]) for j in range(8)]
    for j in range(k.parts):
        for q in range(2):
            made.append((shards[8 + q].at[:, col(j)], mlp_full[q].at[:, col(j)]))
    made += [(shards[10].at[:, col(j)], mlp_full[2].at[:, col(j)]) for j in range(k.parts)]
    gather = ColGather(k.at, made, ahead, *gather_sem)
    sums = []
    for q, out in enumerate((gate_out, up_out, down_out)):
        sums += [(k.part.at[:, col(q * k.parts + j)], out.at[:, col(j)]) for j in range(k.parts)]
    sums += [(k.part.at[:, col(3 * k.parts + j)], square_out[j]) for j in range(8)]
    scatter = ColScatter(k.at, sums, s_ahead, slots, bufs, scatter_sem)
    red = [None]
    for j in range(5):
        red.append(RowReduce(k.at, k.send_a, k.recv_a, None, k.p1, k.p2, sems[j], free[j], red[j]))
    red = red[1:]
    k.last_sum = red[4]
    front_phase(k, gather)
    mid_phase(k, gather, red[0], red[1])
    full = pltpu.VMEM((TP, k.wide), BF)

    def back(h, hid, sg, tt, dm):
        mlp_phase(k, gather, red[2], red[3], h, hid, sg, tt, dm)
        mid_back_phase(k, scatter, red[3], red[4], h, hid, sg, tt, dm)

    pl.run_scoped(back, h=full, hid=full, sg=full, tt=full, dm=full)
    end_phase(k, scatter)


def layer_call(n, lat, teach, cond, trig, small, shards, front_pieces=9, mid_pieces=15, back_pieces=5, ahead=4, s_ahead=2, slots=4):
    f = lat.shape[1]
    wide, size, outer = 4 * f, shards[0].shape[0], n // 2
    ffl = shards[8].shape[1]
    sd = jax.ShapeDtypeStruct
    dma = pltpu.SemaphoreType.DMA
    vm = pltpu.VMEM
    half = wide // 2
    results = [sd((TP, f), BF), sd((TP, f), BF), sd((CP, f), BF), sd((8, f), F32)]
    results += [sd((size, ffl), F32)] * 3 + [sd((size, f), F32)] * 8
    between = [sd((wide, f), BF)] * 8 + [sd((wide, ffl), BF)] * 3
    rows, rows32 = sd((TP, wide), BF), sd((TP, wide), F32)
    between += [rows, sd((8, wide), F32), sd((CP, wide), BF), rows, rows, sd((TP, 128), F32), sd((TP, 3 * f), BF), sd((TP, f), BF), sd((TP, 128), F32)]
    between += [rows32, rows, sd((TP, f), BF), sd((CP, 2 * f), BF), sd((TP, f), BF), sd((TP, 128), F32), rows32, rows]
    between += [rows32, sd((8, wide), F32), rows32, rows, rows, sd((TP, f), BF), sd((CP, 2 * f), BF), sd((4, 8, wide), F32), sd((wide, 3 * ffl + 8 * f), BF)]
    pieces = 8 + 3 * ffl // f
    scratch = [
        vm((TP, half), BF), vm((TP, half), BF), vm((2, TP, half), BF), vm((2, TP, half), BF),
        vm((4, 8, TP), F32), vm((7, CP, f), BF), vm((outer + 1, 8, f), F32),
    ] + [dma((NCH,))] * 40 + [pltpu.SemaphoreType.REGULAR((NCH,))] * 5 + [dma((NCH,))] * 4 + [dma((4, 3)), dma((3,)), dma((3,)), dma((outer + 1,))]
    bufs, sems = scatter_scratch(pieces, slots, n, f, wide)
    scratch += gather_sems(pieces, n) + bufs + sems
    out = pl.pallas_call(
        functools.partial(layer_kernel, n, f, pieces, front_pieces, mid_pieces, back_pieces, ahead, s_ahead, slots),
        out_shape=results + between,
        in_specs=[hspec()] * 4 + [vspec()] * 6 + [hspec()] * 11,
        out_specs=[hspec()] * (len(results) + len(between)),
        scratch_shapes=scratch,
        compiler_params=pltpu.CompilerParams(collective_id=0, has_side_effects=True, vmem_limit_bytes=66_900_000),
        name="layer",
    )(lat, teach, cond, trig, *small, *shards)
    return out[:len(results)]


def emit_kernel(n, scale, *refs):
    refs = list(refs)
    take = lambda count: [refs.pop(0) for _ in range(count)]
    moved, grads = take(4), take(11)
    y_out, lat_out, cond_out, vec_out = take(4)
    grad_outs = take(11)
    y, lat, cond, vec, sem, vsem = take(6)
    held = take(11)
    cps = [local(src, dst, sem.at[j]) for j, (src, dst) in enumerate(zip(grads, held))]
    out_cps = [local(src, dst, sem.at[j]) for j, (src, dst) in enumerate(zip(held, grad_outs))]
    ins = [local(src, dst, vsem.at[j]) for j, (src, dst) in enumerate(zip(moved, (y, lat, cond, vec)))]
    start_all(cps + ins)
    for cp, out in zip(cps, out_cps):
        cp.wait()
        out.start()
    wait_all(ins)
    y_out[...] = y[:y_out.shape[0]]
    lat_out[...] = lat[:lat_out.shape[0]]
    cond_out[...] = cond[:cond_out.shape[0]]
    width = vec_out.shape[1]
    v = vec[...]
    rows = lax.broadcasted_iota(jnp.int32, v.shape, 0)
    turned = pltpu.roll(v, lax.rem((n - lax.axis_index("col")) * width, v.shape[1]), 1)
    vec_out[...] = jnp.where(rows == 6, v * scale, turned)[:, :width]
    wait_all(out_cps)


def emit_call(n, scale, y, lat, cond, vec, grads):
    f = y.shape[1]
    sd = jax.ShapeDtypeStruct
    return pl.pallas_call(
        functools.partial(emit_kernel, n, scale),
        out_shape=[sd((LEN, f), BF), sd((LEN, f), BF), sd((CLEN, f), BF), sd((8, f // n), F32)] + [sd(g.shape, F32) for g in grads],
        in_specs=[hspec()] * 15,
        out_specs=[vspec()] * 4 + [hspec()] * 11,
        scratch_shapes=[
            pltpu.VMEM((TP, f), BF), pltpu.VMEM((TP, f), BF), pltpu.VMEM((CP, f), BF), pltpu.VMEM((8, f), F32),
            pltpu.SemaphoreType.DMA((11,)), pltpu.SemaphoreType.DMA((4,)),
        ] + [pltpu.VMEM(g.shape, F32) for g in grads],
        compiler_params=pltpu.CompilerParams(vmem_limit_bytes=62 << 20),
        name="emit",
    )(y, lat, cond, vec, *grads)


def trig_table():
    half_size = ROT // 2
    rates = np.exp(np.arange(half_size) * (-2.0 * math.log(10000.0) / ROT))
    angles = np.arange(TP)[:, None] * rates[None, :]
    table = np.zeros((TP, 128), np.float32)
    table[:, :half_size], table[:, half_size:ROT] = np.cos(angles), np.sin(angles)
    return jnp.asarray(table)


def body(
    latents,
    conditioning,
    teacher,
    gain_attn,
    bias_attn,
    gain_cross,
    bias_cross,
    gain_mlp,
    bias_mlp,
    w_query,
    w_key,
    w_value,
    w_out,
    w_cross_query,
    w_cross_key,
    w_cross_value,
    w_cross_out,
    w_gate,
    w_up,
    w_down,
):

    F = latents.shape[1]
    wide = F * lax.axis_size("row")
    n = lax.axis_size("col")
    y, glat, gcond, vec, *grads = layer_call(
        n, latents, teacher, conditioning, trig_table(), [gain_attn, bias_attn, gain_cross, bias_cross, gain_mlp, bias_mlp],
        [w_query, w_key, w_value, w_out.T, w_cross_query, w_cross_key, w_cross_value, w_cross_out.T, w_gate, w_up, w_down.T],
    )
    outputs, glat, gcond, vec, ggate, gup, gdown, go, gco, gcq, gck, gcv, gq, gk, gv = emit_call(
        n, 1.0 / (LEN * wide * n), y, glat, gcond, vec, grads
    )
    return (
        outputs, vec[6, 0], glat, gcond, gq, gk, gv, go.T, gcq, gck, gcv, gco.T, ggate, gup, gdown.T,
        vec[0], vec[1], vec[2], vec[3], vec[4], vec[5],
    )


def solution(mesh):
    in_specs = (
        P("col", "row"),
        P("col", "row"),
        P("col", "row"),
        P("row"),
        P("row"),
        P("row"),
        P("row"),
        P("row"),
        P("row"),
        P("col", "row"),
        P("col", "row"),
        P("col", "row"),
        P("row", "col"),
        P("col", "row"),
        P("col", "row"),
        P("col", "row"),
        P("row", "col"),
        P("col", "row"),
        P("col", "row"),
        P("row", "col"),
    )
    out_specs = (
        P("col", "row"),
        P(),
        P("col", "row"),
        P("col", "row"),
        P("col", "row"),
        P("col", "row"),
        P("col", "row"),
        P("row", "col"),
        P("col", "row"),
        P("col", "row"),
        P("col", "row"),
        P("row", "col"),
        P("col", "row"),
        P("col", "row"),
        P("row", "col"),
        P(("row", "col")),
        P(("row", "col")),
        P(("row", "col")),
        P(("row", "col")),
        P(("row", "col")),
        P(("row", "col")),
    )
    return jax.shard_map(body, mesh=mesh, in_specs=in_specs, out_specs=out_specs, check_vma=False)
```

time: 1120 us -> 709 us (0.63)
  waiting for transfers between devices: 477 us -> 0 us
  Pallas kernels: 405 us -> 697 us
  matrix products: 73.5 us -> 0 us
  local copies, waits for them, and re-layouts: 66.6 us -> 2.63 us
  blocking collectives: 56 us -> 0 us
  other arithmetic: 22.6 us -> 0 us
  between operations: 15.4 us -> 0.87 us
    pallas_call x10 -> x2, Pallas kernels: 405 us -> 697 us  [the longest x1 690 us: layer_call(): pl.pallas_call(functools.partial(layer_kernel, n, f, pieces, front_pieces...]
    reduce_scatter x2 -> x0, waiting for transfers between devices: 227 us -> none  [body(): lax.psum_scatter(jnp.concatenate([g.astype(BF) for g in gs], axis=1), 'co...]
    all_gather x5 -> x0, waiting for transfers between devices: 213 us -> none  [the longest x3 207 us: body(): lax.all_gather(jnp.concatenate(ws, axis=1), 'col', axis=0, tiled=True)]
    dot_general x11 -> x0, matrix products: 73.5 us -> none  [the longest x7 41.4 us: tn(): lax.dot_general(left, right, (((0,), (0,)), ((), ())), preferred_element_...]
    psum x1 -> x0, blocking collectives: 39.2 us -> none  [body(): sums, loss = lax.psum((own_cols(sums, F), loss_part), 'col')]
    unnamed x11 -> x0, waiting for transfers between devices: 38.2 us -> none
    unnamed x79 -> x0, local copies, waits for them, and re-layouts: 28.5 us -> none
    slice x7 -> x1, local copies, waits for them, and re-layouts: 23.1 us -> 1.2 us  [body(): vec[6, 0]]
  transfers between devices with their start and end apart: 9 -> 0, of which waited for: 7 -> 0; matrix products, arithmetic and copies ran while one was open for 11% -> 0% of each run, Pallas kernels for 26% -> 0%
where the time goes in v3:
time: 709 us; the launch traced here: 701 us
  Pallas kernels  697 us (98%)
    pallas_call x1, Pallas kernels, layer_call(): pl.pallas_call(functools.partial(layer_kernel, n, f, pieces, front_pieces...  690 us

profile of v3, /device:TPU:0, one launch (start us, length us, event | category | flops | bytes accessed | tf_op | source)
XLA Modules:
  0.0 700.9 jit_solution(7136157313786520555)
XLA Ops:
  0.7 690.4 %layer.1 = (bf16[1040,384]{1,0:T(8,128)(2,1)}, bf16[1040,384]{1,0:T(8,128)(2,1)}, bf16[144,384]{1,0:T(8,128)(2,1)}, f32[8,384]{1,0:T(8,128)}, f32[192,1536]{1,0:...) custom-call(bf16[1025,384]{1,0:T(8,128)(2,1)} %refs_0_.1, ...), custom_call_target="tpu_custom_call" | custom-call | tf_op jit(solution)/shard_map/layer/pallas_call | solution.py:1445
  691.1 7.0 emit.1
  698.1 1.2 slice.21
  699.3 1.4 slice_bitcast_fusion

commit v4 on v3

--- a/solution.py
+++ b/solution.py
@@ -95,6 +95,8 @@
 
 
 class ColGather:
+    more = 8
+
     def __init__(self, place, pieces, ahead, ssem, rsem, lsem):
         self.at, self.pieces, self.ahead, self.ssem, self.rsem, self.lsem = place, pieces, ahead, ssem, rsem, lsem
         self.line = place.outer == 4
@@ -156,6 +158,9 @@
 
         self.steps(one, True, far)
 
+    def started(self, p):
+        return self.ahead + p + 1 + max(0, min(p - 2, self.more))
+
     def begin(self):
         for p in range(self.ahead):
             self.start(p)
@@ -163,7 +168,8 @@
     def advance(self, p, flush=True):
         self.pass_on(p, False)
         self.relay(p, lambda cp: cp.start())
-        self.start(p + self.ahead)
+        for later in range(self.started(p - 1), self.started(p)):
+            self.start(later)
         if flush and p > 0:
             self.pass_on(p - 1, True)
         if p == len(self.pieces) - 1:
@@ -202,16 +208,16 @@
         )
 
     def own(self, p, z):
-        return pltpu.make_async_copy(self.rows(p, 2 * z + self.at.yi), self.hb.at[p % self.slots, z], self.ls.at[p, z])
+        return pltpu.make_async_copy(self.rows(p, 2 * z + self.at.yi), self.hb.at[p % 2, z], self.ls.at[p, z])
 
     def outward(self, p, z):
         at, s = self.at, p % self.slots
-        return remote(self.hb.at[s, z], self.rz.at[s, at.zo], self.sz.at[p, z], self.rzr.at[p, at.zo], (at.r, 2 * z + at.yi))
+        return remote(self.ry.at[s, z], self.rz.at[s, at.zo], self.sz.at[p, z], self.rzr.at[p, at.zo], (at.r, 2 * z + at.yi))
 
     def detour(self, p, z):
         at, s = self.at, p % self.slots
         via = lax.div(at.zo, 3) + 1
-        return remote(self.hb.at[s, z], self.rl.at[s], self.sz.at[p, z], self.rlr.at[p], (at.r, 2 * via + at.yi))
+        return remote(self.ry.at[s, z], self.rl.at[s], self.sz.at[p, z], self.rlr.at[p], (at.r, 2 * via + at.yi))
 
     def merging(self, z):
         zo = self.at.zo
@@ -235,7 +241,8 @@
 
         def one(z):
             self.across(p, z).start()
-            self.own(p, z).start()
+            if p < 2:
+                self.own(p, z).start()
 
         each(0, self.at.outer, one)
 
@@ -248,7 +255,7 @@
             self.across(p, z).wait_recv()
 
             def add(rs):
-                self.hb[s, z, rs] = (self.hb[s, z, rs].astype(F32) + self.ry[s, z, rs].astype(F32)).astype(BF)
+                self.ry[s, z, rs] = (self.hb[p % 2, z, rs].astype(F32) + self.ry[s, z, rs].astype(F32)).astype(BF)
 
             self.blocks(add)
 
@@ -262,6 +269,8 @@
                 pl.when(jnp.logical_and(near, jnp.logical_not(self.merging(z))))(lambda: self.outward(p, z).start())
 
         each(1, at.outer + 1, one)
+        if p + 2 < len(self.pieces):
+            each(0, at.outer, lambda z: self.own(p + 2, z).start())
 
     def merge(self, p):
         if not self.line:
@@ -273,7 +282,7 @@
                 remote(self.rl.at[s], self.rl.at[s], self.sz.at[p, z], self.rlr.at[p], at.ypar).wait_recv()
 
                 def add(rs):
-                    self.hb[s, z, rs] = (self.hb[s, z, rs].astype(F32) + self.rl[s, rs].astype(F32)).astype(BF)
+                    self.ry[s, z, rs] = (self.ry[s, z, rs].astype(F32) + self.rl[s, rs].astype(F32)).astype(BF)
 
                 self.blocks(add)
                 self.outward(p, z).start()
@@ -287,7 +296,7 @@
             self.result(p - 2).wait()
 
         def first(rs):
-            self.ob[p % 2, rs] = self.hb[s, at.zo, rs].astype(F32)
+            self.ob[p % 2, rs] = self.ry[s, at.zo, rs].astype(F32)
 
         self.blocks(first)
 
@@ -350,7 +359,7 @@
     dma = pltpu.SemaphoreType.DMA
     block = lambda *lead: pltpu.VMEM(lead + (size, f), BF)
     return [
-        block(slots, outer), block(slots, outer), block(slots, outer), block(slots),
+        block(slots, outer), block(2, outer), block(slots, outer), block(slots),
         pltpu.VMEM((2, size, f), F32),
     ], [
         dma((pieces, outer)), dma((pieces, outer)), dma((pieces, outer)), dma((pieces, outer)), dma((pieces, outer)),
@@ -1181,25 +1190,9 @@
         again.start()
         wck_cp = local(k.full[5], wt, sem.at[1])
         wck_cp.start()
-        ready("qkv", "lse", "trig")
-        spread_tables(trig, cos, low, high)
-
-        def emit_q(pair, dq):
-            dqkv[:, 128 * pair:128 * (pair + 1)] = rotate_lanes(dq * HEAD ** (-0.5), cos[...], -low[...], -high[...]).astype(BF)
-
-        def emit_kv(pair, rows, dk, dv):
-            dqkv[rows, f + 128 * pair:f + 128 * (pair + 1)] = rotate_lanes(dk, cos[rows], -low[rows], -high[rows]).astype(BF)
-            dqkv[rows, 2 * f + 128 * pair:2 * f + 128 * (pair + 1)] = dv.astype(BF)
-
-        pairs = f // 128
         nxt = k.back_pieces
-
-        def hook(pair, j):
-            pl.when(j == 3)(lambda: scatter.advance(nxt + pair))
-
-        attend_back(qkv, 0, qkv, f, qkv, 2 * f, TP, CH, LEN, da, a, lse, lse_t, delta_t, dqt, emit_q, emit_kv, f // HEAD, hook)
-        nxt = nxt + pairs
-
+        scatter.advance(nxt)
+        nxt = nxt + 1
         ready("h2", "c", "dcq", "dckv", "cond")
         again.wait()
         make(13, xa, lambda: c[...])
@@ -1208,15 +1201,35 @@
         h1_cp.start()
         make(15, cond, lambda: dckv[:, :f])
         make(16, cond, lambda: dckv[:, f:])
+        ready("qkv", "lse", "trig")
+        spread_tables(trig, cos, low, high)
+
+        def emit_q(pair, dq):
+            dqkv[:, 128 * pair:128 * (pair + 1)] = rotate_lanes(dq * HEAD ** (-0.5), cos[...], -low[...], -high[...]).astype(BF)
+
+        def emit_kv(pair, rows, dk, dv):
+            dqkv[rows, f + 128 * pair:f + 128 * (pair + 1)] = rotate_lanes(dk, cos[rows], -low[rows], -high[rows]).astype(BF)
+            dqkv[rows, 2 * f + 128 * pair:2 * f + 128 * (pair + 1)] = dv.astype(BF)
+
+
+        def hook(pair, j):
+            for step, spot in enumerate(k.end_spots):
+                if spot[0] == pair:
+                    pl.when(j == spot[1])(lambda: scatter.advance(nxt + step))
+
+        attend_back(qkv, 0, qkv, f, qkv, 2 * f, TP, CH, LEN, da, a, lse, lse_t, delta_t, dqt, emit_q, emit_kv, f // HEAD, hook)
+        nxt = nxt + len(k.end_spots)
+
+        h1_cp.wait()
+        for j in range(3):
+            make(17 + j, xb, lambda: dqkv[:, j * f:(j + 1) * f])
         scatter.advance(nxt)
+
         wck_cp.wait()
         for j in range(4):
             cpart[j] = nt(dckv[:, :f], wt[j * f:(j + 1) * f])
         wcv_cp = local(k.full[6], wt, sem.at[1])
         wcv_cp.start()
-        h1_cp.wait()
-        for j in range(3):
-            make(17 + j, xb, lambda: dqkv[:, j * f:(j + 1) * f])
         scatter.advance(nxt + 1)
         wcv_cp.wait()
         crecv = k.crecv
@@ -1373,6 +1386,7 @@
     k = Names()
     k.at, k.f, k.wide, k.outer = Place(n), f, 4 * f, n // 2
     k.front_pieces, k.mid_pieces, k.back_pieces = front_pieces, mid_pieces, back_pieces
+    k.end_spots = ((0, 2), (1, 0), (1, 3), (2, 2))
     k.lat, k.teach, k.cond, k.trig = take(4)
     k.small = take(6)
     shards = take(11)
@@ -1420,7 +1434,7 @@
     end_phase(k, scatter)
 
 
-def layer_call(n, lat, teach, cond, trig, small, shards, front_pieces=9, mid_pieces=15, back_pieces=5, ahead=4, s_ahead=2, slots=4):
+def layer_call(n, lat, teach, cond, trig, small, shards, front_pieces=12, mid_pieces=19, back_pieces=9, ahead=4, s_ahead=3, slots=5):
     f = lat.shape[1]
     wide, size, outer = 4 * f, shards[0].shape[0], n // 2
     ffl = shards[8].shape[1]

time: 709 us -> 659 us (0.929)
  Pallas kernels: 697 us -> 647 us
    pallas_call x1, Pallas kernels: 690 us -> 640 us  [layer_call(): pl.pallas_call(functools.partial(layer_kernel, n, f, pieces, front_pieces...]
where the time goes in v4:
time: 659 us; the launch traced here: 650 us
  Pallas kernels  647 us (98%)
    pallas_call x1, Pallas kernels, layer_call(): pl.pallas_call(functools.partial(layer_kernel, n, f, pieces, front_pieces...  640 us

profile of v4, /device:TPU:0, one launch (start us, length us, event | category | flops | bytes accessed | tf_op | source)
XLA Modules:
  0.0 650.2 jit_solution(5557651580482297719)
XLA Ops:
  0.7 639.7 %layer.1 = (bf16[1040,384]{1,0:T(8,128)(2,1)}, bf16[1040,384]{1,0:T(8,128)(2,1)}, bf16[144,384]{1,0:T(8,128)(2,1)}, f32[8,384]{1,0:T(8,128)}, f32[192,1536]{1,0:...) custom-call(bf16[1025,384]{1,0:T(8,128)(2,1)} %refs_0_.1, ...), custom_call_target="tpu_custom_call" | custom-call | tf_op jit(solution)/shard_map/layer/pallas_call | solution.py:1459
  640.4 7.0 %emit.1 = (bf16[1025,384]{1,0:T(8,128)(2,1)}, bf16[1025,384]{1,0:T(8,128)(2,1)}, bf16[130,384]{1,0:T(8,128)(2,1)}, f32[8,48]{1,0:T(8,128)}, f32[192,1536]{1,0:T(...) custom-call(bf16[1040,384]{1,0:T(8,128)(2,1)} %get-tuple-element.51., ...), custom_call_target="tpu_custom_call" | custom-call | tf_op jit(solution)/shard_map/emit/pallas_call | solution.py:1501
  647.4 1.2 slice.21
  648.6 1.4 slice_bitcast_fusion

commit v5 on v4

--- a/solution.py
+++ b/solution.py
@@ -648,9 +648,10 @@
         pad_into(teachp, teachv, LEN)
         ins[3].wait()
         spread_tables(trig, cos, low, high)
+        gather.advance(0)
         rowg.forward(0)
         rowg.forward(1)
-        gather.advance(0)
+        gather.advance(1)
         rowg.finish(0)
         rowg.finish(1)
         more = [local(k.x0, x, sem.at[0]), local(k.vecs, vec, sem.at[1])]
@@ -671,7 +672,6 @@
         each(0, TP // SUB, norm)
         outs = [local(h, k.h1, sem.at[2]), local(st, k.st1, sem.at[3])]
         start_all(outs)
-        gather.advance(1)
         gather.advance(2)
         rowg.forward(2)
         fetch = lambda p: local(gather.pieces[p][1], w.at[p % 2], sem.at[4 + p % 2])
@@ -679,9 +679,8 @@
         fetch(0).start()
         for part in range(3):
             fetch(part).wait()
+            gather.advance(3 + part)
             if part < 2:
-                if part == 1:
-                    gather.pass_on(2, True)
                 gather.finish(part + 1)
                 fetch(part + 1).start()
 
@@ -700,12 +699,11 @@
                     qkv[rows, part * f + pair * 128:part * f + (pair + 1) * 128] = u
 
             each(0, NCH, project)
-        gather.advance(3, flush=False)
 
         def attend(i):
             def hook(pair):
-                for p in range(4, k.front_pieces):
-                    pl.when(i * 3 + pair == (p - 4) * 15 // (k.front_pieces - 4))(lambda: gather.advance(p))
+                for p in range(6, k.front_pieces):
+                    pl.when(i * 3 + pair == (p - 6) * 15 // (k.front_pieces - 6))(lambda: gather.advance(p))
 
             attend_step(i, qkv, 0, qkv, f, qkv, 2 * f, TP, LEN, a, lse, f // HEAD, hook)
 
@@ -762,9 +760,11 @@
                 local(low.at[rows_of(i)], lowest.at[rows_of(i)], osem.at[which, 2 * i + 1]),
             ]
 
-        def hook(slot):
+        def hook(slot, base):
             for j, p in enumerate(slots):
-                pl.when(slot == j * 2 * NCH // len(slots))(lambda: gather.advance(p))
+                spot = j * 2 * NCH // len(slots)
+                if base <= spot < base + NCH:
+                    pl.when(slot == spot - base)(lambda: gather.advance(p))
 
         def cross(i):
             first.ready(i)
@@ -786,7 +786,7 @@
         def step(i):
             first.share(i)
             pl.when(i > 0)(lambda: cross(i - 1))
-            hook(i)
+            hook(i, 0)
 
         each(0, NCH, step)
         cross(NCH - 1)
@@ -809,7 +809,7 @@
         def step_two(i):
             second.share(i)
             pl.when(i > 0)(lambda: last(i - 1))
-            hook(NCH + i)
+            hook(i, NCH)
 
         each(0, NCH, step_two)
         last(NCH - 1)
@@ -1004,9 +1004,9 @@
             scatter.start(p)
         wait_all(rest)
 
-        def hook(slot):
-            for p in range(2, 12):
-                @pl.when(slot == p - 2)
+        def hook(slot, base):
+            for p in range(base + 2, base + 2 + NCH):
+                @pl.when(slot == p - 2 - base)
                 def _():
                     make(p)
                     grads.copy(p).wait()
@@ -1014,7 +1014,9 @@
                         scatter.start(p)
 
             for p in range(k.back_pieces):
-                pl.when(slot == p * 2 * NCH // k.back_pieces + 1)(lambda: scatter.advance(p))
+                spot = p * 2 * NCH // k.back_pieces + 1
+                if base <= spot < base + NCH:
+                    pl.when(slot == spot - base)(lambda: scatter.advance(p))
 
         def low_out(i, which):
             return local(low.at[lax.rem(i + which * NCH, 2)], (k.dco, k.do)[which].at[rows_of(i)], osem.at[which, i])
@@ -1079,7 +1081,7 @@
         def step(i):
             first.share(i)
             pl.when(i > 0)(lambda: cross(i - 1))
-            hook(i)
+            hook(i, 0)
 
         each(0, NCH, step)
         cross(NCH - 1)
@@ -1109,7 +1111,7 @@
         def step_two(i):
             second.share(i)
             pl.when(i > 0)(lambda: last(i - 1))
-            hook(NCH + i)
+            hook(i, NCH)
 
         each(0, NCH, step_two)
         last(NCH - 1)

time: 659 us -> 637 us (0.967)
  Pallas kernels: 647 us -> 623 us
    pallas_call x1, Pallas kernels: 640 us -> 616 us  [layer_call(): pl.pallas_call(functools.partial(layer_kernel, n, f, pieces, front_pieces...]
where the time goes in v5:
time: 637 us; the launch traced here: 627 us
  Pallas kernels  623 us (98%)
    pallas_call x1, Pallas kernels, layer_call(): pl.pallas_call(functools.partial(layer_kernel, n, f, pieces, front_pieces...  616 us

profile of v5, /device:TPU:0, one launch (start us, length us, event | category | flops | bytes accessed | tf_op | source)
XLA Modules:
  0.0 627.2 jit_solution(10359005913270688615)
XLA Ops:
  0.7 616.5 %layer.1 = (bf16[1040,384]{1,0:T(8,128)(2,1)}, bf16[1040,384]{1,0:T(8,128)(2,1)}, bf16[144,384]{1,0:T(8,128)(2,1)}, f32[8,384]{1,0:T(8,128)}, f32[192,1536]{1,0:...) custom-call(bf16[1025,384]{1,0:T(8,128)(2,1)} %refs_0_.1, ...), custom_call_target="tpu_custom_call" | custom-call | tf_op jit(solution)/shard_map/layer/pallas_call | solution.py:1461
  617.2 7.0 %emit.1 = (bf16[1025,384]{1,0:T(8,128)(2,1)}, bf16[1025,384]{1,0:T(8,128)(2,1)}, bf16[130,384]{1,0:T(8,128)(2,1)}, f32[8,48]{1,0:T(8,128)}, f32[192,1536]{1,0:T(...) custom-call(bf16[1040,384]{1,0:T(8,128)(2,1)} %get-tuple-element.51., ...), custom_call_target="tpu_custom_call" | custom-call | tf_op jit(solution)/shard_map/emit/pallas_call | solution.py:1503
  624.1 1.2 slice.21
  625.3 1.4 slice_bitcast_fusion

commit v6 on v5

--- a/solution.py
+++ b/solution.py
@@ -1436,7 +1436,7 @@
     end_phase(k, scatter)
 
 
-def layer_call(n, lat, teach, cond, trig, small, shards, front_pieces=12, mid_pieces=19, back_pieces=9, ahead=4, s_ahead=3, slots=5):
+def layer_call(n, lat, teach, cond, trig, small, shards, front_pieces=12, mid_pieces=18, back_pieces=9, ahead=4, s_ahead=3, slots=5):
     f = lat.shape[1]
     wide, size, outer = 4 * f, shards[0].shape[0], n // 2
     ffl = shards[8].shape[1]

time: 637 us -> 643 us (level)
  Pallas kernels: 623 us -> 631 us
    pallas_call x1, Pallas kernels: 616 us -> 624 us  [layer_call(): pl.pallas_call(functools.partial(layer_kernel, n, f, pieces, front_pieces...]
where the time goes in v6:
time: 643 us; the launch traced here: 635 us
  Pallas kernels  631 us (98%)
    pallas_call x1, Pallas kernels, layer_call(): pl.pallas_call(functools.partial(layer_kernel, n, f, pieces, front_pieces...  624 us

profile of v6, /device:TPU:0, one launch (start us, length us, event | category | flops | bytes accessed | tf_op | source)
XLA Modules:
  0.0 634.7 jit_solution(15961048266035162878)
XLA Ops:
  0.7 624.0 %layer.1 = (bf16[1040,384]{1,0:T(8,128)(2,1)}, bf16[1040,384]{1,0:T(8,128)(2,1)}, bf16[144,384]{1,0:T(8,128)(2,1)}, f32[8,384]{1,0:T(8,128)}, f32[192,1536]{1,0:...) custom-call(bf16[1025,384]{1,0:T(8,128)(2,1)} %refs_0_.1, ...), custom_call_target="tpu_custom_call" | custom-call | tf_op jit(solution)/shard_map/layer/pallas_call | solution.py:1461
  624.7 7.0 %emit.1 = (bf16[1025,384]{1,0:T(8,128)(2,1)}, bf16[1025,384]{1,0:T(8,128)(2,1)}, bf16[130,384]{1,0:T(8,128)(2,1)}, f32[8,48]{1,0:T(8,128)}, f32[192,1536]{1,0:T(...) custom-call(bf16[1040,384]{1,0:T(8,128)(2,1)} %get-tuple-element.51., ...), custom_call_target="tpu_custom_call" | custom-call | tf_op jit(solution)/shard_map/emit/pallas_call | solution.py:1503
  631.6 1.2 slice.21
  632.8 1.4 slice_bitcast_fusion
